TPU v7x, 128 devices: a whole 4x4x4 slice. The times are simulated.
128 devices in a mesh: gx: 4 (over y), gy: 32 (over z, x, core).
Axes of the slice: x: 4, y: 4, z: 4, core: 2. Of those that a mesh axis runs over, the one named last changes fastest.
Arguments:
- patches: bfloat16 [256, 4096, 256], P(('gx', 'gy')), may hold values from -6 to 6
- start_frames: float32 [256, 256, 256], P(('gx', 'gy')), may hold values from -6 to 6
- pair_ends: int32 [1024, 2], P('gx'), may hold values from 0 to 255, as said below
- margin_blocks: int32 [1024, 2, 4], P('gx'), may hold values from 0 to 31, as said below
Outputs:
- aligned: bfloat16 [256, 4096, 256], P(('gx', 'gy'))
- final_frames: float32 [256, 256, 256], P(('gx', 'gy'))
- frame_total: float32 [256, 256], replicated
Inputs may be any that keep to these rules, and one draw needn't show every extreme that they name: `pair_ends`: both ends of a pair lie in the owner's group of 64 patches (patches of the devices with the owner's gx index), on distinct patches; at most 1 ends of one owner's pairs lie on any one device, and ends on one device are of distinct patches; some device holds exactly 1 of some owner's ends. Every patch is an end of some pair. Patch p lives on device p // 2, devices counted with gx slowest. Patch degrees are uneven. `margin_blocks`: the 4 blocks of one end are distinct.
All inputs are finite; a program needn't handle non-finite values.
Results may differ from a plain program's by a relative error of at most 0.012.
The roundings to bfloat16 on the way count: a program that leaves them out, or rounds other values in their place, can miss the bound.
Values may be sent and summed in bfloat16 or wider, within the bound.
No kernel may reach another device: no remote copies, remote signals or barrier semaphores. Data moves between devices by JAX's collectives and lax.ppermute only.
A program may use at most 128 MiB of HBM per device.

v0:
```python
import functools

import jax
import jax.numpy as jnp
import numpy as np
from jax import lax
from jax.experimental import pallas as pl
from jax.experimental.pallas import tpu as pltpu
from jax.sharding import Mesh
from jax.sharding import PartitionSpec as P


BLOCK = 128
OVB = 4
D = 256
SWEEPS = 2
NS_STEPS = 5
PER = 2
DEVS = 32
BATCH = 4
GY = ("gy_0", "gy_1", "gy_2")
GX_GY = ("gx", "gy_0", "gy_1", "gy_2")
F32, BF16 = jnp.float32, jnp.bfloat16

coef_first = 3.4445
coef_second = -4.775
coef_third = 2.0315

OFFS = (
    ((0, 0), (1, 0), (2, 0), (0, 1), (0, 3), (0, 2)),
    ((0, 0), (0, 1), (0, 2), (1, 0), (3, 0), (2, 0)),
)
CROSS = (1, 2, 3)
OWN = len(OFFS[0])
SLOTS = OWN + len(CROSS)
MAX_PAIRS = -(-(SLOTS * DEVS // 2) // BATCH) * BATCH


def device_at(z, x, c):
    return (z % 4) * 8 + (x % 4) * 2 + c % 2


def place_of(m):
    return m // 8, (m // 2) % 4, m % 2


def step_perm(steps):
    perm = []
    for m in range(DEVS):
        z, x, c = place_of(m)
        dz, dx = steps[c]
        perm.append((m, device_at(z + dz, x + dx, c)))
    return perm


def flip(step):
    return (step, (step[1], step[0]))


UP, RIGHT, LEFT = flip((1, 0)), flip((0, 1)), flip((0, -1))
SIBLING = [(m, m ^ 1) for m in range(DEVS)]


@functools.cache
def sources():
    same = []
    for m in range(DEVS):
        z, x, c = place_of(m)
        same.append([device_at(z - dz, x - dx, c) for dz, dx in OFFS[c]])
    return [same[m] + [same[m ^ 1][k] for k in CROSS] for m in range(DEVS)]


READY = ((0, 0), (0, 0), (1, 1), (0, 2), (0, 0), (1, 1), (0, 0), (1, 1), (0, 2))
CLASSES = 3
CHOICES = 3


@functools.cache
def meeting_table():
    found = {}
    src = sources()
    for m in range(DEVS):
        for i in range(SLOTS):
            for j in range(SLOTS):
                if src[m][i] != src[m][j]:
                    found.setdefault((src[m][i], src[m][j]), []).append((m, i, j))
    table = np.full((DEVS, PER, DEVS, PER, CHOICES), -1, np.int32)
    for (a, b), places in found.items():
        for pa in range(PER):
            for pb in range(PER):
                ranked = {}
                for m, i, j in places:
                    ready = max(READY[i][pa], READY[j][pb])
                    ranked[m] = min(ranked.get(m, (9,)), (ready, i, j))
                first = min(r[0] for r in ranked.values())
                codes = [
                    ((r * DEVS + m) << 8) | (i << 4) | j for m, (r, i, j) in sorted(ranked.items()) if r == first
                ]
                turn = (a + b) % len(codes)
                codes = (codes[turn:] + codes[:turn])[:CHOICES]
                codes += codes[-1:] * (CHOICES - len(codes))
                table[a, pa, b, pb] = codes
    return table.reshape(-1)


HBM = pl.BlockSpec(memory_space=pltpu.HBM)
VM = pl.BlockSpec(memory_space=pltpu.VMEM)
SM = pl.BlockSpec(memory_space=pltpu.SMEM)
INFO = 2 + 2 * OVB


def params():
    return pltpu.CompilerParams(vmem_limit_bytes=56 * 1024 * 1024)


def halves(a):
    high = a.astype(BF16)
    return high, (a - high.astype(F32)).astype(BF16)


def dot(a, b, ca=1, cb=0):
    return lax.dot_general(a, b, (((ca,), (cb,)), ((), ())), preferred_element_type=F32)


def dot3(a, b, cb=0):
    (ah, al), (bh, bl) = a, b
    return dot(ah, bh, 1, cb) + (dot(ah, bl, 1, cb) + dot(al, bh, 1, cb))


def newton_schulz(ref, count):
    for i in range(count):
        m = ref[i]
        total = jnp.sum(jnp.sum(m * m, axis=1, keepdims=True), axis=0, keepdims=True)
        ref[i] = m * lax.rsqrt(total + 1e-6)

    def step(_, carry):
        ms = [ref[i] for i in range(count)]
        hs = [halves(m) for m in ms]
        squares = [dot3(h, h, 1) for h in hs]
        sh = [halves(s) for s in squares]
        polys = [coef_second * s + coef_third * dot3(h, h) for s, h in zip(squares, sh)]
        ph = [halves(p) for p in polys]
        for i in range(count):
            ref[i] = coef_first * ms[i] + dot3(ph[i], hs[i])
        return carry

    lax.fori_loop(0, NS_STEPS, step, 0)


def index_kernel(me_ref, table_ref, ends_ref, blocks_ref, info_ref, count_ref, load_ref):
    me, base = me_ref[0], me_ref[1]
    for n in range(CLASSES * DEVS):
        load_ref[n] = 0

    def step(q, carry):
        a, b = ends_ref[2 * q] - base, ends_ref[2 * q + 1] - base
        first = (a * (DEVS * PER) + b) * CHOICES
        code = table_ref[first]
        least = load_ref[code >> 8]
        for k in range(1, CHOICES):
            other = table_ref[first + k]
            less = load_ref[other >> 8]
            code = jnp.where(less < least, other, code)
            least = jnp.minimum(less, least)
        place = code >> 8
        load_ref[place] = least + 1

        @pl.when((place & (DEVS - 1)) == me)
        def _():
            line = ((place >> 5) * MAX_PAIRS + least) * INFO
            info_ref[line] = ((code >> 4) & 15) * PER + (a & 1)
            info_ref[line + 1] = (code & 15) * PER + (b & 1)
            for k in range(2 * OVB):
                info_ref[line + 2 + k] = blocks_ref[q * 2 * OVB + k]

        return carry

    lax.fori_loop(0, ends_ref.shape[0] // 2, step, 0)
    for c in range(CLASSES):
        count_ref[c] = load_ref[c * DEVS + me]


def make_index(me, table, ends, blocks):
    return pl.pallas_call(
        index_kernel,
        in_specs=[SM] * 4,
        out_specs=[SM] * 2,
        out_shape=[
            jax.ShapeDtypeStruct((CLASSES * MAX_PAIRS * INFO,), jnp.int32),
            jax.ShapeDtypeStruct((CLASSES,), jnp.int32),
        ],
        scratch_shapes=[pltpu.SMEM((CLASSES * DEVS,), jnp.int32)],
        name="pair_index",
    )(me, table, ends, blocks)


def rotation_kernel(layout, ready, size, info_ref, count_ref, *refs):
    arrays, (rot_ref, rows, mats, outs, load_sem, out_sem) = refs[:-6], refs[-6:]
    count = count_ref[ready]
    first = jnp.int32(0)
    for c in range(ready):
        first = first + count_ref[c]
    batches = (count + size - 1) // size

    def block_ref(slot, block):
        number, part = layout[slot]
        ref = arrays[number]
        lines = pl.ds(pl.multiple_of(block * BLOCK, BLOCK), BLOCK)
        return ref.at[lines] if part is None else ref.at[part, lines]

    def load(batch, buf):
        def one(i, carry):
            line = (ready * MAX_PAIRS + jnp.minimum(batch * size + i, count - 1)) * INFO
            for e in range(2):
                slot = info_ref[line + e]
                for s in layout:

                    @pl.when(slot == s)
                    def _():
                        for k in range(OVB):
                            pltpu.make_async_copy(
                                block_ref(s, info_ref[line + 2 + e * OVB + k]),
                                rows.at[buf, i, e, pl.ds(k * BLOCK, BLOCK)],
                                load_sem.at[buf],
                            ).start()

            return carry

        lax.fori_loop(0, size, one, 0)

    def out_copy(batch):
        return pltpu.make_async_copy(outs, rot_ref.at[pl.ds(first + batch * size, size)], out_sem)

    @pl.when(batches > 0)
    def _():
        load(0, 0)

    def step(batch, carry):
        buf = batch & 1

        @pl.when(batch + 1 < batches)
        def _():
            load(batch + 1, 1 - buf)

        pltpu.make_async_copy(rows.at[buf], rows.at[buf], load_sem.at[buf]).wait()
        for i in range(size):
            mats[i] = dot(rows[buf, i, 1], rows[buf, i, 0], 0, 0)
        newton_schulz(mats, size)

        @pl.when(batch > 0)
        def _():
            out_copy(batch - 1).wait()

        for i in range(size):
            outs[i] = mats[i]
        out_copy(batch).start()
        return carry

    lax.fori_loop(0, batches, step, 0)

    @pl.when(batches > 0)
    def _():
        out_copy(batches - 1).wait()


def make_rotations(info, count, arrays, layout, ready, size, rot=None):
    layout = {s: at for s, at in enumerate(layout) if at[0] < len(arrays)}
    more = [] if rot is None else [rot]
    return pl.pallas_call(
        functools.partial(rotation_kernel, layout, ready, size),
        in_specs=[SM, SM] + [HBM] * (len(arrays) + len(more)),
        out_specs=HBM,
        out_shape=jax.ShapeDtypeStruct((MAX_PAIRS + BATCH, D, D), F32),
        input_output_aliases={2 + len(arrays): 0} if more else {},
        scratch_shapes=[
            pltpu.VMEM((2, size, 2, OVB * BLOCK, D), BF16),
            pltpu.VMEM((size, D, D), F32),
            pltpu.VMEM((size, D, D), F32),
            pltpu.SemaphoreType.DMA((2,)),
            pltpu.SemaphoreType.DMA,
        ],
        compiler_params=params(),
    )(info, count, *arrays, *more)


def start_kernel(start_ref, frame_ref, low_ref):
    for p in range(PER):
        frame_ref[p] = start_ref[p]
    newton_schulz(frame_ref, PER)
    low_ref[...] = frame_ref[...].astype(BF16)


def make_start(start):
    return pl.pallas_call(
        start_kernel,
        in_specs=[VM],
        out_specs=[VM, VM],
        out_shape=[
            jax.ShapeDtypeStruct((PER, D, D), F32),
            jax.ShapeDtypeStruct((PER, D, D), BF16),
        ],
        compiler_params=params(),
        name="start_frames",
    )(start)


def estimate_kernel(info_ref, count_ref, rot_ref, *refs):
    lows = refs[:SLOTS]
    outs = refs[SLOTS : SLOTS + OWN + 1]
    frames, acc, rot, frame_sem, rot_sem, out_sem = refs[SLOTS + OWN + 1 :]
    ends = [count_ref[0]]
    for c in range(1, CLASSES):
        ends.append(ends[-1] + count_ref[c])
    count = ends[-1]

    def line_of(j):
        line = j
        for c in range(1, CLASSES):
            line = jnp.where(j >= ends[c - 1], c * MAX_PAIRS + j - ends[c - 1], line)
        return line * INFO

    def rot_copy(j, buf):
        return pltpu.make_async_copy(rot_ref.at[j], rot.at[buf], rot_sem.at[buf])

    copies = [
        pltpu.make_async_copy(lows[s], frames.at[pl.ds(s * PER, PER)], frame_sem.at[s])
        for s in range(SLOTS)
    ]
    for copy in copies:
        copy.start()

    @pl.when(count > 0)
    def _():
        rot_copy(0, 0).start()

    acc[...] = jnp.zeros_like(acc)
    for copy in copies:
        copy.wait()

    def step(j, carry):
        buf = j & 1

        @pl.when(j + 1 < count)
        def _():
            rot_copy(j + 1, 1 - buf).start()

        rot_copy(j, buf).wait()
        line = line_of(j)
        sa, sb = info_ref[line], info_ref[line + 1]
        high, rest = halves(rot[buf])
        fa, fb = frames[sa], frames[sb]
        acc[sa] += dot(high, fb, 0, 0) + dot(rest, fb, 0, 0)
        acc[sb] += dot(high, fa) + dot(rest, fa)
        return carry

    lax.fori_loop(0, count, step, 0)
    parts = [(s * PER, PER) for s in range(OWN)] + [(OWN * PER, len(CROSS) * PER)]
    copies = [
        pltpu.make_async_copy(acc.at[pl.ds(*part)], outs[n], out_sem.at[n]) for n, part in enumerate(parts)
    ]
    for copy in copies:
        copy.start()
    for copy in copies:
        copy.wait()


def make_estimates(info, count, rot, lows):
    return pl.pallas_call(
        estimate_kernel,
        in_specs=[SM, SM, HBM] + [HBM] * SLOTS,
        out_specs=[HBM] * (OWN + 1),
        out_shape=[jax.ShapeDtypeStruct((PER, D, D), F32)] * OWN
        + [jax.ShapeDtypeStruct((len(CROSS) * PER, D, D), F32)],
        scratch_shapes=[
            pltpu.VMEM((SLOTS * PER, D, D), BF16),
            pltpu.VMEM((SLOTS * PER, D, D), F32),
            pltpu.VMEM((2, D, D), F32),
            pltpu.SemaphoreType.DMA((SLOTS,)),
            pltpu.SemaphoreType.DMA((2,)),
            pltpu.SemaphoreType.DMA((OWN + 1,)),
        ],
        compiler_params=params(),
        name="estimates",
    )(info, count, rot, *lows)


def update_kernel(frame_ref, *refs):
    parts, (out_ref, low_ref, sum_ref) = refs[:-3], refs[-3:]
    for p in range(PER):
        total = frame_ref[p]
        for part in parts:
            total = total + part[p]
        out_ref[p] = total
    newton_schulz(out_ref, PER)
    low_ref[...] = out_ref[...].astype(BF16)
    sum_ref[...] = out_ref[0] + out_ref[1]


def make_update(frames, parts):
    return pl.pallas_call(
        update_kernel,
        in_specs=[VM] * (1 + len(parts)),
        out_specs=[VM] * 3,
        out_shape=[
            jax.ShapeDtypeStruct((PER, D, D), F32),
            jax.ShapeDtypeStruct((PER, D, D), BF16),
            jax.ShapeDtypeStruct((D, D), F32),
        ],
        compiler_params=params(),
        name="update_frames",
    )(frames, *parts)


CHUNK = 1024


def final_kernel(total_ref, frame_ref, patch_ref, aligned_ref, final_ref, gauge, rows, outs, low, in_sem, out_sem):
    chunks = [(p, pl.ds(r, CHUNK)) for p in range(PER) for r in range(0, patch_ref.shape[1], CHUNK)]
    ins = [
        pltpu.make_async_copy(patch_ref.at[p, r], rows.at[p, r], in_sem.at[n])
        for n, (p, r) in enumerate(chunks)
    ]
    for copy in ins:
        copy.start()
    gauge[0] = total_ref[...]
    newton_schulz(gauge, 1)
    g = halves(gauge[0])
    for p in range(PER):
        final = dot3(halves(frame_ref[p]), g, 1)
        final_ref[p] = final
        low[p] = final.astype(BF16)
    done = []
    for n, (p, r) in enumerate(chunks):
        ins[n].wait()
        outs[p, r] = dot(rows[p, r], low[p]).astype(BF16)
        copy = pltpu.make_async_copy(outs.at[p, r], aligned_ref.at[p, r], out_sem.at[n])
        copy.start()
        done.append(copy)
    for copy in done:
        copy.wait()


def make_final(total, frames, patches):
    pieces = PER * patches.shape[1] // CHUNK
    return pl.pallas_call(
        final_kernel,
        in_specs=[VM, VM, HBM],
        out_specs=[HBM, VM],
        out_shape=[
            jax.ShapeDtypeStruct(patches.shape, BF16),
            jax.ShapeDtypeStruct((PER, D, D), F32),
        ],
        scratch_shapes=[
            pltpu.VMEM((1, D, D), F32),
            pltpu.VMEM(patches.shape, BF16),
            pltpu.VMEM(patches.shape, BF16),
            pltpu.VMEM((PER, D, D), BF16),
            pltpu.SemaphoreType.DMA((pieces,)),
            pltpu.SemaphoreType.DMA((pieces,)),
        ],
        compiler_params=params(),
        name="aligned_rows",
    )(total, frames, patches)


def send(value, perm):
    return lax.ppermute(value, GY, perm)


LAYOUT = (
    ((0, 0), (0, 1), (1, 0), (1, 1), (6, 0), (6, 1), (3, None), (9, None), (2, 0), (2, 1), (7, 0), (7, 1))
    + ((4, 0), (4, 1), (8, 0), (8, 1), (5, None), (10, None))
)


def back_perm(steps):
    return [(d, m) for m, d in step_perm(steps)]


def spread_frames(low):
    one, four, three = send(low, step_perm(UP)), send(low, step_perm(LEFT)), send(low, step_perm(RIGHT))
    two, five = send(one, step_perm(UP)), send(four, step_perm(LEFT))
    return [low, one, two, three, four, five] + [send(v, SIBLING) for v in (one, two, three)]


def bring_back(parts):
    own, one, two, three, four, five, cross = parts
    cross = send(cross, SIBLING)
    five = send(five, back_perm(LEFT))
    one, two, three = (v + cross[PER * n : PER * (n + 1)] for n, v in enumerate((one, two, three)))
    two = send(two, back_perm(UP))
    return [
        own,
        send(three, back_perm(RIGHT)),
        send(four + five, back_perm(LEFT)),
        send(one + two, back_perm(UP)),
    ]


def from_everyone(value, axis):
    size = lax.axis_size(axis)
    return lax.all_to_all(jnp.broadcast_to(value[None], (size, *value.shape)), axis, 0, 0, tiled=True)


def sum_over_all(value):
    size = lax.axis_size(GY)
    rows = value.shape[0] // size
    mine = lax.all_to_all(value.reshape(size, rows, D), GY, 0, 0, tiled=True).sum(0)
    mine = from_everyone(mine, "gx").sum(0)
    return from_everyone(mine, GY).reshape(value.shape)


def local(patches, start_frames, pair_ends, margin_blocks):
    me = lax.axis_index(GY).astype(jnp.int32)
    base = lax.axis_index("gx").astype(jnp.int32) * (DEVS * PER)
    one = send(patches, step_perm(UP))
    four = send(patches, step_perm(LEFT))
    three_0 = send(patches[0], step_perm(RIGHT))
    info, count = make_index(
        jnp.stack([me, base]),
        jnp.asarray(meeting_table()),
        pair_ends.reshape(-1),
        margin_blocks.reshape(-1),
    )
    frames, low = make_start(start_frames)
    lows = spread_frames(low)
    two = send(one, step_perm(UP))
    five = send(four, step_perm(LEFT))
    cross_1 = send(one, SIBLING)
    cross_3_0 = send(three_0, SIBLING)
    arrays = [patches, one, four, three_0, cross_1, cross_3_0]
    rot = make_rotations(info, count, arrays, LAYOUT, 0, BATCH)
    three_1 = send(five[1], step_perm(LEFT))
    cross_2 = send(two, SIBLING)
    arrays += [two, five, cross_2]
    rot = make_rotations(info, count, arrays, LAYOUT, 1, BATCH, rot)
    cross_3_1 = send(three_1, SIBLING)
    arrays += [three_1, cross_3_1]
    rot = make_rotations(info, count, arrays, LAYOUT, 2, 2, rot)
    for sweep in range(SWEEPS):
        if sweep:
            lows = spread_frames(low)
        back = bring_back(make_estimates(info, count, rot, lows))
        frames, low, frame_sum = make_update(frames, back)
    total = sum_over_all(frame_sum)
    aligned, final_frames = make_final(total, frames, patches)
    return aligned, final_frames, total


def solution(mesh):
    torus = Mesh(mesh.devices.reshape(mesh.shape["gx"], 4, 4, 2), ("gx", "gy_0", "gy_1", "gy_2"))
    return jax.shard_map(
        local,
        mesh=torus,
        in_specs=(P(GX_GY, None, None), P(GX_GY, None, None), P("gx", None), P("gx", None, None)),
        out_specs=(P(GX_GY, None, None), P(GX_GY, None, None), P()),
        check_vma=False,
    )
```

profile of v0, /device:TPU:1, one launch (start us, length us, event | category | flops | bytes accessed | tf_op | source)
XLA Modules:
  0.0 438.8 jit_solution(585079086891567484)
XLA Ops:
  0.6 2.1 collective-permute-start
  2.7 3.8 collective-permute-start.1
  6.5 43.9 %collective-permute-done.refs_1_ = bf16[2,4096,256]{2,1,0:T(8,128)(2,1)S(1)} collective-permute-done((bf16[2,4096,256]{2,1,0:T(8,128)(2,1)}, bf16[2,4096,256]{2,1,0:T(8,128)(2,1)S(1)}, u32[]{:S(2)}, u32[]{:S(2)}) %collective-permute-start) | collective-permute-done | bytes 4194336 | tf_op jit(solution)/shard_map/ppermute | solution.py:467
  52.3 3.0 collective-permute-start.6
  58.7 63.1 %collective-permute-done.5.refs_6_ = bf16[2,4096,256]{2,1,0:T(8,128)(2,1)} collective-permute-done((bf16[2,4096,256]{2,1,0:T(8,128)(2,1)S(1)}, bf16[2,4096,256]{2,1,0:T(8,128)(2,1)}, u32[]{:S(2)}, u32[]{:S(2)}) %collective-permute-start.5) | collective-permute-done | bytes 4194336 | tf_op jit(solution)/shard_map/ppermute | solution.py:467
  121.8 3.4 collective-permute-start.7
  127.7 2.2 collective-permute-start.4
  130.0 22.5 %collective-permute-done.8.refs_9_ = bf16[4096,256]{1,0:T(8,128)(2,1)} collective-permute-done((bf16[4096,256]{1,0:T(8,128)(2,1)S(1)}, bf16[4096,256]{1,0:T(8,128)(2,1)}, u32[]{:S(2)}, u32[]{:S(2)}) %collective-permute-start.8) | collective-permute-done | bytes 2097184 | tf_op jit(solution)/shard_map/ppermute | solution.py:467
  153.5 7.4 %start_frames.1 = (f32[2,256,256]{2,1,0:T(8,128)}, bf16[2,256,256]{2,1,0:T(8,128)(2,1)}) custom-call(f32[2,256,256]{2,1,0:T(8,128)} %start_ref.1), custom_call_target="tpu_custom_call" | custom-call | tf_op jit(solution)/shard_map/start_frames/pallas_call | solution.py:294
  161.9 6.5 %collective-permute-done.10.refs_1_ = bf16[2,256,256]{2,1,0:T(8,128)(2,1)S(1)} collective-permute-done((bf16[2,256,256]{2,1,0:T(8,128)(2,1)}, bf16[2,256,256]{2,1,0:T(8,128)(2,1)S(1)}, u32[]{:S(2)}, u32[]{:S(2)}) %collective-permute-start.10) | collective-permute-done | bytes 262176 | tf_op jit(solution)/shard_map/ppermute | solution.py:467
  168.9 5.2 %collective-permute-done.13.refs_4_ = bf16[2,256,256]{2,1,0:T(8,128)(2,1)S(1)} collective-permute-done((bf16[2,256,256]{2,1,0:T(8,128)(2,1)}, bf16[2,256,256]{2,1,0:T(8,128)(2,1)S(1)}, u32[]{:S(2)}, u32[]{:S(2)}) %collective-permute-start.13) | collective-permute-done | bytes 262176 | tf_op jit(solution)/shard_map/ppermute | solution.py:467
  174.1 6.6 %collective-permute-done.12.refs_3_ = bf16[2,256,256]{2,1,0:T(8,128)(2,1)S(1)} collective-permute-done((bf16[2,256,256]{2,1,0:T(8,128)(2,1)}, bf16[2,256,256]{2,1,0:T(8,128)(2,1)S(1)}, u32[]{:S(2)}, u32[]{:S(2)}) %collective-permute-start.12) | collective-permute-done | bytes 262176 | tf_op jit(solution)/shard_map/ppermute | solution.py:467
  180.8 6.4 %collective-permute-done.11.refs_2_ = bf16[2,256,256]{2,1,0:T(8,128)(2,1)S(1)} collective-permute-done((bf16[2,256,256]{2,1,0:T(8,128)(2,1)S(1)}, bf16[2,256,256]{2,1,0:T(8,128)(2,1)S(1)}, u32[]{:S(2)}, u32[]{:S(2)}) %collective-permute-start.11) | collective-permute-done | bytes 262176 | tf_op jit(solution)/shard_map/ppermute | solution.py:467
  187.2 5.2 %collective-permute-start.15 = (bf16[2,256,256]{2,1,0:T(8,128)(2,1)S(1)}, bf16[2,256,256]{2,1,0:T(8,128)(2,1)}, u32[]{:S(2)}, u32[]{:S(2)}) collective-permute-start(bf16[2,256,256]{2,1,0:T(8,128)(2,1)S(1)} %collective-permute-done.10.refs_1_), channel_id=1, source_target_pairs={{0,1},{1,0},{2,3},{3,2},{4,5},{5,4},{6,7},{7,6},{8,9},{9,8},{10,11... | collective-permute-start | bytes 786440 | tf_op jit(solution)/shard_map/ppermute | solution.py:467
  192.4 3.3 collective-permute-start.17
  198.5 12.5 %pair_index.1 = (s32[4320]{0:T(1024)}, s32[3]{0:T(128)}) custom-call(s32[2]{0:T(128)} %pad_add_fusion.me_ref, s32[12288]{0:T(1024)} %constant.25.clone.table_ref, s32[512]{0:T(512)} %reshape.20.ends_ref, s32[2048]{0:T(1024)} %reshape.21.blocks_ref), custom_call_target="tpu_custom_call" | custom-call | tf_op jit(solution)/shard_map/pair_index/pallas_call | solution.py:184
  210.9 21.0 %shard_map.76.refs_9_ = f32[148,256,256]{2,1,0:T(8,128)} custom-call(s32[4320]{0:T(1024)} %get-tuple-element.28.info_ref, s32[3]{0:T(128)} %get-tuple-element.29.count_ref, bf16[2,4096,256]{2,1,0:T(8,128)(2,1)} %patch_ref.1, bf16[2,4096,256]{2,1,0:T(8,128)(2,1)} %copy-done, bf16[2,4096,256]{2,1,0:T(8,128)(2,1)} %copy-done.1, bf16[4096,256]{1,0:T(8,128)(2,1)} %copy-done.3, ...), custom_call_target="tpu_custom_call" | custom-call | tf_op jit(solution)/shard_map/pallas_call | solution.py:269
  232.0 13.0 %shard_map.77.refs_11_ = f32[148,256,256]{2,1,0:T(8,128)} custom-call(s32[4320]{0:T(1024)} %get-tuple-element.28.info_ref, s32[3]{0:T(128)} %get-tuple-element.29.count_ref, bf16[2,4096,256]{2,1,0:T(8,128)(2,1)} %patch_ref.1, bf16[2,4096,256]{2,1,0:T(8,128)(2,1)} %copy-done, bf16[2,4096,256]{2,1,0:T(8,128)(2,1)} %copy-done.1, ...), custom_call_target="tpu_custom_call", output_to_operand_aliasing={{}: (11, {})} | custom-call | tf_op jit(solution)/shard_map/pallas_call | solution.py:269
  244.9 15.5 %shard_map.78.rot_ref = f32[148,256,256]{2,1,0:T(8,128)} custom-call(s32[4320]{0:T(1024)} %get-tuple-element.28.info_ref, s32[3]{0:T(128)} %get-tuple-element.29.count_ref, bf16[2,4096,256]{2,1,0:T(8,128)(2,1)} %patch_ref.1, bf16[2,4096,256]{2,1,0:T(8,128)(2,1)} %copy-done, bf16[2,4096,256]{2,1,0:T(8,128)(2,1)} %copy-done.1, ...), custom_call_target="tpu_custom_call", output_to_operand_aliasing={{}: (13, {})} | custom-call | tf_op jit(solution)/shard_map/pallas_call | solution.py:269
  260.5 10.5 %estimates.2 = (f32[2,256,256]{2,1,0:T(8,128)}, f32[2,256,256]{2,1,0:T(8,128)}, f32[2,256,256]{2,1,0:T(8,128)}, f32[2,256,256]{2,1,0:T(8,128)}, f32[2,256,256]{2...) custom-call(s32[4320]{0:T(1024)} %get-tuple-element.28.info_ref, s32[3]{0:T(128)} %get-tuple-element.29.count_ref, ...), custom_call_target="tpu_custom_call" | custom-call | tf_op jit(solution)/shard_map/estimates/pallas_call | solution.py:368
  271.0 3.7 collective-permute-start.18
  274.7 3.2 collective-permute-done.18
  279.2 5.3 %collective-permute-done.20 = f32[2,256,256]{2,1,0:T(8,128)S(1)} collective-permute-done((f32[2,256,256]{2,1,0:T(8,128)}, f32[2,256,256]{2,1,0:T(8,128)S(1)}, u32[]{:S(2)}, u32[]{:S(2)}) %collective-permute-start.20) | collective-permute-done | bytes 524320 | tf_op jit(solution)/shard_map/ppermute | solution.py:467
  288.6 2.5 collective-permute-start.23
  291.1 4.1 collective-permute-done.21.refs_2_
  295.2 3.7 collective-permute-done.19.refs_1_
  298.9 3.1 collective-permute-done.23.refs_3_
  302.9 8.2 %update_frames.2 = (f32[2,256,256]{2,1,0:T(8,128)}, bf16[2,256,256]{2,1,0:T(8,128)(2,1)}, f32[256,256]{1,0:T(8,128)}) custom-call(f32[2,256,256]{2,1,0:T(8,128)} %get-tuple-element.27.frame_ref, f32[2,256,256]{2,1,0:T(8,128)} %get-tuple-element.31.refs_0_, f32[2,256,256]{2,1,0:T(8,128)} %copy-done.11, f32[2,256,256]{2,1,0:T(8,128)} %copy-done.9, ...), custom_call_target="tpu_custom_call" | custom-call | tf_op jit(solution)/shard_map/update_frames/pallas_call | solution.py:400
  311.0 2.1 collective-permute-start.24
  313.1 5.2 %collective-permute-start.27 = (bf16[2,256,256]{2,1,0:T(8,128)(2,1)}, bf16[2,256,256]{2,1,0:T(8,128)(2,1)S(1)}, u32[]{:S(2)}, u32[]{:S(2)}) collective-permute-start(bf16[2,256,256]{2,1,0:T(8,128)(2,1)} %get-tuple-element.39.refs_0_), channel_id=1, source_target_pairs={{0,6},{1,25},{2,0},{3,27},{4,2},{5,29},{6,4},{7,31},{8,14},{9,1},{... | collective-permute-start | bytes 786440 | tf_op jit(solution)/shard_map/ppermute | solution.py:467
  320.2 4.8 %collective-permute-start.29 = (bf16[2,256,256]{2,1,0:T(8,128)(2,1)S(1)}, bf16[2,256,256]{2,1,0:T(8,128)(2,1)S(1)}, u32[]{:S(2)}, u32[]{:S(2)}) collective-permute-start(bf16[2,256,256]{2,1,0:T(8,128)(2,1)S(1)} %collective-permute-done.24.refs_1_), channel_id=1, source_target_pairs={{0,1},{1,0},{2,3},{3,2},{4,5},{5,4},{6,7},{7,6},{8,9},{9,8},{10,11... | collective-permute-start | bytes 786440 | tf_op jit(solution)/shard_map/ppermute | solution.py:467
  326.0 2.4 collective-permute-start.31
  328.9 2.2 collective-permute-done.28.refs_5_
  332.6 10.5 %estimates.3 = (f32[2,256,256]{2,1,0:T(8,128)}, f32[2,256,256]{2,1,0:T(8,128)}, f32[2,256,256]{2,1,0:T(8,128)}, f32[2,256,256]{2,1,0:T(8,128)}, f32[2,256,256]{2...) custom-call(s32[4320]{0:T(1024)} %get-tuple-element.28.info_ref, s32[3]{0:T(128)} %get-tuple-element.29.count_ref, ...), custom_call_target="tpu_custom_call" | custom-call | tf_op jit(solution)/shard_map/estimates/pallas_call | solution.py:368
  343.2 2.7 collective-permute-start.32
  345.8 3.2 collective-permute-done.32
  350.2 1.9 collective-permute-start.36
  352.1 3.5 collective-permute-done.34
  356.8 2.1 collective-permute-done.36
  360.5 3.4 collective-permute-start.37
  363.9 2.4 collective-permute-done.35.refs_2_
  366.3 3.2 collective-permute-done.33.refs_1_
  369.5 4.9 %collective-permute-done.37.refs_3_ = f32[2,256,256]{2,1,0:T(8,128)S(1)} collective-permute-done((f32[2,256,256]{2,1,0:T(8,128)S(1)}, f32[2,256,256]{2,1,0:T(8,128)S(1)}, u32[]{:S(2)}, u32[]{:S(2)}) %collective-permute-start.37) | collective-permute-done | bytes 524320 | tf_op jit(solution)/shard_map/ppermute | solution.py:467
  375.2 8.1 %update_frames.3 = (f32[2,256,256]{2,1,0:T(8,128)}, bf16[2,256,256]{2,1,0:T(8,128)(2,1)}, f32[256,256]{1,0:T(8,128)}) custom-call(f32[2,256,256]{2,1,0:T(8,128)} %get-tuple-element.38.frame_ref, f32[2,256,256]{2,1,0:T(8,128)} %get-tuple-element.40.refs_0_, f32[2,256,256]{2,1,0:T(8,128)} %copy-done.12, f32[2,256,256]{2,1,0:T(8,128)} %copy-done.10, ...), custom_call_target="tpu_custom_call" | custom-call | tf_op jit(solution)/shard_map/update_frames/pallas_call | solution.py:400
  383.3 17.9 %all_to_all.15 = f32[32,8,256]{2,1,0:T(8,128)S(1)} all-to-all(f32[32,8,256]{2,1,0:T(8,128)} %bitcast.10), channel_id=1, replica_groups=mesh['gx'=4,'gy_0'=4,'gy_1'=4,'gy_2'=2] {'gy_0','gy_1','gy_2'}, dimensions={0} | all-to-all | bytes 524288 | tf_op jit(solution)/shard_map/all_to_all | solution.py:508
  401.3 11.3 %all_to_all.16 = f32[4,8,256]{2,1,0:T(8,128)S(1)} all-to-all(f32[4,8,256]{2,1,0:T(8,128)S(1)} %broadcast_in_dim.4), channel_id=1, replica_groups=mesh['gx'=4,'gy_0'=4,'gy_1'=4,'gy_2'=2] {'gx'}, dimensions={0} | all-to-all | bytes 65536 | tf_op jit(solution)/shard_map/all_to_all | solution.py:502
  412.6 14.0 %all_to_all.17 = f32[32,8,256]{2,1,0:T(8,128)} all-to-all(f32[32,8,256]{2,1,0:T(8,128)S(1)} %broadcast_in_dim.5), channel_id=1, replica_groups=mesh['gx'=4,'gy_0'=4,'gy_1'=4,'gy_2'=2] {'gy_0','gy_1','gy_2'}, dimensions={0} | all-to-all | bytes 524288 | tf_op jit(solution)/shard_map/all_to_all | solution.py:502
  426.6 11.4 %aligned_rows.1 = (bf16[2,4096,256]{2,1,0:T(8,128)(2,1)}, f32[2,256,256]{2,1,0:T(8,128)}) custom-call(f32[256,256]{1,0:T(8,128)} %bitcast.8, f32[2,256,256]{2,1,0:T(8,128)} %get-tuple-element.48.frame_ref, bf16[2,4096,256]{2,1,0:T(8,128)(2,1)} %patch_ref.1), custom_call_target="tpu_custom_call" | custom-call | tf_op jit(solution)/shard_map/aligned_rows/pallas_call | solution.py:445
  (117 shorter events, 29.5 us)
Async XLA Ops:
  0.6 49.8 %collective-permute-start = (bf16[2,4096,256]{2,1,0:T(8,128)(2,1)}, bf16[2,4096,256]{2,1,0:T(8,128)(2,1)S(1)}, u32[]{:S(2)}, u32[]{:S(2)}) collective-permute-start(bf16[2,4096,256]{2,1,0:T(8,128)(2,1)} %patch_ref.1), channel_id=1, source_target_pairs={{0,8},{1,3},{2,10},{3,5},{4,12},{5,7},{6,14},{7,1},{8,16},{9,11},{... | collective-permute-start | bytes 12582920 | tf_op jit(solution)/shard_map/ppermute | solution.py:467
  2.7 49.5 %collective-permute-start.1 = (bf16[2,4096,256]{2,1,0:T(8,128)(2,1)}, bf16[2,4096,256]{2,1,0:T(8,128)(2,1)S(1)}, u32[]{:S(2)}, u32[]{:S(2)}) collective-permute-start(bf16[2,4096,256]{2,1,0:T(8,128)(2,1)} %patch_ref.1), channel_id=1, source_target_pairs={{0,6},{1,25},{2,0},{3,27},{4,2},{5,29},{6,4},{7,31},{8,14},{9,1},{... | collective-permute-start | bytes 12582920 | tf_op jit(solution)/shard_map/ppermute | solution.py:467
  50.4 71.4 %collective-permute-start.5 = (bf16[2,4096,256]{2,1,0:T(8,128)(2,1)S(1)}, bf16[2,4096,256]{2,1,0:T(8,128)(2,1)}, u32[]{:S(2)}, u32[]{:S(2)}) collective-permute-start(bf16[2,4096,256]{2,1,0:T(8,128)(2,1)S(1)} %collective-permute-done.refs_1_), channel_id=1, source_target_pairs={{0,8},{1,3},{2,10},{3,5},{4,12},{5,7},{6,14},{7,1},{8,16},{9,11},{... | collective-permute-start | bytes 12582920 | tf_op jit(solution)/shard_map/ppermute | solution.py:467
  52.3 69.6 %copy-start.1 = (bf16[2,4096,256]{2,1,0:T(8,128)(2,1)}, bf16[2,4096,256]{2,1,0:T(8,128)(2,1)S(1)}, u32[]{:S(2)}) copy-start(bf16[2,4096,256]{2,1,0:T(8,128)(2,1)S(1)} %collective-permute-done.1.refs_2_) | copy-start | bytes 12582916
  52.3 73.0 %collective-permute-start.6 = (bf16[2,4096,256]{2,1,0:T(8,128)(2,1)S(1)}, bf16[2,4096,256]{2,1,0:T(8,128)(2,1)S(1)}, u32[]{:S(2)}, u32[]{:S(2)}) collective-permute-start(bf16[2,4096,256]{2,1,0:T(8,128)(2,1)S(1)} %collective-permute-done.1.refs_2_), channel_id=1, source_target_pairs={{0,6},{1,25},{2,0},{3,27},{4,2},{5,29},{6,4},{7,31},{8,14},{9,1},{... | collective-permute-start | bytes 12582920 | tf_op jit(solution)/shard_map/ppermute | solution.py:467
  57.0 138.9 %copy-start.27 = (s32[256,2,4]{0,2,1:T(4,128)S(1)}, s32[256,2,4]{0,2,1:T(4,128)}, u32[]{:S(2)}) copy-start(s32[256,2,4]{0,2,1:T(4,128)} %param.8) | copy-start | bytes 24580
  57.0 140.0 %copy-start.28 = (s32[256,2]{0,1:T(2,128)S(1)}, s32[256,2]{0,1:T(2,128)}, u32[]{:S(2)}) copy-start(s32[256,2]{0,1:T(2,128)} %param.7) | copy-start | bytes 6148
  57.0 70.7 %collective-permute-start.2 = (bf16[4096,256]{1,0:T(8,128)(2,1)S(1)}, bf16[4096,256]{1,0:T(8,128)(2,1)S(1)}, u32[]{:S(2)}, u32[]{:S(2)}) collective-permute-start(bf16[4096,256]{1,0:T(8,128)(2,1)S(1)} %slice_bitcast_fusion.1), channel_id=1, source_target_pairs={{0,2},{1,9},{2,4},{3,11},{4,6},{5,13},{6,0},{7,15},{8,10},{9,17},{... | collective-permute-start | bytes 6291464 | tf_op jit(solution)/shard_map/ppermute | solution.py:467
  57.1 135.3 %collective-permute-start.3 = (bf16[2,4096,256]{2,1,0:T(8,128)(2,1)S(1)}, bf16[2,4096,256]{2,1,0:T(8,128)(2,1)}, u32[]{:S(2)}, u32[]{:S(2)}) collective-permute-start(bf16[2,4096,256]{2,1,0:T(8,128)(2,1)S(1)} %collective-permute-done.refs_1_), channel_id=1, source_target_pairs={{0,1},{1,0},{2,3},{3,2},{4,5},{5,4},{6,7},{7,6},{8,9},{9,8},{10,11... | collective-permute-start | bytes 12582920 | tf_op jit(solution)/shard_map/ppermute | solution.py:467
  121.8 73.9 %collective-permute-start.7 = (bf16[2,4096,256]{2,1,0:T(8,128)(2,1)}, bf16[2,4096,256]{2,1,0:T(8,128)(2,1)}, u32[]{:S(2)}, u32[]{:S(2)}) collective-permute-start(bf16[2,4096,256]{2,1,0:T(8,128)(2,1)} %collective-permute-done.5.refs_6_), channel_id=1, source_target_pairs={{0,1},{1,0},{2,3},{3,2},{4,5},{5,4},{6,7},{7,6},{8,9},{9,8},{10,11... | collective-permute-start | bytes 12582920 | tf_op jit(solution)/shard_map/ppermute | solution.py:467
  127.2 25.3 %collective-permute-start.8 = (bf16[4096,256]{1,0:T(8,128)(2,1)S(1)}, bf16[4096,256]{1,0:T(8,128)(2,1)}, u32[]{:S(2)}, u32[]{:S(2)}) collective-permute-start(bf16[4096,256]{1,0:T(8,128)(2,1)S(1)} %slice_bitcast_fusion), channel_id=1, source_target_pairs={{0,6},{1,25},{2,0},{3,27},{4,2},{5,29},{6,4},{7,31},{8,14},{9,1},{... | collective-permute-start | bytes 6291464 | tf_op jit(solution)/shard_map/ppermute | solution.py:467
  127.7 83.2 %copy-start.3 = (bf16[4096,256]{1,0:T(8,128)(2,1)}, bf16[4096,256]{1,0:T(8,128)(2,1)S(1)}, u32[]{:S(2)}) copy-start(bf16[4096,256]{1,0:T(8,128)(2,1)S(1)} %collective-permute-done.2.refs_3_) | copy-start | bytes 6291460
  127.7 64.7 %collective-permute-start.4 = (bf16[4096,256]{1,0:T(8,128)(2,1)S(1)}, bf16[4096,256]{1,0:T(8,128)(2,1)}, u32[]{:S(2)}, u32[]{:S(2)}) collective-permute-start(bf16[4096,256]{1,0:T(8,128)(2,1)S(1)} %collective-permute-done.2.refs_3_), channel_id=1, source_target_pairs={{0,1},{1,0},{2,3},{3,2},{4,5},{5,4},{6,7},{7,6},{8,9},{9,8},{10,11... | collective-permute-start | bytes 6291464 | tf_op jit(solution)/shard_map/ppermute | solution.py:467
  152.5 92.5 %collective-permute-start.9 = (bf16[4096,256]{1,0:T(8,128)(2,1)}, bf16[4096,256]{1,0:T(8,128)(2,1)}, u32[]{:S(2)}, u32[]{:S(2)}) collective-permute-start(bf16[4096,256]{1,0:T(8,128)(2,1)} %collective-permute-done.8.refs_9_), channel_id=1, source_target_pairs={{0,1},{1,0},{2,3},{3,2},{4,5},{5,4},{6,7},{7,6},{8,9},{9,8},{10,11... | collective-permute-start | bytes 6291464 | tf_op jit(solution)/shard_map/ppermute | solution.py:467
  160.9 7.5 %collective-permute-start.10 = (bf16[2,256,256]{2,1,0:T(8,128)(2,1)}, bf16[2,256,256]{2,1,0:T(8,128)(2,1)S(1)}, u32[]{:S(2)}, u32[]{:S(2)}) collective-permute-start(bf16[2,256,256]{2,1,0:T(8,128)(2,1)} %get-tuple-element.30.refs_0_), channel_id=1, source_target_pairs={{0,8},{1,3},{2,10},{3,5},{4,12},{5,7},{6,14},{7,1},{8,16},{9,11},{... | collective-permute-start | bytes 786440 | tf_op jit(solution)/shard_map/ppermute | solution.py:467
  168.4 63.5 %copy-start.15 = (bf16[2,256,256]{2,1,0:T(8,128)(2,1)}, bf16[2,256,256]{2,1,0:T(8,128)(2,1)S(1)}, u32[]{:S(2)}) copy-start(bf16[2,256,256]{2,1,0:T(8,128)(2,1)S(1)} %collective-permute-done.10.refs_1_) | copy-start | bytes 786436
  168.4 5.7 %collective-permute-start.13 = (bf16[2,256,256]{2,1,0:T(8,128)(2,1)}, bf16[2,256,256]{2,1,0:T(8,128)(2,1)S(1)}, u32[]{:S(2)}, u32[]{:S(2)}) collective-permute-start(bf16[2,256,256]{2,1,0:T(8,128)(2,1)} %get-tuple-element.30.refs_0_), channel_id=1, source_target_pairs={{0,6},{1,25},{2,0},{3,27},{4,2},{5,29},{6,4},{7,31},{8,14},{9,1},{... | collective-permute-start | bytes 786440 | tf_op jit(solution)/shard_map/ppermute | solution.py:467
  174.1 57.8 %copy-start.16 = (bf16[2,256,256]{2,1,0:T(8,128)(2,1)}, bf16[2,256,256]{2,1,0:T(8,128)(2,1)S(1)}, u32[]{:S(2)}) copy-start(bf16[2,256,256]{2,1,0:T(8,128)(2,1)S(1)} %collective-permute-done.13.refs_4_) | copy-start | bytes 786436
  174.1 6.6 %collective-permute-start.12 = (bf16[2,256,256]{2,1,0:T(8,128)(2,1)}, bf16[2,256,256]{2,1,0:T(8,128)(2,1)S(1)}, u32[]{:S(2)}, u32[]{:S(2)}) collective-permute-start(bf16[2,256,256]{2,1,0:T(8,128)(2,1)} %get-tuple-element.30.refs_0_), channel_id=1, source_target_pairs={{0,2},{1,9},{2,4},{3,11},{4,6},{5,13},{6,0},{7,15},{8,10},{9,17},{... | collective-permute-start | bytes 786440 | tf_op jit(solution)/shard_map/ppermute | solution.py:467
  180.8 51.2 %copy-start.17 = (bf16[2,256,256]{2,1,0:T(8,128)(2,1)}, bf16[2,256,256]{2,1,0:T(8,128)(2,1)S(1)}, u32[]{:S(2)}) copy-start(bf16[2,256,256]{2,1,0:T(8,128)(2,1)S(1)} %collective-permute-done.12.refs_3_) | copy-start | bytes 786436
  180.8 6.4 %collective-permute-start.11 = (bf16[2,256,256]{2,1,0:T(8,128)(2,1)S(1)}, bf16[2,256,256]{2,1,0:T(8,128)(2,1)S(1)}, u32[]{:S(2)}, u32[]{:S(2)}) collective-permute-start(bf16[2,256,256]{2,1,0:T(8,128)(2,1)S(1)} %collective-permute-done.10.refs_1_), channel_id=1, source_target_pairs={{0,8},{1,3},{2,10},{3,5},{4,12},{5,7},{6,14},{7,1},{8,16},{9,11},{... | collective-permute-start | bytes 786440 | tf_op jit(solution)/shard_map/ppermute | solution.py:467
  187.2 44.7 %copy-start.18 = (bf16[2,256,256]{2,1,0:T(8,128)(2,1)}, bf16[2,256,256]{2,1,0:T(8,128)(2,1)S(1)}, u32[]{:S(2)}) copy-start(bf16[2,256,256]{2,1,0:T(8,128)(2,1)S(1)} %collective-permute-done.11.refs_2_) | copy-start | bytes 786436
  187.2 73.2 %collective-permute-start.15 = (bf16[2,256,256]{2,1,0:T(8,128)(2,1)S(1)}, bf16[2,256,256]{2,1,0:T(8,128)(2,1)}, u32[]{:S(2)}, u32[]{:S(2)}) collective-permute-start(bf16[2,256,256]{2,1,0:T(8,128)(2,1)S(1)} %collective-permute-done.10.refs_1_), channel_id=1, source_target_pairs={{0,1},{1,0},{2,3},{3,2},{4,5},{5,4},{6,7},{7,6},{8,9},{9,8},{10,11... | collective-permute-start | bytes 786440 | tf_op jit(solution)/shard_map/ppermute | solution.py:467
  192.4 68.0 %collective-permute-start.14 = (bf16[2,256,256]{2,1,0:T(8,128)(2,1)S(1)}, bf16[2,256,256]{2,1,0:T(8,128)(2,1)}, u32[]{:S(2)}, u32[]{:S(2)}) collective-permute-start(bf16[2,256,256]{2,1,0:T(8,128)(2,1)S(1)} %collective-permute-done.13.refs_4_), channel_id=1, source_target_pairs={{0,6},{1,25},{2,0},{3,27},{4,2},{5,29},{6,4},{7,31},{8,14},{9,1},{... | collective-permute-start | bytes 786440 | tf_op jit(solution)/shard_map/ppermute | solution.py:467
  192.4 68.0 %collective-permute-start.17 = (bf16[2,256,256]{2,1,0:T(8,128)(2,1)S(1)}, bf16[2,256,256]{2,1,0:T(8,128)(2,1)}, u32[]{:S(2)}, u32[]{:S(2)}) collective-permute-start(bf16[2,256,256]{2,1,0:T(8,128)(2,1)S(1)} %collective-permute-done.12.refs_3_), channel_id=1, source_target_pairs={{0,1},{1,0},{2,3},{3,2},{4,5},{5,4},{6,7},{7,6},{8,9},{9,8},{10,11... | collective-permute-start | bytes 786440 | tf_op jit(solution)/shard_map/ppermute | solution.py:467
  195.8 64.7 %collective-permute-start.16 = (bf16[2,256,256]{2,1,0:T(8,128)(2,1)S(1)}, bf16[2,256,256]{2,1,0:T(8,128)(2,1)}, u32[]{:S(2)}, u32[]{:S(2)}) collective-permute-start(bf16[2,256,256]{2,1,0:T(8,128)(2,1)S(1)} %collective-permute-done.11.refs_2_), channel_id=1, source_target_pairs={{0,1},{1,0},{2,3},{3,2},{4,5},{5,4},{6,7},{7,6},{8,9},{9,8},{10,11... | collective-permute-start | bytes 786440 | tf_op jit(solution)/shard_map/ppermute | solution.py:467
  271.0 16.5 %copy-start.7 = (f32[2,256,256]{2,1,0:T(8,128)S(1)}, f32[2,256,256]{2,1,0:T(8,128)}, u32[]{:S(2)}) copy-start(f32[2,256,256]{2,1,0:T(8,128)} %get-tuple-element.36) | copy-start | bytes 1572868
  271.0 16.5 %copy-start.8 = (f32[2,256,256]{2,1,0:T(8,128)S(1)}, f32[2,256,256]{2,1,0:T(8,128)}, u32[]{:S(2)}) copy-start(f32[2,256,256]{2,1,0:T(8,128)} %get-tuple-element.32) | copy-start | bytes 1572868
  271.0 7.0 %collective-permute-start.18 = (f32[6,256,256]{2,1,0:T(8,128)}, f32[6,256,256]{2,1,0:T(8,128)S(1)}, u32[]{:S(2)}, u32[]{:S(2)}) collective-permute-start(f32[6,256,256]{2,1,0:T(8,128)} %get-tuple-element.33), channel_id=1, source_target_pairs={{0,1},{1,0},{2,3},{3,2},{4,5},{5,4},{6,7},{7,6},{8,9},{9,8},{10,11... | collective-permute-start | bytes 4718600 | tf_op jit(solution)/shard_map/ppermute | solution.py:467
  274.7 9.7 %collective-permute-start.20 = (f32[2,256,256]{2,1,0:T(8,128)}, f32[2,256,256]{2,1,0:T(8,128)S(1)}, u32[]{:S(2)}, u32[]{:S(2)}) collective-permute-start(f32[2,256,256]{2,1,0:T(8,128)} %get-tuple-element.35), channel_id=1, source_target_pairs={{6,0},{25,1},{0,2},{27,3},{2,4},{29,5},{4,6},{31,7},{14,8},{1,9},{... | collective-permute-start | bytes 1572872 | tf_op jit(solution)/shard_map/ppermute | solution.py:467
  279.1 8.4 %collective-permute-start.22 = (f32[2,256,256]{2,1,0:T(8,128)S(1)}, f32[2,256,256]{2,1,0:T(8,128)S(1)}, u32[]{:S(2)}, u32[]{:S(2)}) collective-permute-start(f32[2,256,256]{2,1,0:T(8,128)S(1)} %slice_add_fusion.3), channel_id=1, source_target_pairs={{8,0},{3,1},{10,2},{5,3},{12,4},{7,5},{14,6},{1,7},{16,8},{11,9},{... | collective-permute-start | bytes 1572872 | tf_op jit(solution)/shard_map/ppermute | solution.py:467
  285.6 9.6 %collective-permute-start.21 = (f32[2,256,256]{2,1,0:T(8,128)S(1)}, f32[2,256,256]{2,1,0:T(8,128)S(1)}, u32[]{:S(2)}, u32[]{:S(2)}) collective-permute-start(f32[2,256,256]{2,1,0:T(8,128)S(1)} %add.39), channel_id=1, source_target_pairs={{6,0},{25,1},{0,2},{27,3},{2,4},{29,5},{4,6},{31,7},{14,8},{1,9},{... | collective-permute-start | bytes 1572872 | tf_op jit(solution)/shard_map/ppermute | solution.py:467
  287.7 11.2 %collective-permute-start.19 = (f32[2,256,256]{2,1,0:T(8,128)S(1)}, f32[2,256,256]{2,1,0:T(8,128)S(1)}, u32[]{:S(2)}, u32[]{:S(2)}) collective-permute-start(f32[2,256,256]{2,1,0:T(8,128)S(1)} %get-tuple-element.54), channel_id=1, source_target_pairs={{2,0},{9,1},{4,2},{11,3},{6,4},{13,5},{0,6},{15,7},{10,8},{17,9},{... | collective-permute-start | bytes 1572872 | tf_op jit(solution)/shard_map/ppermute | solution.py:467
  288.6 13.4 %collective-permute-start.23 = (f32[2,256,256]{2,1,0:T(8,128)S(1)}, f32[2,256,256]{2,1,0:T(8,128)S(1)}, u32[]{:S(2)}, u32[]{:S(2)}) collective-permute-start(f32[2,256,256]{2,1,0:T(8,128)S(1)} %get-tuple-element.53), channel_id=1, source_target_pairs={{8,0},{3,1},{10,2},{5,3},{12,4},{7,5},{14,6},{1,7},{16,8},{11,9},{... | collective-permute-start | bytes 1572872 | tf_op jit(solution)/shard_map/ppermute | solution.py:467
  311.0 7.4 %collective-permute-start.24 = (bf16[2,256,256]{2,1,0:T(8,128)(2,1)}, bf16[2,256,256]{2,1,0:T(8,128)(2,1)S(1)}, u32[]{:S(2)}, u32[]{:S(2)}) collective-permute-start(bf16[2,256,256]{2,1,0:T(8,128)(2,1)} %get-tuple-element.39.refs_0_), channel_id=1, source_target_pairs={{0,8},{1,3},{2,10},{3,5},{4,12},{5,7},{6,14},{7,1},{8,16},{9,11},{... | collective-permute-start | bytes 786440 | tf_op jit(solution)/shard_map/ppermute | solution.py:467
  313.1 11.9 %collective-permute-start.27 = (bf16[2,256,256]{2,1,0:T(8,128)(2,1)}, bf16[2,256,256]{2,1,0:T(8,128)(2,1)S(1)}, u32[]{:S(2)}, u32[]{:S(2)}) collective-permute-start(bf16[2,256,256]{2,1,0:T(8,128)(2,1)} %get-tuple-element.39.refs_0_), channel_id=1, source_target_pairs={{0,6},{1,25},{2,0},{3,27},{4,2},{5,29},{6,4},{7,31},{8,14},{9,1},{... | collective-permute-start | bytes 786440 | tf_op jit(solution)/shard_map/ppermute | solution.py:467
  318.4 7.6 %collective-permute-start.26 = (bf16[2,256,256]{2,1,0:T(8,128)(2,1)}, bf16[2,256,256]{2,1,0:T(8,128)(2,1)S(1)}, u32[]{:S(2)}, u32[]{:S(2)}) collective-permute-start(bf16[2,256,256]{2,1,0:T(8,128)(2,1)} %get-tuple-element.39.refs_0_), channel_id=1, source_target_pairs={{0,2},{1,9},{2,4},{3,11},{4,6},{5,13},{6,0},{7,15},{8,10},{9,17},{... | collective-permute-start | bytes 786440 | tf_op jit(solution)/shard_map/ppermute | solution.py:467
  318.4 9.9 %collective-permute-start.25 = (bf16[2,256,256]{2,1,0:T(8,128)(2,1)S(1)}, bf16[2,256,256]{2,1,0:T(8,128)(2,1)S(1)}, u32[]{:S(2)}, u32[]{:S(2)}) collective-permute-start(bf16[2,256,256]{2,1,0:T(8,128)(2,1)S(1)} %collective-permute-done.24.refs_1_), channel_id=1, source_target_pairs={{0,8},{1,3},{2,10},{3,5},{4,12},{5,7},{6,14},{7,1},{8,16},{9,11},{... | collective-permute-start | bytes 786440 | tf_op jit(solution)/shard_map/ppermute | solution.py:467
  320.2 10.9 %collective-permute-start.29 = (bf16[2,256,256]{2,1,0:T(8,128)(2,1)S(1)}, bf16[2,256,256]{2,1,0:T(8,128)(2,1)S(1)}, u32[]{:S(2)}, u32[]{:S(2)}) collective-permute-start(bf16[2,256,256]{2,1,0:T(8,128)(2,1)S(1)} %collective-permute-done.24.refs_1_), channel_id=1, source_target_pairs={{0,1},{1,0},{2,3},{3,2},{4,5},{5,4},{6,7},{7,6},{8,9},{9,8},{10,11... | collective-permute-start | bytes 786440 | tf_op jit(solution)/shard_map/ppermute | solution.py:467
  325.0 6.1 %collective-permute-start.28 = (bf16[2,256,256]{2,1,0:T(8,128)(2,1)S(1)}, bf16[2,256,256]{2,1,0:T(8,128)(2,1)S(1)}, u32[]{:S(2)}, u32[]{:S(2)}) collective-permute-start(bf16[2,256,256]{2,1,0:T(8,128)(2,1)S(1)} %collective-permute-done.27.refs_4_), channel_id=1, source_target_pairs={{0,6},{1,25},{2,0},{3,27},{4,2},{5,29},{6,4},{7,31},{8,14},{9,1},{... | collective-permute-start | bytes 786440 | tf_op jit(solution)/shard_map/ppermute | solution.py:467
  326.0 5.0 %collective-permute-start.31 = (bf16[2,256,256]{2,1,0:T(8,128)(2,1)S(1)}, bf16[2,256,256]{2,1,0:T(8,128)(2,1)S(1)}, u32[]{:S(2)}, u32[]{:S(2)}) collective-permute-start(bf16[2,256,256]{2,1,0:T(8,128)(2,1)S(1)} %collective-permute-done.26.refs_3_), channel_id=1, source_target_pairs={{0,1},{1,0},{2,3},{3,2},{4,5},{5,4},{6,7},{7,6},{8,9},{9,8},{10,11... | collective-permute-start | bytes 786440 | tf_op jit(solution)/shard_map/ppermute | solution.py:467
  328.4 2.7 collective-permute-start.30
  343.2 5.9 %collective-permute-start.32 = (f32[6,256,256]{2,1,0:T(8,128)}, f32[6,256,256]{2,1,0:T(8,128)S(1)}, u32[]{:S(2)}, u32[]{:S(2)}) collective-permute-start(f32[6,256,256]{2,1,0:T(8,128)} %get-tuple-element.42), channel_id=1, source_target_pairs={{0,1},{1,0},{2,3},{3,2},{4,5},{5,4},{6,7},{7,6},{8,9},{9,8},{10,11... | collective-permute-start | bytes 4718600 | tf_op jit(solution)/shard_map/ppermute | solution.py:467
  345.8 9.7 %collective-permute-start.34 = (f32[2,256,256]{2,1,0:T(8,128)}, f32[2,256,256]{2,1,0:T(8,128)S(1)}, u32[]{:S(2)}, u32[]{:S(2)}) collective-permute-start(f32[2,256,256]{2,1,0:T(8,128)} %get-tuple-element.44), channel_id=1, source_target_pairs={{6,0},{25,1},{0,2},{27,3},{2,4},{29,5},{4,6},{31,7},{14,8},{1,9},{... | collective-permute-start | bytes 1572872 | tf_op jit(solution)/shard_map/ppermute | solution.py:467
  350.2 8.7 %collective-permute-start.36 = (f32[2,256,256]{2,1,0:T(8,128)S(1)}, f32[2,256,256]{2,1,0:T(8,128)S(1)}, u32[]{:S(2)}, u32[]{:S(2)}) collective-permute-start(f32[2,256,256]{2,1,0:T(8,128)S(1)} %slice_add_fusion), channel_id=1, source_target_pairs={{8,0},{3,1},{10,2},{5,3},{12,4},{7,5},{14,6},{1,7},{16,8},{11,9},{... | collective-permute-start | bytes 1572872 | tf_op jit(solution)/shard_map/ppermute | solution.py:467
  356.7 9.6 %collective-permute-start.35 = (f32[2,256,256]{2,1,0:T(8,128)S(1)}, f32[2,256,256]{2,1,0:T(8,128)S(1)}, u32[]{:S(2)}, u32[]{:S(2)}) collective-permute-start(f32[2,256,256]{2,1,0:T(8,128)S(1)} %add.44), channel_id=1, source_target_pairs={{6,0},{25,1},{0,2},{27,3},{2,4},{29,5},{4,6},{31,7},{14,8},{1,9},{... | collective-permute-start | bytes 1572872 | tf_op jit(solution)/shard_map/ppermute | solution.py:467
  359.1 10.5 %collective-permute-start.33 = (f32[2,256,256]{2,1,0:T(8,128)S(1)}, f32[2,256,256]{2,1,0:T(8,128)S(1)}, u32[]{:S(2)}, u32[]{:S(2)}) collective-permute-start(f32[2,256,256]{2,1,0:T(8,128)S(1)} %get-tuple-element.52), channel_id=1, source_target_pairs={{2,0},{9,1},{4,2},{11,3},{6,4},{13,5},{0,6},{15,7},{10,8},{17,9},{... | collective-permute-start | bytes 1572872 | tf_op jit(solution)/shard_map/ppermute | solution.py:467
  360.5 13.9 %collective-permute-start.37 = (f32[2,256,256]{2,1,0:T(8,128)S(1)}, f32[2,256,256]{2,1,0:T(8,128)S(1)}, u32[]{:S(2)}, u32[]{:S(2)}) collective-permute-start(f32[2,256,256]{2,1,0:T(8,128)S(1)} %get-tuple-element.51), channel_id=1, source_target_pairs={{8,0},{3,1},{10,2},{5,3},{12,4},{7,5},{14,6},{1,7},{16,8},{11,9},{... | collective-permute-start | bytes 1572872 | tf_op jit(solution)/shard_map/ppermute | solution.py:467
  (19 other events, 105.8 us)
where the time goes:
time: 440 us; the launch traced here: 439 us
  waiting for transfers between devices  199 us (45%)
  Pallas kernels  118 us (27%)
  starting transfers between devices  62.7 us (14%)
  blocking collectives  43.2 us (10%)
  local copies, waits for them, and re-layouts  9.61 us (2%)
  other arithmetic  5.44 us (1%)
    ppermute x38, waiting for transfers between devices, send(): return lax.ppermute(value, GY, perm)  199 us
    ppermute x38, starting transfers between devices, send(): return lax.ppermute(value, GY, perm)  62.7 us
    pallas_call x3, Pallas kernels, make_rotations(): pl.pallas_call(functools.partial(rotation_kernel, layout, ready, size), i...  49.4 us
    all_to_all x2, blocking collectives, from_everyone(): lax.all_to_all(jnp.broadcast_to(value[None], (size, *value.shape)), axis,...  25.3 us
    pallas_call x2, Pallas kernels, make_estimates(): pl.pallas_call(estimate_kernel, in_specs=[SM, SM, HBM] + [HBM] * SLOTS, o...  21 us
    all_to_all x1, blocking collectives, sum_over_all(): lax.all_to_all(value.reshape(size, rows, D), GY, 0, 0, tiled=True).sum(0)  17.9 us
    pallas_call x2, Pallas kernels, make_update(): pl.pallas_call(update_kernel, in_specs=[VM] * (1 + len(parts)), out_specs...  16.3 us
    pallas_call x1, Pallas kernels, make_index(): pl.pallas_call(index_kernel, in_specs=[SM] * 4, out_specs=[SM] * 2, out_s...  12.5 us
  transfers between devices with their start and end apart: 38, of which 22 were waited for; matrix products, arithmetic and copies ran while one was open for 2% of the time, Pallas kernels for 16%

commit v1 on v0

--- a/solution.py
+++ b/solution.py
@@ -70,7 +70,7 @@
     return [same[m] + [same[m ^ 1][k] for k in CROSS] for m in range(DEVS)]
 
 
-READY = ((0, 0), (0, 0), (1, 1), (0, 2), (0, 0), (1, 1), (0, 0), (1, 1), (0, 2))
+READY = ((0, 0), (0, 0), (1, 1), (2, 2), (0, 0), (1, 1), (0, 0), (1, 1), (2, 2))
 CLASSES = 3
 CHOICES = 3
 
@@ -92,12 +92,8 @@
                 for m, i, j in places:
                     ready = max(READY[i][pa], READY[j][pb])
                     ranked[m] = min(ranked.get(m, (9,)), (ready, i, j))
-                first = min(r[0] for r in ranked.values())
-                codes = [
-                    ((r * DEVS + m) << 8) | (i << 4) | j for m, (r, i, j) in sorted(ranked.items()) if r == first
-                ]
-                turn = (a + b) % len(codes)
-                codes = (codes[turn:] + codes[:turn])[:CHOICES]
+                codes = [((r * DEVS + m) << 8) | (i << 4) | j for r, m, i, j in sorted((r, m, i, j) for m, (r, i, j) in ranked.items())]
+                codes = codes[:CHOICES]
                 codes += codes[-1:] * (CHOICES - len(codes))
                 table[a, pa, b, pb] = codes
     return table.reshape(-1)
@@ -149,25 +145,33 @@
 
 def index_kernel(me_ref, table_ref, ends_ref, blocks_ref, info_ref, count_ref, load_ref):
     me, base = me_ref[0], me_ref[1]
-    for n in range(CLASSES * DEVS):
+    for n in range((CLASSES + 1) * DEVS):
         load_ref[n] = 0
+
+    def cost(code):
+        place = code >> 8
+        own = load_ref[place]
+        late = jnp.where(place >= (CLASSES - 1) * DEVS, 2 * own + 4, 0)
+        return own + late + load_ref[CLASSES * DEVS + (place & (DEVS - 1))]
 
     def step(q, carry):
         a, b = ends_ref[2 * q] - base, ends_ref[2 * q + 1] - base
         first = (a * (DEVS * PER) + b) * CHOICES
         code = table_ref[first]
-        least = load_ref[code >> 8]
+        least = cost(code)
         for k in range(1, CHOICES):
             other = table_ref[first + k]
-            less = load_ref[other >> 8]
+            less = cost(other)
             code = jnp.where(less < least, other, code)
             least = jnp.minimum(less, least)
         place = code >> 8
-        load_ref[place] = least + 1
-
-        @pl.when((place & (DEVS - 1)) == me)
+        device, ahead = place & (DEVS - 1), load_ref[place]
+        load_ref[place] = ahead + 1
+        load_ref[CLASSES * DEVS + device] += 1
+
+        @pl.when(device == me)
         def _():
-            line = ((place >> 5) * MAX_PAIRS + least) * INFO
+            line = ((place >> 5) * MAX_PAIRS + ahead) * INFO
             info_ref[line] = ((code >> 4) & 15) * PER + (a & 1)
             info_ref[line + 1] = (code & 15) * PER + (b & 1)
             for k in range(2 * OVB):
@@ -189,7 +193,7 @@
             jax.ShapeDtypeStruct((CLASSES * MAX_PAIRS * INFO,), jnp.int32),
             jax.ShapeDtypeStruct((CLASSES,), jnp.int32),
         ],
-        scratch_shapes=[pltpu.SMEM((CLASSES * DEVS,), jnp.int32)],
+        scratch_shapes=[pltpu.SMEM(((CLASSES + 1) * DEVS,), jnp.int32)],
         name="pair_index",
     )(me, table, ends, blocks)
 
@@ -319,8 +323,8 @@
             line = jnp.where(j >= ends[c - 1], c * MAX_PAIRS + j - ends[c - 1], line)
         return line * INFO
 
-    def rot_copy(j, buf):
-        return pltpu.make_async_copy(rot_ref.at[j], rot.at[buf], rot_sem.at[buf])
+    def rot_copy(t, buf):
+        return pltpu.make_async_copy(rot_ref.at[pl.ds(2 * t, 2)], rot.at[buf], rot_sem.at[buf])
 
     copies = [
         pltpu.make_async_copy(lows[s], frames.at[pl.ds(s * PER, PER)], frame_sem.at[s])
@@ -337,23 +341,35 @@
     for copy in copies:
         copy.wait()
 
-    def step(j, carry):
-        buf = j & 1
-
-        @pl.when(j + 1 < count)
+    def step(t, carry):
+        buf = t & 1
+
+        @pl.when(2 * t + 2 < count)
         def _():
-            rot_copy(j + 1, 1 - buf).start()
-
-        rot_copy(j, buf).wait()
-        line = line_of(j)
-        sa, sb = info_ref[line], info_ref[line + 1]
-        high, rest = halves(rot[buf])
-        fa, fb = frames[sa], frames[sb]
-        acc[sa] += dot(high, fb, 0, 0) + dot(rest, fb, 0, 0)
-        acc[sb] += dot(high, fa) + dot(rest, fa)
+            rot_copy(t + 1, 1 - buf).start()
+
+        rot_copy(t, buf).wait()
+        found = []
+        for i in range(2):
+            line = line_of(jnp.minimum(2 * t + i, count - 1))
+            sa, sb = info_ref[line], info_ref[line + 1]
+            high, rest = halves(rot[buf, i])
+            fa, fb = frames[sa], frames[sb]
+            found.append((sa, dot(high, fb, 0, 0) + dot(rest, fb, 0, 0), sb, dot(high, fa) + dot(rest, fa)))
+
+        def add(sa, ea, sb, eb):
+            acc[sa] += ea
+            acc[sb] += eb
+
+        add(*found[0])
+
+        @pl.when(2 * t + 1 < count)
+        def _():
+            add(*found[1])
+
         return carry
 
-    lax.fori_loop(0, count, step, 0)
+    lax.fori_loop(0, (count + 1) // 2, step, 0)
     parts = [(s * PER, PER) for s in range(OWN)] + [(OWN * PER, len(CROSS) * PER)]
     copies = [
         pltpu.make_async_copy(acc.at[pl.ds(*part)], outs[n], out_sem.at[n]) for n, part in enumerate(parts)
@@ -374,7 +390,7 @@
         scratch_shapes=[
             pltpu.VMEM((SLOTS * PER, D, D), BF16),
             pltpu.VMEM((SLOTS * PER, D, D), F32),
-            pltpu.VMEM((2, D, D), F32),
+            pltpu.VMEM((2, 2, D, D), F32),
             pltpu.SemaphoreType.DMA((SLOTS,)),
             pltpu.SemaphoreType.DMA((2,)),
             pltpu.SemaphoreType.DMA((OWN + 1,)),
@@ -468,8 +484,8 @@
 
 
 LAYOUT = (
-    ((0, 0), (0, 1), (1, 0), (1, 1), (6, 0), (6, 1), (3, None), (9, None), (2, 0), (2, 1), (7, 0), (7, 1))
-    + ((4, 0), (4, 1), (8, 0), (8, 1), (5, None), (10, None))
+    ((0, 0), (0, 1), (1, 0), (1, 1), (4, 0), (4, 1), (7, None), (8, None), (2, 0), (2, 1), (5, 0), (5, 1))
+    + ((3, 0), (3, 1), (6, 0), (6, 1), (9, None), (10, None))
 )
 
 
@@ -515,7 +531,6 @@
     base = lax.axis_index("gx").astype(jnp.int32) * (DEVS * PER)
     one = send(patches, step_perm(UP))
     four = send(patches, step_perm(LEFT))
-    three_0 = send(patches[0], step_perm(RIGHT))
     info, count = make_index(
         jnp.stack([me, base]),
         jnp.asarray(meeting_table()),
@@ -527,16 +542,15 @@
     two = send(one, step_perm(UP))
     five = send(four, step_perm(LEFT))
     cross_1 = send(one, SIBLING)
-    cross_3_0 = send(three_0, SIBLING)
-    arrays = [patches, one, four, three_0, cross_1, cross_3_0]
+    arrays = [patches, one, four, cross_1]
     rot = make_rotations(info, count, arrays, LAYOUT, 0, BATCH)
+    three_0 = send(patches[0], step_perm(RIGHT))
     three_1 = send(five[1], step_perm(LEFT))
     cross_2 = send(two, SIBLING)
     arrays += [two, five, cross_2]
     rot = make_rotations(info, count, arrays, LAYOUT, 1, BATCH, rot)
-    cross_3_1 = send(three_1, SIBLING)
-    arrays += [three_1, cross_3_1]
-    rot = make_rotations(info, count, arrays, LAYOUT, 2, 2, rot)
+    arrays += [three_0, three_1, send(three_0, SIBLING), send(three_1, SIBLING)]
+    rot = make_rotations(info, count, arrays, LAYOUT, 2, 3, rot)
     for sweep in range(SWEEPS):
         if sweep:
             lows = spread_frames(low)

time: 440 us -> 429 us (0.975)
  Pallas kernels: 118 us -> 102 us
  starting transfers between devices: 62.7 us -> 71.2 us
  blocking collectives: 43.2 us -> 35.7 us
  waiting for transfers between devices: 199 us -> 204 us
    pallas_call x3, Pallas kernels: 49.4 us -> 36 us  [make_rotations(): pl.pallas_call(functools.partial(rotation_kernel, layout, ready, size), i...]
    ppermute x38, starting transfers between devices: 62.7 us -> 71.2 us  [send(): return lax.ppermute(value, GY, perm)]
    all_to_all x2, blocking collectives: 25.3 us -> 20.3 us  [from_everyone(): lax.all_to_all(jnp.broadcast_to(value[None], (size, *value.shape)), axis,...]
    ppermute x38, waiting for transfers between devices: 199 us -> 204 us  [send(): return lax.ppermute(value, GY, perm)]
    pallas_call x2, Pallas kernels: 21 us -> 16.1 us  [make_estimates(): pl.pallas_call(estimate_kernel, in_specs=[SM, SM, HBM] + [HBM] * SLOTS, o...]
  transfers between devices with their start and end apart: 38 -> 38, of which waited for: 22 -> 23; matrix products, arithmetic and copies ran while one was open for 2% -> 2% of each run, Pallas kernels for 16% -> 14%
where the time goes in v1:
time: 429 us; the launch traced here: 427 us
  waiting for transfers between devices  204 us (48%)
  Pallas kernels  102 us (24%)
  starting transfers between devices  71.2 us (17%)
  blocking collectives  35.7 us (8%)
  local copies, waits for them, and re-layouts  8.78 us (2%)
  other arithmetic  5.44 us (1%)
    ppermute x38, waiting for transfers between devices, send(): return lax.ppermute(value, GY, perm)  204 us
    ppermute x38, starting transfers between devices, send(): return lax.ppermute(value, GY, perm)  71.2 us
    pallas_call x3, Pallas kernels, make_rotations(): pl.pallas_call(functools.partial(rotation_kernel, layout, ready, size), i...  36 us
    all_to_all x2, blocking collectives, from_everyone(): lax.all_to_all(jnp.broadcast_to(value[None], (size, *value.shape)), axis,...  20.3 us
    pallas_call x2, Pallas kernels, make_update(): pl.pallas_call(update_kernel, in_specs=[VM] * (1 + len(parts)), out_specs...  16.3 us
    pallas_call x2, Pallas kernels, make_estimates(): pl.pallas_call(estimate_kernel, in_specs=[SM, SM, HBM] + [HBM] * SLOTS, o...  16.1 us
    all_to_all x1, blocking collectives, sum_over_all(): lax.all_to_all(value.reshape(size, rows, D), GY, 0, 0, tiled=True).sum(0)  15.3 us
    pallas_call x1, Pallas kernels, make_index(): pl.pallas_call(index_kernel, in_specs=[SM] * 4, out_specs=[SM] * 2, out_s...  14.4 us
  transfers between devices with their start and end apart: 38, of which 23 were waited for; matrix products, arithmetic and copies ran while one was open for 2% of the time, Pallas kernels for 14%

profile of v1, /device:TPU:1, one launch (start us, length us, event | category | flops | bytes accessed | tf_op | source)
XLA Modules:
  0.0 427.5 jit_solution(17320526852721534203)
XLA Ops:
  0.6 2.1 collective-permute-start
  2.7 3.8 collective-permute-start.1
  6.5 43.9 %collective-permute-done.refs_1_ = bf16[2,4096,256]{2,1,0:T(8,128)(2,1)S(1)} collective-permute-done((bf16[2,4096,256]{2,1,0:T(8,128)(2,1)}, bf16[2,4096,256]{2,1,0:T(8,128)(2,1)S(1)}, u32[]{:S(2)}, u32[]{:S(2)}) %collective-permute-start) | collective-permute-done | bytes 4194336 | tf_op jit(solution)/shard_map/ppermute | solution.py:483
  52.3 3.0 collective-permute-start.4
  58.7 63.1 %collective-permute-done.3.refs_4_ = bf16[2,4096,256]{2,1,0:T(8,128)(2,1)} collective-permute-done((bf16[2,4096,256]{2,1,0:T(8,128)(2,1)S(1)}, bf16[2,4096,256]{2,1,0:T(8,128)(2,1)}, u32[]{:S(2)}, u32[]{:S(2)}) %collective-permute-start.3) | collective-permute-done | bytes 4194336 | tf_op jit(solution)/shard_map/ppermute | solution.py:483
  121.8 3.4 collective-permute-start.5
  125.4 1.8 copy-done.2
  127.7 2.2 collective-permute-start.8
  130.0 22.5 %collective-permute-done.7.refs_8_ = bf16[4096,256]{1,0:T(8,128)(2,1)} collective-permute-done((bf16[4096,256]{1,0:T(8,128)(2,1)S(1)}, bf16[4096,256]{1,0:T(8,128)(2,1)}, u32[]{:S(2)}, u32[]{:S(2)}) %collective-permute-start.7) | collective-permute-done | bytes 2097184 | tf_op jit(solution)/shard_map/ppermute | solution.py:483
  153.5 7.4 %start_frames.1 = (f32[2,256,256]{2,1,0:T(8,128)}, bf16[2,256,256]{2,1,0:T(8,128)(2,1)}) custom-call(f32[2,256,256]{2,1,0:T(8,128)} %start_ref.1), custom_call_target="tpu_custom_call" | custom-call | tf_op jit(solution)/shard_map/start_frames/pallas_call | solution.py:298
  161.9 6.5 %collective-permute-done.10.refs_1_ = bf16[2,256,256]{2,1,0:T(8,128)(2,1)S(1)} collective-permute-done((bf16[2,256,256]{2,1,0:T(8,128)(2,1)}, bf16[2,256,256]{2,1,0:T(8,128)(2,1)S(1)}, u32[]{:S(2)}, u32[]{:S(2)}) %collective-permute-start.10) | collective-permute-done | bytes 262176 | tf_op jit(solution)/shard_map/ppermute | solution.py:483
  168.9 5.2 %collective-permute-done.13.refs_4_ = bf16[2,256,256]{2,1,0:T(8,128)(2,1)S(1)} collective-permute-done((bf16[2,256,256]{2,1,0:T(8,128)(2,1)}, bf16[2,256,256]{2,1,0:T(8,128)(2,1)S(1)}, u32[]{:S(2)}, u32[]{:S(2)}) %collective-permute-start.13) | collective-permute-done | bytes 262176 | tf_op jit(solution)/shard_map/ppermute | solution.py:483
  174.1 6.6 %collective-permute-done.12.refs_3_ = bf16[2,256,256]{2,1,0:T(8,128)(2,1)S(1)} collective-permute-done((bf16[2,256,256]{2,1,0:T(8,128)(2,1)}, bf16[2,256,256]{2,1,0:T(8,128)(2,1)S(1)}, u32[]{:S(2)}, u32[]{:S(2)}) %collective-permute-start.12) | collective-permute-done | bytes 262176 | tf_op jit(solution)/shard_map/ppermute | solution.py:483
  180.8 6.4 %collective-permute-done.11.refs_2_ = bf16[2,256,256]{2,1,0:T(8,128)(2,1)S(1)} collective-permute-done((bf16[2,256,256]{2,1,0:T(8,128)(2,1)S(1)}, bf16[2,256,256]{2,1,0:T(8,128)(2,1)S(1)}, u32[]{:S(2)}, u32[]{:S(2)}) %collective-permute-start.11) | collective-permute-done | bytes 262176 | tf_op jit(solution)/shard_map/ppermute | solution.py:483
  187.2 5.2 %collective-permute-start.15 = (bf16[2,256,256]{2,1,0:T(8,128)(2,1)S(1)}, bf16[2,256,256]{2,1,0:T(8,128)(2,1)}, u32[]{:S(2)}, u32[]{:S(2)}) collective-permute-start(bf16[2,256,256]{2,1,0:T(8,128)(2,1)S(1)} %collective-permute-done.10.refs_1_), channel_id=1, source_target_pairs={{0,1},{1,0},{2,3},{3,2},{4,5},{5,4},{6,7},{7,6},{8,9},{9,8},{10,11... | collective-permute-start | bytes 786440 | tf_op jit(solution)/shard_map/ppermute | solution.py:483
  192.4 3.3 collective-permute-start.17
  198.5 14.4 %pair_index.1 = (s32[4320]{0:T(1024)}, s32[3]{0:T(128)}) custom-call(s32[2]{0:T(128)} %pad_add_fusion.me_ref, s32[12288]{0:T(1024)} %constant.25.clone.table_ref, s32[512]{0:T(512)} %reshape.20.ends_ref, s32[2048]{0:T(1024)} %reshape.21.blocks_ref), custom_call_target="tpu_custom_call" | custom-call | tf_op jit(solution)/shard_map/pair_index/pallas_call | solution.py:188
  212.8 12.3 %shard_map.76.refs_7_ = f32[148,256,256]{2,1,0:T(8,128)} custom-call(s32[4320]{0:T(1024)} %get-tuple-element.28.info_ref, s32[3]{0:T(128)} %get-tuple-element.29.count_ref, bf16[2,4096,256]{2,1,0:T(8,128)(2,1)} %patch_ref.1, bf16[2,4096,256]{2,1,0:T(8,128)(2,1)} %copy-done, bf16[2,4096,256]{2,1,0:T(8,128)(2,1)} %copy-done.1, ...), custom_call_target="tpu_custom_call" | custom-call | tf_op jit(solution)/shard_map/pallas_call | solution.py:273
  225.2 12.8 %shard_map.77.refs_11_ = f32[148,256,256]{2,1,0:T(8,128)} custom-call(s32[4320]{0:T(1024)} %get-tuple-element.28.info_ref, s32[3]{0:T(128)} %get-tuple-element.29.count_ref, bf16[2,4096,256]{2,1,0:T(8,128)(2,1)} %patch_ref.1, bf16[2,4096,256]{2,1,0:T(8,128)(2,1)} %copy-done, bf16[2,4096,256]{2,1,0:T(8,128)(2,1)} %copy-done.1, ...), custom_call_target="tpu_custom_call", output_to_operand_aliasing={{}: (9, {})} | custom-call | tf_op jit(solution)/shard_map/pallas_call | solution.py:273
  238.0 10.9 %shard_map.78.rot_ref = f32[148,256,256]{2,1,0:T(8,128)} custom-call(s32[4320]{0:T(1024)} %get-tuple-element.28.info_ref, s32[3]{0:T(128)} %get-tuple-element.29.count_ref, bf16[2,4096,256]{2,1,0:T(8,128)(2,1)} %patch_ref.1, bf16[2,4096,256]{2,1,0:T(8,128)(2,1)} %copy-done, bf16[2,4096,256]{2,1,0:T(8,128)(2,1)} %copy-done.1, ...), custom_call_target="tpu_custom_call", output_to_operand_aliasing={{}: (13, {})} | custom-call | tf_op jit(solution)/shard_map/pallas_call | solution.py:273
  248.9 8.1 %estimates.2 = (f32[2,256,256]{2,1,0:T(8,128)}, f32[2,256,256]{2,1,0:T(8,128)}, f32[2,256,256]{2,1,0:T(8,128)}, f32[2,256,256]{2,1,0:T(8,128)}, f32[2,256,256]{2...) custom-call(s32[4320]{0:T(1024)} %get-tuple-element.28.info_ref, s32[3]{0:T(128)} %get-tuple-element.29.count_ref, ...), custom_call_target="tpu_custom_call" | custom-call | tf_op jit(solution)/shard_map/estimates/pallas_call | solution.py:384
  257.0 18.7 %collective-permute-start.18 = (f32[6,256,256]{2,1,0:T(8,128)}, f32[6,256,256]{2,1,0:T(8,128)S(1)}, u32[]{:S(2)}, u32[]{:S(2)}) collective-permute-start(f32[6,256,256]{2,1,0:T(8,128)} %get-tuple-element.33), channel_id=1, source_target_pairs={{0,1},{1,0},{2,3},{3,2},{4,5},{5,4},{6,7},{7,6},{8,9},{9,8},{10,11... | collective-permute-start | bytes 4718600 | tf_op jit(solution)/shard_map/ppermute | solution.py:483
  275.8 3.2 collective-permute-done.18
  280.9 4.6 %collective-permute-done.20 = f32[2,256,256]{2,1,0:T(8,128)S(1)} collective-permute-done((f32[2,256,256]{2,1,0:T(8,128)}, f32[2,256,256]{2,1,0:T(8,128)S(1)}, u32[]{:S(2)}, u32[]{:S(2)}) %collective-permute-start.20) | collective-permute-done | bytes 524320 | tf_op jit(solution)/shard_map/ppermute | solution.py:483
  286.7 1.8 collective-permute-done.22
  290.5 5.7 %collective-permute-done.21.refs_2_ = f32[2,256,256]{2,1,0:T(8,128)S(1)} collective-permute-done((f32[2,256,256]{2,1,0:T(8,128)S(1)}, f32[2,256,256]{2,1,0:T(8,128)S(1)}, u32[]{:S(2)}, u32[]{:S(2)}) %collective-permute-start.21) | collective-permute-done | bytes 524320 | tf_op jit(solution)/shard_map/ppermute | solution.py:483
  296.2 3.7 collective-permute-done.19.refs_1_
  299.9 2.8 collective-permute-done.23.refs_3_
  303.6 8.2 %update_frames.2 = (f32[2,256,256]{2,1,0:T(8,128)}, bf16[2,256,256]{2,1,0:T(8,128)(2,1)}, f32[256,256]{1,0:T(8,128)}) custom-call(f32[2,256,256]{2,1,0:T(8,128)} %get-tuple-element.27.frame_ref, f32[2,256,256]{2,1,0:T(8,128)} %get-tuple-element.31.refs_0_, f32[2,256,256]{2,1,0:T(8,128)} %copy-done.11, f32[2,256,256]{2,1,0:T(8,128)} %copy-done.9, ...), custom_call_target="tpu_custom_call" | custom-call | tf_op jit(solution)/shard_map/update_frames/pallas_call | solution.py:416
  313.2 5.5 %collective-permute-done.24.refs_1_ = bf16[2,256,256]{2,1,0:T(8,128)(2,1)S(1)} collective-permute-done((bf16[2,256,256]{2,1,0:T(8,128)(2,1)}, bf16[2,256,256]{2,1,0:T(8,128)(2,1)S(1)}, u32[]{:S(2)}, u32[]{:S(2)}) %collective-permute-start.24) | collective-permute-done | bytes 262176 | tf_op jit(solution)/shard_map/ppermute | solution.py:483
  318.7 3.7 collective-permute-start.29
  322.4 2.5 collective-permute-start.28
  325.4 4.2 collective-permute-start.30
  331.5 8.1 %estimates.3 = (f32[2,256,256]{2,1,0:T(8,128)}, f32[2,256,256]{2,1,0:T(8,128)}, f32[2,256,256]{2,1,0:T(8,128)}, f32[2,256,256]{2,1,0:T(8,128)}, f32[2,256,256]{2...) custom-call(s32[4320]{0:T(1024)} %get-tuple-element.28.info_ref, s32[3]{0:T(128)} %get-tuple-element.29.count_ref, ...), custom_call_target="tpu_custom_call" | custom-call | tf_op jit(solution)/shard_map/estimates/pallas_call | solution.py:384
  339.5 2.0 collective-permute-start.32
  341.5 3.2 collective-permute-done.32
  345.9 2.7 collective-permute-start.36
  348.6 2.7 collective-permute-done.34
  352.5 2.2 collective-permute-done.36
  356.5 3.4 collective-permute-start.37
  359.9 2.1 collective-permute-done.35.refs_2_
  362.0 2.7 collective-permute-done.33.refs_1_
  364.7 5.9 %collective-permute-done.37.refs_3_ = f32[2,256,256]{2,1,0:T(8,128)S(1)} collective-permute-done((f32[2,256,256]{2,1,0:T(8,128)S(1)}, f32[2,256,256]{2,1,0:T(8,128)S(1)}, u32[]{:S(2)}, u32[]{:S(2)}) %collective-permute-start.37) | collective-permute-done | bytes 524320 | tf_op jit(solution)/shard_map/ppermute | solution.py:483
  371.4 8.2 %update_frames.3 = (f32[2,256,256]{2,1,0:T(8,128)}, bf16[2,256,256]{2,1,0:T(8,128)(2,1)}, f32[256,256]{1,0:T(8,128)}) custom-call(f32[2,256,256]{2,1,0:T(8,128)} %get-tuple-element.38.frame_ref, f32[2,256,256]{2,1,0:T(8,128)} %get-tuple-element.40.refs_0_, f32[2,256,256]{2,1,0:T(8,128)} %copy-done.12, f32[2,256,256]{2,1,0:T(8,128)} %copy-done.10, ...), custom_call_target="tpu_custom_call" | custom-call | tf_op jit(solution)/shard_map/update_frames/pallas_call | solution.py:416
  379.6 15.3 %all_to_all.15 = f32[32,8,256]{2,1,0:T(8,128)S(1)} all-to-all(f32[32,8,256]{2,1,0:T(8,128)} %bitcast.10), channel_id=1, replica_groups=mesh['gx'=4,'gy_0'=4,'gy_1'=4,'gy_2'=2] {'gy_0','gy_1','gy_2'}, dimensions={0} | all-to-all | bytes 524288 | tf_op jit(solution)/shard_map/all_to_all | solution.py:524
  395.0 6.7 %all_to_all.16 = f32[4,8,256]{2,1,0:T(8,128)S(1)} all-to-all(f32[4,8,256]{2,1,0:T(8,128)S(1)} %broadcast_in_dim.4), channel_id=1, replica_groups=mesh['gx'=4,'gy_0'=4,'gy_1'=4,'gy_2'=2] {'gx'}, dimensions={0} | all-to-all | bytes 65536 | tf_op jit(solution)/shard_map/all_to_all | solution.py:518
  401.7 13.7 %all_to_all.17 = f32[32,8,256]{2,1,0:T(8,128)} all-to-all(f32[32,8,256]{2,1,0:T(8,128)S(1)} %broadcast_in_dim.5), channel_id=1, replica_groups=mesh['gx'=4,'gy_0'=4,'gy_1'=4,'gy_2'=2] {'gy_0','gy_1','gy_2'}, dimensions={0} | all-to-all | bytes 524288 | tf_op jit(solution)/shard_map/all_to_all | solution.py:518
  415.3 11.4 %aligned_rows.1 = (bf16[2,4096,256]{2,1,0:T(8,128)(2,1)}, f32[2,256,256]{2,1,0:T(8,128)}) custom-call(f32[256,256]{1,0:T(8,128)} %bitcast.8, f32[2,256,256]{2,1,0:T(8,128)} %get-tuple-element.48.frame_ref, bf16[2,4096,256]{2,1,0:T(8,128)(2,1)} %patch_ref.1), custom_call_target="tpu_custom_call" | custom-call | tf_op jit(solution)/shard_map/aligned_rows/pallas_call | solution.py:461
  (117 shorter events, 26.6 us)
Async XLA Ops:
  0.6 49.8 %collective-permute-start = (bf16[2,4096,256]{2,1,0:T(8,128)(2,1)}, bf16[2,4096,256]{2,1,0:T(8,128)(2,1)S(1)}, u32[]{:S(2)}, u32[]{:S(2)}) collective-permute-start(bf16[2,4096,256]{2,1,0:T(8,128)(2,1)} %patch_ref.1), channel_id=1, source_target_pairs={{0,8},{1,3},{2,10},{3,5},{4,12},{5,7},{6,14},{7,1},{8,16},{9,11},{... | collective-permute-start | bytes 12582920 | tf_op jit(solution)/shard_map/ppermute | solution.py:483
  2.7 49.5 %collective-permute-start.1 = (bf16[2,4096,256]{2,1,0:T(8,128)(2,1)}, bf16[2,4096,256]{2,1,0:T(8,128)(2,1)S(1)}, u32[]{:S(2)}, u32[]{:S(2)}) collective-permute-start(bf16[2,4096,256]{2,1,0:T(8,128)(2,1)} %patch_ref.1), channel_id=1, source_target_pairs={{0,6},{1,25},{2,0},{3,27},{4,2},{5,29},{6,4},{7,31},{8,14},{9,1},{... | collective-permute-start | bytes 12582920 | tf_op jit(solution)/shard_map/ppermute | solution.py:483
  50.4 71.4 %collective-permute-start.3 = (bf16[2,4096,256]{2,1,0:T(8,128)(2,1)S(1)}, bf16[2,4096,256]{2,1,0:T(8,128)(2,1)}, u32[]{:S(2)}, u32[]{:S(2)}) collective-permute-start(bf16[2,4096,256]{2,1,0:T(8,128)(2,1)S(1)} %collective-permute-done.refs_1_), channel_id=1, source_target_pairs={{0,8},{1,3},{2,10},{3,5},{4,12},{5,7},{6,14},{7,1},{8,16},{9,11},{... | collective-permute-start | bytes 12582920 | tf_op jit(solution)/shard_map/ppermute | solution.py:483
  52.3 69.6 %copy-start.1 = (bf16[2,4096,256]{2,1,0:T(8,128)(2,1)}, bf16[2,4096,256]{2,1,0:T(8,128)(2,1)S(1)}, u32[]{:S(2)}) copy-start(bf16[2,4096,256]{2,1,0:T(8,128)(2,1)S(1)} %collective-permute-done.1.refs_2_) | copy-start | bytes 12582916
  52.3 73.0 %collective-permute-start.4 = (bf16[2,4096,256]{2,1,0:T(8,128)(2,1)S(1)}, bf16[2,4096,256]{2,1,0:T(8,128)(2,1)S(1)}, u32[]{:S(2)}, u32[]{:S(2)}) collective-permute-start(bf16[2,4096,256]{2,1,0:T(8,128)(2,1)S(1)} %collective-permute-done.1.refs_2_), channel_id=1, source_target_pairs={{0,6},{1,25},{2,0},{3,27},{4,2},{5,29},{6,4},{7,31},{8,14},{9,1},{... | collective-permute-start | bytes 12582920 | tf_op jit(solution)/shard_map/ppermute | solution.py:483
  57.0 138.9 %copy-start.27 = (s32[256,2,4]{0,2,1:T(4,128)S(1)}, s32[256,2,4]{0,2,1:T(4,128)}, u32[]{:S(2)}) copy-start(s32[256,2,4]{0,2,1:T(4,128)} %param.8) | copy-start | bytes 24580
  57.0 140.0 %copy-start.28 = (s32[256,2]{0,1:T(2,128)S(1)}, s32[256,2]{0,1:T(2,128)}, u32[]{:S(2)}) copy-start(s32[256,2]{0,1:T(2,128)} %param.7) | copy-start | bytes 6148
  57.0 70.7 %collective-permute-start.6 = (bf16[4096,256]{1,0:T(8,128)(2,1)S(1)}, bf16[4096,256]{1,0:T(8,128)(2,1)S(1)}, u32[]{:S(2)}, u32[]{:S(2)}) collective-permute-start(bf16[4096,256]{1,0:T(8,128)(2,1)S(1)} %slice_bitcast_fusion.1), channel_id=1, source_target_pairs={{0,2},{1,9},{2,4},{3,11},{4,6},{5,13},{6,0},{7,15},{8,10},{9,17},{... | collective-permute-start | bytes 6291464 | tf_op jit(solution)/shard_map/ppermute | solution.py:483
  57.1 135.3 %collective-permute-start.2 = (bf16[2,4096,256]{2,1,0:T(8,128)(2,1)S(1)}, bf16[2,4096,256]{2,1,0:T(8,128)(2,1)}, u32[]{:S(2)}, u32[]{:S(2)}) collective-permute-start(bf16[2,4096,256]{2,1,0:T(8,128)(2,1)S(1)} %collective-permute-done.refs_1_), channel_id=1, source_target_pairs={{0,1},{1,0},{2,3},{3,2},{4,5},{5,4},{6,7},{7,6},{8,9},{9,8},{10,11... | collective-permute-start | bytes 12582920 | tf_op jit(solution)/shard_map/ppermute | solution.py:483
  121.8 73.9 %collective-permute-start.5 = (bf16[2,4096,256]{2,1,0:T(8,128)(2,1)}, bf16[2,4096,256]{2,1,0:T(8,128)(2,1)}, u32[]{:S(2)}, u32[]{:S(2)}) collective-permute-start(bf16[2,4096,256]{2,1,0:T(8,128)(2,1)} %collective-permute-done.3.refs_4_), channel_id=1, source_target_pairs={{0,1},{1,0},{2,3},{3,2},{4,5},{5,4},{6,7},{7,6},{8,9},{9,8},{10,11... | collective-permute-start | bytes 12582920 | tf_op jit(solution)/shard_map/ppermute | solution.py:483
  127.2 25.3 %collective-permute-start.7 = (bf16[4096,256]{1,0:T(8,128)(2,1)S(1)}, bf16[4096,256]{1,0:T(8,128)(2,1)}, u32[]{:S(2)}, u32[]{:S(2)}) collective-permute-start(bf16[4096,256]{1,0:T(8,128)(2,1)S(1)} %slice_bitcast_fusion), channel_id=1, source_target_pairs={{0,6},{1,25},{2,0},{3,27},{4,2},{5,29},{6,4},{7,31},{8,14},{9,1},{... | collective-permute-start | bytes 6291464 | tf_op jit(solution)/shard_map/ppermute | solution.py:483
  127.7 97.4 %copy-start.4 = (bf16[4096,256]{1,0:T(8,128)(2,1)}, bf16[4096,256]{1,0:T(8,128)(2,1)S(1)}, u32[]{:S(2)}) copy-start(bf16[4096,256]{1,0:T(8,128)(2,1)S(1)} %collective-permute-done.6.refs_7_) | copy-start | bytes 6291460
  127.7 64.7 %collective-permute-start.8 = (bf16[4096,256]{1,0:T(8,128)(2,1)S(1)}, bf16[4096,256]{1,0:T(8,128)(2,1)}, u32[]{:S(2)}, u32[]{:S(2)}) collective-permute-start(bf16[4096,256]{1,0:T(8,128)(2,1)S(1)} %collective-permute-done.6.refs_7_), channel_id=1, source_target_pairs={{0,1},{1,0},{2,3},{3,2},{4,5},{5,4},{6,7},{7,6},{8,9},{9,8},{10,11... | collective-permute-start | bytes 6291464 | tf_op jit(solution)/shard_map/ppermute | solution.py:483
  152.5 85.5 %collective-permute-start.9 = (bf16[4096,256]{1,0:T(8,128)(2,1)}, bf16[4096,256]{1,0:T(8,128)(2,1)}, u32[]{:S(2)}, u32[]{:S(2)}) collective-permute-start(bf16[4096,256]{1,0:T(8,128)(2,1)} %collective-permute-done.7.refs_8_), channel_id=1, source_target_pairs={{0,1},{1,0},{2,3},{3,2},{4,5},{5,4},{6,7},{7,6},{8,9},{9,8},{10,11... | collective-permute-start | bytes 6291464 | tf_op jit(solution)/shard_map/ppermute | solution.py:483
  160.9 7.5 %collective-permute-start.10 = (bf16[2,256,256]{2,1,0:T(8,128)(2,1)}, bf16[2,256,256]{2,1,0:T(8,128)(2,1)S(1)}, u32[]{:S(2)}, u32[]{:S(2)}) collective-permute-start(bf16[2,256,256]{2,1,0:T(8,128)(2,1)} %get-tuple-element.30.refs_0_), channel_id=1, source_target_pairs={{0,8},{1,3},{2,10},{3,5},{4,12},{5,7},{6,14},{7,1},{8,16},{9,11},{... | collective-permute-start | bytes 786440 | tf_op jit(solution)/shard_map/ppermute | solution.py:483
  168.4 56.7 %copy-start.15 = (bf16[2,256,256]{2,1,0:T(8,128)(2,1)}, bf16[2,256,256]{2,1,0:T(8,128)(2,1)S(1)}, u32[]{:S(2)}) copy-start(bf16[2,256,256]{2,1,0:T(8,128)(2,1)S(1)} %collective-permute-done.10.refs_1_) | copy-start | bytes 786436
  168.4 5.7 %collective-permute-start.13 = (bf16[2,256,256]{2,1,0:T(8,128)(2,1)}, bf16[2,256,256]{2,1,0:T(8,128)(2,1)S(1)}, u32[]{:S(2)}, u32[]{:S(2)}) collective-permute-start(bf16[2,256,256]{2,1,0:T(8,128)(2,1)} %get-tuple-element.30.refs_0_), channel_id=1, source_target_pairs={{0,6},{1,25},{2,0},{3,27},{4,2},{5,29},{6,4},{7,31},{8,14},{9,1},{... | collective-permute-start | bytes 786440 | tf_op jit(solution)/shard_map/ppermute | solution.py:483
  174.1 51.0 %copy-start.16 = (bf16[2,256,256]{2,1,0:T(8,128)(2,1)}, bf16[2,256,256]{2,1,0:T(8,128)(2,1)S(1)}, u32[]{:S(2)}) copy-start(bf16[2,256,256]{2,1,0:T(8,128)(2,1)S(1)} %collective-permute-done.13.refs_4_) | copy-start | bytes 786436
  174.1 6.6 %collective-permute-start.12 = (bf16[2,256,256]{2,1,0:T(8,128)(2,1)}, bf16[2,256,256]{2,1,0:T(8,128)(2,1)S(1)}, u32[]{:S(2)}, u32[]{:S(2)}) collective-permute-start(bf16[2,256,256]{2,1,0:T(8,128)(2,1)} %get-tuple-element.30.refs_0_), channel_id=1, source_target_pairs={{0,2},{1,9},{2,4},{3,11},{4,6},{5,13},{6,0},{7,15},{8,10},{9,17},{... | collective-permute-start | bytes 786440 | tf_op jit(solution)/shard_map/ppermute | solution.py:483
  180.8 44.4 %copy-start.17 = (bf16[2,256,256]{2,1,0:T(8,128)(2,1)}, bf16[2,256,256]{2,1,0:T(8,128)(2,1)S(1)}, u32[]{:S(2)}) copy-start(bf16[2,256,256]{2,1,0:T(8,128)(2,1)S(1)} %collective-permute-done.12.refs_3_) | copy-start | bytes 786436
  180.8 6.4 %collective-permute-start.11 = (bf16[2,256,256]{2,1,0:T(8,128)(2,1)S(1)}, bf16[2,256,256]{2,1,0:T(8,128)(2,1)S(1)}, u32[]{:S(2)}, u32[]{:S(2)}) collective-permute-start(bf16[2,256,256]{2,1,0:T(8,128)(2,1)S(1)} %collective-permute-done.10.refs_1_), channel_id=1, source_target_pairs={{0,8},{1,3},{2,10},{3,5},{4,12},{5,7},{6,14},{7,1},{8,16},{9,11},{... | collective-permute-start | bytes 786440 | tf_op jit(solution)/shard_map/ppermute | solution.py:483
  187.2 38.0 %copy-start.18 = (bf16[2,256,256]{2,1,0:T(8,128)(2,1)}, bf16[2,256,256]{2,1,0:T(8,128)(2,1)S(1)}, u32[]{:S(2)}) copy-start(bf16[2,256,256]{2,1,0:T(8,128)(2,1)S(1)} %collective-permute-done.11.refs_2_) | copy-start | bytes 786436
  187.2 61.7 %collective-permute-start.15 = (bf16[2,256,256]{2,1,0:T(8,128)(2,1)S(1)}, bf16[2,256,256]{2,1,0:T(8,128)(2,1)}, u32[]{:S(2)}, u32[]{:S(2)}) collective-permute-start(bf16[2,256,256]{2,1,0:T(8,128)(2,1)S(1)} %collective-permute-done.10.refs_1_), channel_id=1, source_target_pairs={{0,1},{1,0},{2,3},{3,2},{4,5},{5,4},{6,7},{7,6},{8,9},{9,8},{10,11... | collective-permute-start | bytes 786440 | tf_op jit(solution)/shard_map/ppermute | solution.py:483
  192.4 56.5 %collective-permute-start.14 = (bf16[2,256,256]{2,1,0:T(8,128)(2,1)S(1)}, bf16[2,256,256]{2,1,0:T(8,128)(2,1)}, u32[]{:S(2)}, u32[]{:S(2)}) collective-permute-start(bf16[2,256,256]{2,1,0:T(8,128)(2,1)S(1)} %collective-permute-done.13.refs_4_), channel_id=1, source_target_pairs={{0,6},{1,25},{2,0},{3,27},{4,2},{5,29},{6,4},{7,31},{8,14},{9,1},{... | collective-permute-start | bytes 786440 | tf_op jit(solution)/shard_map/ppermute | solution.py:483
  192.4 56.5 %collective-permute-start.17 = (bf16[2,256,256]{2,1,0:T(8,128)(2,1)S(1)}, bf16[2,256,256]{2,1,0:T(8,128)(2,1)}, u32[]{:S(2)}, u32[]{:S(2)}) collective-permute-start(bf16[2,256,256]{2,1,0:T(8,128)(2,1)S(1)} %collective-permute-done.12.refs_3_), channel_id=1, source_target_pairs={{0,1},{1,0},{2,3},{3,2},{4,5},{5,4},{6,7},{7,6},{8,9},{9,8},{10,11... | collective-permute-start | bytes 786440 | tf_op jit(solution)/shard_map/ppermute | solution.py:483
  195.8 53.1 %collective-permute-start.16 = (bf16[2,256,256]{2,1,0:T(8,128)(2,1)S(1)}, bf16[2,256,256]{2,1,0:T(8,128)(2,1)}, u32[]{:S(2)}, u32[]{:S(2)}) collective-permute-start(bf16[2,256,256]{2,1,0:T(8,128)(2,1)S(1)} %collective-permute-done.11.refs_2_), channel_id=1, source_target_pairs={{0,1},{1,0},{2,3},{3,2},{4,5},{5,4},{6,7},{7,6},{8,9},{9,8},{10,11... | collective-permute-start | bytes 786440 | tf_op jit(solution)/shard_map/ppermute | solution.py:483
  257.0 31.5 %copy-start.7 = (f32[2,256,256]{2,1,0:T(8,128)S(1)}, f32[2,256,256]{2,1,0:T(8,128)}, u32[]{:S(2)}) copy-start(f32[2,256,256]{2,1,0:T(8,128)} %get-tuple-element.36) | copy-start | bytes 1572868
  257.0 31.5 %copy-start.8 = (f32[2,256,256]{2,1,0:T(8,128)S(1)}, f32[2,256,256]{2,1,0:T(8,128)}, u32[]{:S(2)}) copy-start(f32[2,256,256]{2,1,0:T(8,128)} %get-tuple-element.32) | copy-start | bytes 1572868
  257.0 22.0 %collective-permute-start.18 = (f32[6,256,256]{2,1,0:T(8,128)}, f32[6,256,256]{2,1,0:T(8,128)S(1)}, u32[]{:S(2)}, u32[]{:S(2)}) collective-permute-start(f32[6,256,256]{2,1,0:T(8,128)} %get-tuple-element.33), channel_id=1, source_target_pairs={{0,1},{1,0},{2,3},{3,2},{4,5},{5,4},{6,7},{7,6},{8,9},{9,8},{10,11... | collective-permute-start | bytes 4718600 | tf_op jit(solution)/shard_map/ppermute | solution.py:483
  275.8 9.7 %collective-permute-start.20 = (f32[2,256,256]{2,1,0:T(8,128)}, f32[2,256,256]{2,1,0:T(8,128)S(1)}, u32[]{:S(2)}, u32[]{:S(2)}) collective-permute-start(f32[2,256,256]{2,1,0:T(8,128)} %get-tuple-element.35), channel_id=1, source_target_pairs={{6,0},{25,1},{0,2},{27,3},{2,4},{29,5},{4,6},{31,7},{14,8},{1,9},{... | collective-permute-start | bytes 1572872 | tf_op jit(solution)/shard_map/ppermute | solution.py:483
  280.1 8.4 %collective-permute-start.22 = (f32[2,256,256]{2,1,0:T(8,128)S(1)}, f32[2,256,256]{2,1,0:T(8,128)S(1)}, u32[]{:S(2)}, u32[]{:S(2)}) collective-permute-start(f32[2,256,256]{2,1,0:T(8,128)S(1)} %slice_add_fusion.3), channel_id=1, source_target_pairs={{8,0},{3,1},{10,2},{5,3},{12,4},{7,5},{14,6},{1,7},{16,8},{11,9},{... | collective-permute-start | bytes 1572872 | tf_op jit(solution)/shard_map/ppermute | solution.py:483
  286.6 9.6 %collective-permute-start.21 = (f32[2,256,256]{2,1,0:T(8,128)S(1)}, f32[2,256,256]{2,1,0:T(8,128)S(1)}, u32[]{:S(2)}, u32[]{:S(2)}) collective-permute-start(f32[2,256,256]{2,1,0:T(8,128)S(1)} %add.39), channel_id=1, source_target_pairs={{6,0},{25,1},{0,2},{27,3},{2,4},{29,5},{4,6},{31,7},{14,8},{1,9},{... | collective-permute-start | bytes 1572872 | tf_op jit(solution)/shard_map/ppermute | solution.py:483
  288.7 11.2 %collective-permute-start.19 = (f32[2,256,256]{2,1,0:T(8,128)S(1)}, f32[2,256,256]{2,1,0:T(8,128)S(1)}, u32[]{:S(2)}, u32[]{:S(2)}) collective-permute-start(f32[2,256,256]{2,1,0:T(8,128)S(1)} %get-tuple-element.54), channel_id=1, source_target_pairs={{2,0},{9,1},{4,2},{11,3},{6,4},{13,5},{0,6},{15,7},{10,8},{17,9},{... | collective-permute-start | bytes 1572872 | tf_op jit(solution)/shard_map/ppermute | solution.py:483
  289.6 13.1 %collective-permute-start.23 = (f32[2,256,256]{2,1,0:T(8,128)S(1)}, f32[2,256,256]{2,1,0:T(8,128)S(1)}, u32[]{:S(2)}, u32[]{:S(2)}) collective-permute-start(f32[2,256,256]{2,1,0:T(8,128)S(1)} %get-tuple-element.53), channel_id=1, source_target_pairs={{8,0},{3,1},{10,2},{5,3},{12,4},{7,5},{14,6},{1,7},{16,8},{11,9},{... | collective-permute-start | bytes 1572872 | tf_op jit(solution)/shard_map/ppermute | solution.py:483
  311.7 6.9 %collective-permute-start.24 = (bf16[2,256,256]{2,1,0:T(8,128)(2,1)}, bf16[2,256,256]{2,1,0:T(8,128)(2,1)S(1)}, u32[]{:S(2)}, u32[]{:S(2)}) collective-permute-start(bf16[2,256,256]{2,1,0:T(8,128)(2,1)} %get-tuple-element.39.refs_0_), channel_id=1, source_target_pairs={{0,8},{1,3},{2,10},{3,5},{4,12},{5,7},{6,14},{7,1},{8,16},{9,11},{... | collective-permute-start | bytes 786440 | tf_op jit(solution)/shard_map/ppermute | solution.py:483
  311.7 10.7 %collective-permute-start.27 = (bf16[2,256,256]{2,1,0:T(8,128)(2,1)}, bf16[2,256,256]{2,1,0:T(8,128)(2,1)S(1)}, u32[]{:S(2)}, u32[]{:S(2)}) collective-permute-start(bf16[2,256,256]{2,1,0:T(8,128)(2,1)} %get-tuple-element.39.refs_0_), channel_id=1, source_target_pairs={{0,6},{1,25},{2,0},{3,27},{4,2},{5,29},{6,4},{7,31},{8,14},{9,1},{... | collective-permute-start | bytes 786440 | tf_op jit(solution)/shard_map/ppermute | solution.py:483
  311.8 13.2 %collective-permute-start.26 = (bf16[2,256,256]{2,1,0:T(8,128)(2,1)}, bf16[2,256,256]{2,1,0:T(8,128)(2,1)S(1)}, u32[]{:S(2)}, u32[]{:S(2)}) collective-permute-start(bf16[2,256,256]{2,1,0:T(8,128)(2,1)} %get-tuple-element.39.refs_0_), channel_id=1, source_target_pairs={{0,2},{1,9},{2,4},{3,11},{4,6},{5,13},{6,0},{7,15},{8,10},{9,17},{... | collective-permute-start | bytes 786440 | tf_op jit(solution)/shard_map/ppermute | solution.py:483
  318.7 6.7 %collective-permute-start.25 = (bf16[2,256,256]{2,1,0:T(8,128)(2,1)S(1)}, bf16[2,256,256]{2,1,0:T(8,128)(2,1)S(1)}, u32[]{:S(2)}, u32[]{:S(2)}) collective-permute-start(bf16[2,256,256]{2,1,0:T(8,128)(2,1)S(1)} %collective-permute-done.24.refs_1_), channel_id=1, source_target_pairs={{0,8},{1,3},{2,10},{3,5},{4,12},{5,7},{6,14},{7,1},{8,16},{9,11},{... | collective-permute-start | bytes 786440 | tf_op jit(solution)/shard_map/ppermute | solution.py:483
  318.7 10.9 %collective-permute-start.29 = (bf16[2,256,256]{2,1,0:T(8,128)(2,1)S(1)}, bf16[2,256,256]{2,1,0:T(8,128)(2,1)S(1)}, u32[]{:S(2)}, u32[]{:S(2)}) collective-permute-start(bf16[2,256,256]{2,1,0:T(8,128)(2,1)S(1)} %collective-permute-done.24.refs_1_), channel_id=1, source_target_pairs={{0,1},{1,0},{2,3},{3,2},{4,5},{5,4},{6,7},{7,6},{8,9},{9,8},{10,11... | collective-permute-start | bytes 786440 | tf_op jit(solution)/shard_map/ppermute | solution.py:483
  322.4 7.1 %collective-permute-start.28 = (bf16[2,256,256]{2,1,0:T(8,128)(2,1)S(1)}, bf16[2,256,256]{2,1,0:T(8,128)(2,1)S(1)}, u32[]{:S(2)}, u32[]{:S(2)}) collective-permute-start(bf16[2,256,256]{2,1,0:T(8,128)(2,1)S(1)} %collective-permute-done.27.refs_4_), channel_id=1, source_target_pairs={{0,6},{1,25},{2,0},{3,27},{4,2},{5,29},{6,4},{7,31},{8,14},{9,1},{... | collective-permute-start | bytes 786440 | tf_op jit(solution)/shard_map/ppermute | solution.py:483
  324.9 4.6 %collective-permute-start.31 = (bf16[2,256,256]{2,1,0:T(8,128)(2,1)S(1)}, bf16[2,256,256]{2,1,0:T(8,128)(2,1)S(1)}, u32[]{:S(2)}, u32[]{:S(2)}) collective-permute-start(bf16[2,256,256]{2,1,0:T(8,128)(2,1)S(1)} %collective-permute-done.26.refs_3_), channel_id=1, source_target_pairs={{0,1},{1,0},{2,3},{3,2},{4,5},{5,4},{6,7},{7,6},{8,9},{9,8},{10,11... | collective-permute-start | bytes 786440 | tf_op jit(solution)/shard_map/ppermute | solution.py:483
  325.4 5.3 %collective-permute-start.30 = (bf16[2,256,256]{2,1,0:T(8,128)(2,1)S(1)}, bf16[2,256,256]{2,1,0:T(8,128)(2,1)S(1)}, u32[]{:S(2)}, u32[]{:S(2)}) collective-permute-start(bf16[2,256,256]{2,1,0:T(8,128)(2,1)S(1)} %collective-permute-done.25.refs_2_), channel_id=1, source_target_pairs={{0,1},{1,0},{2,3},{3,2},{4,5},{5,4},{6,7},{7,6},{8,9},{9,8},{10,11... | collective-permute-start | bytes 786440 | tf_op jit(solution)/shard_map/ppermute | solution.py:483
  339.5 5.3 %collective-permute-start.32 = (f32[6,256,256]{2,1,0:T(8,128)}, f32[6,256,256]{2,1,0:T(8,128)S(1)}, u32[]{:S(2)}, u32[]{:S(2)}) collective-permute-start(f32[6,256,256]{2,1,0:T(8,128)} %get-tuple-element.42), channel_id=1, source_target_pairs={{0,1},{1,0},{2,3},{3,2},{4,5},{5,4},{6,7},{7,6},{8,9},{9,8},{10,11... | collective-permute-start | bytes 4718600 | tf_op jit(solution)/shard_map/ppermute | solution.py:483
  341.5 9.7 %collective-permute-start.34 = (f32[2,256,256]{2,1,0:T(8,128)}, f32[2,256,256]{2,1,0:T(8,128)S(1)}, u32[]{:S(2)}, u32[]{:S(2)}) collective-permute-start(f32[2,256,256]{2,1,0:T(8,128)} %get-tuple-element.44), channel_id=1, source_target_pairs={{6,0},{25,1},{0,2},{27,3},{2,4},{29,5},{4,6},{31,7},{14,8},{1,9},{... | collective-permute-start | bytes 1572872 | tf_op jit(solution)/shard_map/ppermute | solution.py:483
  345.9 8.8 %collective-permute-start.36 = (f32[2,256,256]{2,1,0:T(8,128)S(1)}, f32[2,256,256]{2,1,0:T(8,128)S(1)}, u32[]{:S(2)}, u32[]{:S(2)}) collective-permute-start(f32[2,256,256]{2,1,0:T(8,128)S(1)} %slice_add_fusion), channel_id=1, source_target_pairs={{8,0},{3,1},{10,2},{5,3},{12,4},{7,5},{14,6},{1,7},{16,8},{11,9},{... | collective-permute-start | bytes 1572872 | tf_op jit(solution)/shard_map/ppermute | solution.py:483
  352.4 9.6 %collective-permute-start.35 = (f32[2,256,256]{2,1,0:T(8,128)S(1)}, f32[2,256,256]{2,1,0:T(8,128)S(1)}, u32[]{:S(2)}, u32[]{:S(2)}) collective-permute-start(f32[2,256,256]{2,1,0:T(8,128)S(1)} %add.44), channel_id=1, source_target_pairs={{6,0},{25,1},{0,2},{27,3},{2,4},{29,5},{4,6},{31,7},{14,8},{1,9},{... | collective-permute-start | bytes 1572872 | tf_op jit(solution)/shard_map/ppermute | solution.py:483
  354.9 9.8 %collective-permute-start.33 = (f32[2,256,256]{2,1,0:T(8,128)S(1)}, f32[2,256,256]{2,1,0:T(8,128)S(1)}, u32[]{:S(2)}, u32[]{:S(2)}) collective-permute-start(f32[2,256,256]{2,1,0:T(8,128)S(1)} %get-tuple-element.52), channel_id=1, source_target_pairs={{2,0},{9,1},{4,2},{11,3},{6,4},{13,5},{0,6},{15,7},{10,8},{17,9},{... | collective-permute-start | bytes 1572872 | tf_op jit(solution)/shard_map/ppermute | solution.py:483
  356.5 14.1 %collective-permute-start.37 = (f32[2,256,256]{2,1,0:T(8,128)S(1)}, f32[2,256,256]{2,1,0:T(8,128)S(1)}, u32[]{:S(2)}, u32[]{:S(2)}) collective-permute-start(f32[2,256,256]{2,1,0:T(8,128)S(1)} %get-tuple-element.51), channel_id=1, source_target_pairs={{8,0},{3,1},{10,2},{5,3},{12,4},{7,5},{14,6},{1,7},{16,8},{11,9},{... | collective-permute-start | bytes 1572872 | tf_op jit(solution)/shard_map/ppermute | solution.py:483
  (19 other events, 111.6 us)

commit v2 on v1

--- a/solution.py
+++ b/solution.py
@@ -105,8 +105,8 @@
 INFO = 2 + 2 * OVB
 
 
-def params():
-    return pltpu.CompilerParams(vmem_limit_bytes=56 * 1024 * 1024)
+def params(mib=56):
+    return pltpu.CompilerParams(vmem_limit_bytes=mib * 1024 * 1024)
 
 
 def halves(a):
@@ -283,7 +283,7 @@
             pltpu.SemaphoreType.DMA((2,)),
             pltpu.SemaphoreType.DMA,
         ],
-        compiler_params=params(),
+        compiler_params=params(60),
     )(info, count, *arrays, *more)
 
 
@@ -431,13 +431,21 @@
 
 
 def final_kernel(total_ref, frame_ref, patch_ref, aligned_ref, final_ref, gauge, rows, outs, low, in_sem, out_sem):
-    chunks = [(p, pl.ds(r, CHUNK)) for p in range(PER) for r in range(0, patch_ref.shape[1], CHUNK)]
-    ins = [
-        pltpu.make_async_copy(patch_ref.at[p, r], rows.at[p, r], in_sem.at[n])
-        for n, (p, r) in enumerate(chunks)
-    ]
-    for copy in ins:
-        copy.start()
+    pieces = patch_ref.shape[1] // CHUNK
+
+    def piece(n):
+        return n // pieces, pl.ds(pl.multiple_of(n % pieces * CHUNK, CHUNK), CHUNK)
+
+    def copy_in(n):
+        p, r = piece(n)
+        return pltpu.make_async_copy(patch_ref.at[p, r], rows.at[p, r], in_sem.at[n])
+
+    def copy_out(n):
+        p, r = piece(n)
+        return pltpu.make_async_copy(outs.at[p, r], aligned_ref.at[p, r], out_sem.at[n])
+
+    for n in range(PER * pieces):
+        copy_in(n).start()
     gauge[0] = total_ref[...]
     newton_schulz(gauge, 1)
     g = halves(gauge[0])
@@ -445,15 +453,17 @@
         final = dot3(halves(frame_ref[p]), g, 1)
         final_ref[p] = final
         low[p] = final.astype(BF16)
-    done = []
-    for n, (p, r) in enumerate(chunks):
-        ins[n].wait()
+
+    def step(n, carry):
+        p, r = piece(n)
+        copy_in(n).wait()
         outs[p, r] = dot(rows[p, r], low[p]).astype(BF16)
-        copy = pltpu.make_async_copy(outs.at[p, r], aligned_ref.at[p, r], out_sem.at[n])
-        copy.start()
-        done.append(copy)
-    for copy in done:
-        copy.wait()
+        copy_out(n).start()
+        return carry
+
+    lax.fori_loop(0, PER * pieces, step, 0)
+    for n in range(PER * pieces):
+        copy_out(n).wait()
 
 
 def make_final(total, frames, patches):
@@ -483,9 +493,8 @@
     return lax.ppermute(value, GY, perm)
 
 
-LAYOUT = (
-    ((0, 0), (0, 1), (1, 0), (1, 1), (4, 0), (4, 1), (7, None), (8, None), (2, 0), (2, 1), (5, 0), (5, 1))
-    + ((3, 0), (3, 1), (6, 0), (6, 1), (9, None), (10, None))
+LAYOUT = ((0, 0), (0, 1)) + tuple(
+    (n + p, None) for n in (1, 7, 13, 3, 9, 5, 11, 15) for p in range(PER)
 )
 
 
@@ -505,32 +514,45 @@
     five = send(five, back_perm(LEFT))
     one, two, three = (v + cross[PER * n : PER * (n + 1)] for n, v in enumerate((one, two, three)))
     two = send(two, back_perm(UP))
-    return [
-        own,
-        send(three, back_perm(RIGHT)),
-        send(four + five, back_perm(LEFT)),
-        send(one + two, back_perm(UP)),
-    ]
-
-
-def from_everyone(value, axis):
+    three = send(three, back_perm(RIGHT))
+    return [own, three, send(four + five, back_perm(LEFT)), send(one + two, back_perm(UP))]
+
+
+def axis_sum(value, axis):
     size = lax.axis_size(axis)
-    return lax.all_to_all(jnp.broadcast_to(value[None], (size, *value.shape)), axis, 0, 0, tiled=True)
+
+    def from_behind(hops):
+        return lax.ppermute(value, axis, [(i, (i + hops) % size) for i in range(size)])
+
+    near = from_behind(1), from_behind(-1)
+    return (value + near[0]) + (near[1] + from_behind(2))
 
 
 def sum_over_all(value):
-    size = lax.axis_size(GY)
-    rows = value.shape[0] // size
-    mine = lax.all_to_all(value.reshape(size, rows, D), GY, 0, 0, tiled=True).sum(0)
-    mine = from_everyone(mine, "gx").sum(0)
-    return from_everyone(mine, GY).reshape(value.shape)
+    core = lax.axis_index("gy_2")
+    swap = [(0, 1), (1, 0)]
+    half = value.shape[0] // 2
+    low, high = value[:half], value[half:]
+    mine = jnp.where(core == 0, low, high) + lax.ppermute(jnp.where(core == 0, high, low), "gy_2", swap)
+    for axis in ("gx", "gy_0", "gy_1"):
+        mine = axis_sum(mine, axis)
+    other = lax.ppermute(mine, "gy_2", swap)
+    return jnp.concatenate([jnp.where(core == 0, mine, other), jnp.where(core == 0, other, mine)])
 
 
 def local(patches, start_frames, pair_ends, margin_blocks):
     me = lax.axis_index(GY).astype(jnp.int32)
     base = lax.axis_index("gx").astype(jnp.int32) * (DEVS * PER)
-    one = send(patches, step_perm(UP))
-    four = send(patches, step_perm(LEFT))
+
+    def hop(values, steps):
+        out = [None] * PER
+        for p in reversed(range(PER)):
+            out[p] = send(values[p], step_perm(steps) if steps else SIBLING)
+        return out
+
+    both = [patches[p] for p in range(PER)]
+    four = hop(both, LEFT)
+    one = hop(both, UP)
     info, count = make_index(
         jnp.stack([me, base]),
         jnp.asarray(meeting_table()),
@@ -539,17 +561,16 @@
     )
     frames, low = make_start(start_frames)
     lows = spread_frames(low)
-    two = send(one, step_perm(UP))
-    five = send(four, step_perm(LEFT))
-    cross_1 = send(one, SIBLING)
-    arrays = [patches, one, four, cross_1]
+    five = hop(four, LEFT)
+    two = hop(one, UP)
+    arrays = [patches, *one, *four, *hop(one, None)]
     rot = make_rotations(info, count, arrays, LAYOUT, 0, BATCH)
-    three_0 = send(patches[0], step_perm(RIGHT))
+    three_0 = send(both[0], step_perm(RIGHT))
     three_1 = send(five[1], step_perm(LEFT))
-    cross_2 = send(two, SIBLING)
-    arrays += [two, five, cross_2]
+    three = [three_0, three_1]
+    arrays += [*two, *five, *hop(two, None)]
     rot = make_rotations(info, count, arrays, LAYOUT, 1, BATCH, rot)
-    arrays += [three_0, three_1, send(three_0, SIBLING), send(three_1, SIBLING)]
+    arrays += [*three, *hop(three, None)]
     rot = make_rotations(info, count, arrays, LAYOUT, 2, 3, rot)
     for sweep in range(SWEEPS):
         if sweep:

time: 429 us -> 388 us (0.904)
  blocking collectives: 35.7 us -> 0 us
  waiting for transfers between devices: 204 us -> 174 us
  starting transfers between devices: 71.2 us -> 94.9 us
    ppermute x38 -> x44, waiting for transfers between devices: 204 us -> 155 us  [send(): return lax.ppermute(value, GY, perm)]
    all_to_all x3 -> x0, blocking collectives: 35.7 us -> none  [the longest x2 20.3 us: from_everyone(): lax.all_to_all(jnp.broadcast_to(value[None], (size, *value.shape)), axis,...]
    ppermute x0 -> x11, waiting for transfers between devices: none -> 18.2 us  [the longest x9 15.9 us: from_behind(): lax.ppermute(value, axis, [(i, (i + hops) % size) for i in range(size)])]
    ppermute x0 -> x11, starting transfers between devices: none -> 14.2 us  [the longest x9 10 us: from_behind(): lax.ppermute(value, axis, [(i, (i + hops) % size) for i in range(size)])]
    ppermute x38 -> x44, starting transfers between devices: 71.2 us -> 80.7 us  [send(): return lax.ppermute(value, GY, perm)]
  transfers between devices with their start and end apart: 38 -> 55, of which waited for: 23 -> 32; matrix products, arithmetic and copies ran while one was open for 2% -> 2% of each run, Pallas kernels for 14% -> 15%
where the time goes in v2:
time: 388 us; the launch traced here: 386 us
  waiting for transfers between devices  174 us (45%)
  Pallas kernels  100 us (26%)
  starting transfers between devices  94.9 us (24%)
  other arithmetic  8.26 us (2%)
  local copies, waits for them, and re-layouts  7.86 us (2%)
    ppermute x44, waiting for transfers between devices, send(): return lax.ppermute(value, GY, perm)  155 us
    ppermute x44, starting transfers between devices, send(): return lax.ppermute(value, GY, perm)  80.7 us
    pallas_call x3, Pallas kernels, make_rotations(): pl.pallas_call(functools.partial(rotation_kernel, layout, ready, size), i...  35.8 us
    pallas_call x2, Pallas kernels, make_update(): pl.pallas_call(update_kernel, in_specs=[VM] * (1 + len(parts)), out_specs...  16.3 us
    pallas_call x2, Pallas kernels, make_estimates(): pl.pallas_call(estimate_kernel, in_specs=[SM, SM, HBM] + [HBM] * SLOTS, o...  16.1 us
    ppermute x9, waiting for transfers between devices, from_behind(): lax.ppermute(value, axis, [(i, (i + hops) % size) for i in range(size)])  15.9 us
    pallas_call x1, Pallas kernels, make_index(): pl.pallas_call(index_kernel, in_specs=[SM] * 4, out_specs=[SM] * 2, out_s...  14.4 us
    pallas_call x1, Pallas kernels, make_final(): pl.pallas_call(final_kernel, in_specs=[VM, VM, HBM], out_specs=[HBM, VM],...  10.4 us
  transfers between devices with their start and end apart: 55, of which 32 were waited for; matrix products, arithmetic and copies ran while one was open for 2% of the time, Pallas kernels for 15%

profile of v2, /device:TPU:1, one launch (start us, length us, event | category | flops | bytes accessed | tf_op | source)
XLA Modules:
  0.0 386.4 jit_solution(2750905423394790491)
XLA Ops:
  0.7 2.5 slice_bitcast_fusion
  3.2 4.6 %collective-permute-start.3 = (bf16[4096,256]{1,0:T(8,128)(2,1)S(1)}, bf16[4096,256]{1,0:T(8,128)(2,1)S(1)}, u32[]{:S(2)}, u32[]{:S(2)}) collective-permute-start(bf16[4096,256]{1,0:T(8,128)(2,1)S(1)} %get-tuple-element.51), channel_id=1, source_target_pairs={{0,6},{1,25},{2,0},{3,27},{4,2},{5,29},{6,4},{7,31},{8,14},{9,1},{... | collective-permute-start | bytes 6291464 | tf_op jit(solution)/shard_map/ppermute | solution.py:493
  7.8 7.4 %start_frames.1 = (f32[2,256,256]{2,1,0:T(8,128)}, bf16[2,256,256]{2,1,0:T(8,128)(2,1)}) custom-call(f32[2,256,256]{2,1,0:T(8,128)} %start_ref.1), custom_call_target="tpu_custom_call" | custom-call | tf_op jit(solution)/shard_map/start_frames/pallas_call | solution.py:298
  17.9 4.3 %collective-permute-done.16.refs_1_ = bf16[2,256,256]{2,1,0:T(8,128)(2,1)S(1)} collective-permute-done((bf16[2,256,256]{2,1,0:T(8,128)(2,1)}, bf16[2,256,256]{2,1,0:T(8,128)(2,1)S(1)}, u32[]{:S(2)}, u32[]{:S(2)}) %collective-permute-start.16) | collective-permute-done | bytes 262176 | tf_op jit(solution)/shard_map/ppermute | solution.py:493
  25.0 8.7 %collective-permute-done.19.refs_4_ = bf16[2,256,256]{2,1,0:T(8,128)(2,1)S(1)} collective-permute-done((bf16[2,256,256]{2,1,0:T(8,128)(2,1)}, bf16[2,256,256]{2,1,0:T(8,128)(2,1)S(1)}, u32[]{:S(2)}, u32[]{:S(2)}) %collective-permute-start.19) | collective-permute-done | bytes 262176 | tf_op jit(solution)/shard_map/ppermute | solution.py:493
  34.9 3.0 collective-permute-start.2
  38.0 2.7 collective-permute-start.9
  40.6 19.6 %collective-permute-done.refs_1_ = bf16[4096,256]{1,0:T(8,128)(2,1)S(1)} collective-permute-done((bf16[4096,256]{1,0:T(8,128)(2,1)S(1)}, bf16[4096,256]{1,0:T(8,128)(2,1)S(1)}, u32[]{:S(2)}, u32[]{:S(2)}) %collective-permute-start) | collective-permute-done | bytes 2097184 | tf_op jit(solution)/shard_map/ppermute | solution.py:493
  60.2 9.5 %collective-permute-start.4 = (bf16[4096,256]{1,0:T(8,128)(2,1)S(1)}, bf16[4096,256]{1,0:T(8,128)(2,1)S(1)}, u32[]{:S(2)}, u32[]{:S(2)}) collective-permute-start(bf16[4096,256]{1,0:T(8,128)(2,1)S(1)} %collective-permute-done.refs_1_), channel_id=1, source_target_pairs={{0,1},{1,0},{2,3},{3,2},{4,5},{5,4},{6,7},{7,6},{8,9},{9,8},{10,11... | collective-permute-start | bytes 6291464 | tf_op jit(solution)/shard_map/ppermute | solution.py:493
  69.7 27.3 %collective-permute-done.1.refs_2_ = bf16[4096,256]{1,0:T(8,128)(2,1)S(1)} collective-permute-done((bf16[4096,256]{1,0:T(8,128)(2,1)S(1)}, bf16[4096,256]{1,0:T(8,128)(2,1)S(1)}, u32[]{:S(2)}, u32[]{:S(2)}) %collective-permute-start.1) | collective-permute-done | bytes 2097184 | tf_op jit(solution)/shard_map/ppermute | solution.py:493
  97.0 3.9 %collective-permute-start.5 = (bf16[4096,256]{1,0:T(8,128)(2,1)S(1)}, bf16[4096,256]{1,0:T(8,128)(2,1)S(1)}, u32[]{:S(2)}, u32[]{:S(2)}) collective-permute-start(bf16[4096,256]{1,0:T(8,128)(2,1)S(1)} %collective-permute-done.1.refs_2_), channel_id=1, source_target_pairs={{0,1},{1,0},{2,3},{3,2},{4,5},{5,4},{6,7},{7,6},{8,9},{9,8},{10,11... | collective-permute-start | bytes 6291464 | tf_op jit(solution)/shard_map/ppermute | solution.py:493
  101.6 3.1 collective-permute-done.5.refs_6_
  105.1 22.2 %collective-permute-done.6.refs_7_ = bf16[4096,256]{1,0:T(8,128)(2,1)S(1)} collective-permute-done((bf16[4096,256]{1,0:T(8,128)(2,1)S(1)}, bf16[4096,256]{1,0:T(8,128)(2,1)S(1)}, u32[]{:S(2)}, u32[]{:S(2)}) %collective-permute-start.6) | collective-permute-done | bytes 2097184 | tf_op jit(solution)/shard_map/ppermute | solution.py:493
  128.2 21.5 %collective-permute-done.7.refs_8_ = bf16[4096,256]{1,0:T(8,128)(2,1)S(1)} collective-permute-done((bf16[4096,256]{1,0:T(8,128)(2,1)S(1)}, bf16[4096,256]{1,0:T(8,128)(2,1)S(1)}, u32[]{:S(2)}, u32[]{:S(2)}) %collective-permute-start.7) | collective-permute-done | bytes 2097184 | tf_op jit(solution)/shard_map/ppermute | solution.py:493
  158.5 14.4 %pair_index.1 = (s32[4320]{0:T(1024)}, s32[3]{0:T(128)}) custom-call(s32[2]{0:T(128)} %pad_add_fusion.me_ref, s32[12288]{0:T(1024)} %constant.25.clone.table_ref, s32[512]{0:T(512)} %reshape.12.ends_ref, s32[2048]{0:T(1024)} %reshape.13.blocks_ref), custom_call_target="tpu_custom_call" | custom-call | tf_op jit(solution)/shard_map/pair_index/pallas_call | solution.py:188
  172.9 12.2 %shard_map.76.refs_13_ = f32[148,256,256]{2,1,0:T(8,128)} custom-call(s32[4320]{0:T(1024)} %get-tuple-element.28.info_ref, s32[3]{0:T(128)} %get-tuple-element.29.count_ref, bf16[2,4096,256]{2,1,0:T(8,128)(2,1)} %patch_ref.1, bf16[4096,256]{1,0:T(8,128)(2,1)} %copy-done.1, bf16[4096,256]{1,0:T(8,128)(2,1)} %copy-done.2, bf16[4096,256]{1,0:T(8,128)(2,1)} %copy-done.3, ...), custom_call_target="tpu_custom_call" | custom-call | tf_op jit(solution)/shard_map/pallas_call | solution.py:273
  185.1 12.7 %shard_map.77.refs_17_ = f32[148,256,256]{2,1,0:T(8,128)} custom-call(s32[4320]{0:T(1024)} %get-tuple-element.28.info_ref, s32[3]{0:T(128)} %get-tuple-element.29.count_ref, bf16[2,4096,256]{2,1,0:T(8,128)(2,1)} %patch_ref.1, bf16[4096,256]{1,0:T(8,128)(2,1)} %copy-done.1, bf16[4096,256]{1,0:T(8,128)(2,1)} %copy-done.2, ...), custom_call_target="tpu_custom_call", output_to_operand_aliasing={{}: (15, {})} | custom-call | tf_op jit(solution)/shard_map/pallas_call | solution.py:273
  197.9 10.9 %shard_map.78.rot_ref = f32[148,256,256]{2,1,0:T(8,128)} custom-call(s32[4320]{0:T(1024)} %get-tuple-element.28.info_ref, s32[3]{0:T(128)} %get-tuple-element.29.count_ref, bf16[2,4096,256]{2,1,0:T(8,128)(2,1)} %patch_ref.1, bf16[4096,256]{1,0:T(8,128)(2,1)} %copy-done.1, bf16[4096,256]{1,0:T(8,128)(2,1)} %copy-done.2, ...), custom_call_target="tpu_custom_call", output_to_operand_aliasing={{}: (19, {})} | custom-call | tf_op jit(solution)/shard_map/pallas_call | solution.py:273
  208.8 8.1 %estimates.2 = (f32[2,256,256]{2,1,0:T(8,128)}, f32[2,256,256]{2,1,0:T(8,128)}, f32[2,256,256]{2,1,0:T(8,128)}, f32[2,256,256]{2,1,0:T(8,128)}, f32[2,256,256]{2...) custom-call(s32[4320]{0:T(1024)} %get-tuple-element.28.info_ref, s32[3]{0:T(128)} %get-tuple-element.29.count_ref, ...), custom_call_target="tpu_custom_call" | custom-call | tf_op jit(solution)/shard_map/estimates/pallas_call | solution.py:384
  216.9 18.5 %collective-permute-start.24 = (f32[6,256,256]{2,1,0:T(8,128)}, f32[6,256,256]{2,1,0:T(8,128)S(1)}, u32[]{:S(2)}, u32[]{:S(2)}) collective-permute-start(f32[6,256,256]{2,1,0:T(8,128)} %get-tuple-element.33), channel_id=1, source_target_pairs={{0,1},{1,0},{2,3},{3,2},{4,5},{5,4},{6,7},{7,6},{8,9},{9,8},{10,11... | collective-permute-start | bytes 4718600 | tf_op jit(solution)/shard_map/ppermute | solution.py:493
  235.4 3.2 collective-permute-done.24
  240.6 4.5 %collective-permute-done.26 = f32[2,256,256]{2,1,0:T(8,128)S(1)} collective-permute-done((f32[2,256,256]{2,1,0:T(8,128)}, f32[2,256,256]{2,1,0:T(8,128)S(1)}, u32[]{:S(2)}, u32[]{:S(2)}) %collective-permute-start.26) | collective-permute-done | bytes 524320 | tf_op jit(solution)/shard_map/ppermute | solution.py:493
  250.4 5.5 %collective-permute-done.27.refs_2_ = f32[2,256,256]{2,1,0:T(8,128)S(1)} collective-permute-done((f32[2,256,256]{2,1,0:T(8,128)S(1)}, f32[2,256,256]{2,1,0:T(8,128)S(1)}, u32[]{:S(2)}, u32[]{:S(2)}) %collective-permute-start.27) | collective-permute-done | bytes 524320 | tf_op jit(solution)/shard_map/ppermute | solution.py:493
  255.9 3.7 collective-permute-done.25.refs_1_
  259.5 2.8 collective-permute-done.29.refs_3_
  263.2 8.2 %update_frames.2 = (f32[2,256,256]{2,1,0:T(8,128)}, bf16[2,256,256]{2,1,0:T(8,128)(2,1)}, f32[256,256]{1,0:T(8,128)}) custom-call(f32[2,256,256]{2,1,0:T(8,128)} %get-tuple-element.27.frame_ref, f32[2,256,256]{2,1,0:T(8,128)} %get-tuple-element.31.refs_0_, f32[2,256,256]{2,1,0:T(8,128)} %copy-done.21, f32[2,256,256]{2,1,0:T(8,128)} %copy-done.19, ...), custom_call_target="tpu_custom_call" | custom-call | tf_op jit(solution)/shard_map/update_frames/pallas_call | solution.py:416
  272.8 5.5 %collective-permute-done.30.refs_1_ = bf16[2,256,256]{2,1,0:T(8,128)(2,1)S(1)} collective-permute-done((bf16[2,256,256]{2,1,0:T(8,128)(2,1)}, bf16[2,256,256]{2,1,0:T(8,128)(2,1)S(1)}, u32[]{:S(2)}, u32[]{:S(2)}) %collective-permute-start.30) | collective-permute-done | bytes 262176 | tf_op jit(solution)/shard_map/ppermute | solution.py:493
  278.3 4.1 %collective-permute-start.35 = (bf16[2,256,256]{2,1,0:T(8,128)(2,1)S(1)}, bf16[2,256,256]{2,1,0:T(8,128)(2,1)S(1)}, u32[]{:S(2)}, u32[]{:S(2)}) collective-permute-start(bf16[2,256,256]{2,1,0:T(8,128)(2,1)S(1)} %collective-permute-done.30.refs_1_), channel_id=1, source_target_pairs={{0,1},{1,0},{2,3},{3,2},{4,5},{5,4},{6,7},{7,6},{8,9},{9,8},{10,11... | collective-permute-start | bytes 786440 | tf_op jit(solution)/shard_map/ppermute | solution.py:493
  282.4 3.0 collective-permute-start.34
  285.9 4.0 %collective-permute-start.36 = (bf16[2,256,256]{2,1,0:T(8,128)(2,1)S(1)}, bf16[2,256,256]{2,1,0:T(8,128)(2,1)S(1)}, u32[]{:S(2)}, u32[]{:S(2)}) collective-permute-start(bf16[2,256,256]{2,1,0:T(8,128)(2,1)S(1)} %collective-permute-done.31.refs_2_), channel_id=1, source_target_pairs={{0,1},{1,0},{2,3},{3,2},{4,5},{5,4},{6,7},{7,6},{8,9},{9,8},{10,11... | collective-permute-start | bytes 786440 | tf_op jit(solution)/shard_map/ppermute | solution.py:493
  291.9 8.1 %estimates.3 = (f32[2,256,256]{2,1,0:T(8,128)}, f32[2,256,256]{2,1,0:T(8,128)}, f32[2,256,256]{2,1,0:T(8,128)}, f32[2,256,256]{2,1,0:T(8,128)}, f32[2,256,256]{2...) custom-call(s32[4320]{0:T(1024)} %get-tuple-element.28.info_ref, s32[3]{0:T(128)} %get-tuple-element.29.count_ref, ...), custom_call_target="tpu_custom_call" | custom-call | tf_op jit(solution)/shard_map/estimates/pallas_call | solution.py:384
  302.0 3.2 collective-permute-done.38
  306.3 3.3 collective-permute-start.42
  309.6 2.1 collective-permute-done.40
  312.9 2.8 collective-permute-done.42
  317.4 3.4 collective-permute-start.43
  322.4 3.3 collective-permute-done.39.refs_1_
  325.7 5.9 %collective-permute-done.43.refs_3_ = f32[2,256,256]{2,1,0:T(8,128)S(1)} collective-permute-done((f32[2,256,256]{2,1,0:T(8,128)S(1)}, f32[2,256,256]{2,1,0:T(8,128)S(1)}, u32[]{:S(2)}, u32[]{:S(2)}) %collective-permute-start.43) | collective-permute-done | bytes 524320 | tf_op jit(solution)/shard_map/ppermute | solution.py:493
  332.4 8.1 %update_frames.3 = (f32[2,256,256]{2,1,0:T(8,128)}, bf16[2,256,256]{2,1,0:T(8,128)(2,1)}, f32[256,256]{1,0:T(8,128)}) custom-call(f32[2,256,256]{2,1,0:T(8,128)} %get-tuple-element.38.frame_ref, f32[2,256,256]{2,1,0:T(8,128)} %get-tuple-element.40.refs_0_, f32[2,256,256]{2,1,0:T(8,128)} %copy-done.20, f32[2,256,256]{2,1,0:T(8,128)} %copy-done.18, ...), custom_call_target="tpu_custom_call" | custom-call | tf_op jit(solution)/shard_map/update_frames/pallas_call | solution.py:416
  344.0 2.7 collective-permute-start.46
  346.7 3.4 collective-permute-done.45
  352.7 2.7 collective-permute-start.49
  355.3 2.3 collective-permute-done.48
  358.7 2.3 collective-permute-done.50
  361.1 3.4 collective-permute-start.52
  366.8 3.2 collective-permute-done.53
  370.0 4.1 %collective-permute-start.54 = (f32[128,256]{1,0:T(8,128)S(1)}, f32[128,256]{1,0:T(8,128)S(1)}, u32[]{:S(2)}, u32[]{:S(2)}) collective-permute-start(f32[128,256]{1,0:T(8,128)S(1)} %add_add_fusion), channel_id=1, source_target_pairs={{0,1},{1,0},{2,3},{3,2},{4,5},{5,4},{6,7},{7,6},{8,9},{9,8},{10,11... | collective-permute-start | bytes 393224 | tf_op jit(solution)/shard_map/ppermute | solution.py:539
  375.8 10.4 %aligned_rows.1 = (bf16[2,4096,256]{2,1,0:T(8,128)(2,1)}, f32[2,256,256]{2,1,0:T(8,128)}) custom-call(f32[256,256]{1,0:T(8,128)} %pad_maximum_fusion.total_ref, f32[2,256,256]{2,1,0:T(8,128)} %get-tuple-element.48.frame_ref, bf16[2,4096,256]{2,1,0:T(8,128)(2,1)} %patch_ref.1), custom_call_target="tpu_custom_call" | custom-call | tf_op jit(solution)/shard_map/aligned_rows/pallas_call | solution.py:471
  (167 shorter events, 48.9 us)
Async XLA Ops:
  3.2 34.8 %collective-permute-start.3 = (bf16[4096,256]{1,0:T(8,128)(2,1)S(1)}, bf16[4096,256]{1,0:T(8,128)(2,1)S(1)}, u32[]{:S(2)}, u32[]{:S(2)}) collective-permute-start(bf16[4096,256]{1,0:T(8,128)(2,1)S(1)} %get-tuple-element.51), channel_id=1, source_target_pairs={{0,6},{1,25},{2,0},{3,27},{4,2},{5,29},{6,4},{7,31},{8,14},{9,1},{... | collective-permute-start | bytes 6291464 | tf_op jit(solution)/shard_map/ppermute | solution.py:493
  15.2 6.9 %collective-permute-start.16 = (bf16[2,256,256]{2,1,0:T(8,128)(2,1)}, bf16[2,256,256]{2,1,0:T(8,128)(2,1)S(1)}, u32[]{:S(2)}, u32[]{:S(2)}) collective-permute-start(bf16[2,256,256]{2,1,0:T(8,128)(2,1)} %get-tuple-element.30.refs_0_), channel_id=1, source_target_pairs={{0,8},{1,3},{2,10},{3,5},{4,12},{5,7},{6,14},{7,1},{8,16},{9,11},{... | collective-permute-start | bytes 786440 | tf_op jit(solution)/shard_map/ppermute | solution.py:493
  16.4 17.3 %collective-permute-start.19 = (bf16[2,256,256]{2,1,0:T(8,128)(2,1)}, bf16[2,256,256]{2,1,0:T(8,128)(2,1)S(1)}, u32[]{:S(2)}, u32[]{:S(2)}) collective-permute-start(bf16[2,256,256]{2,1,0:T(8,128)(2,1)} %get-tuple-element.30.refs_0_), channel_id=1, source_target_pairs={{0,6},{1,25},{2,0},{3,27},{4,2},{5,29},{6,4},{7,31},{8,14},{9,1},{... | collective-permute-start | bytes 786440 | tf_op jit(solution)/shard_map/ppermute | solution.py:493
  16.5 18.4 %collective-permute-start.18 = (bf16[2,256,256]{2,1,0:T(8,128)(2,1)}, bf16[2,256,256]{2,1,0:T(8,128)(2,1)S(1)}, u32[]{:S(2)}, u32[]{:S(2)}) collective-permute-start(bf16[2,256,256]{2,1,0:T(8,128)(2,1)} %get-tuple-element.30.refs_0_), channel_id=1, source_target_pairs={{0,2},{1,9},{2,4},{3,11},{4,6},{5,13},{6,0},{7,15},{8,10},{9,17},{... | collective-permute-start | bytes 786440 | tf_op jit(solution)/shard_map/ppermute | solution.py:493
  22.1 15.8 %collective-permute-start.17 = (bf16[2,256,256]{2,1,0:T(8,128)(2,1)S(1)}, bf16[2,256,256]{2,1,0:T(8,128)(2,1)S(1)}, u32[]{:S(2)}, u32[]{:S(2)}) collective-permute-start(bf16[2,256,256]{2,1,0:T(8,128)(2,1)S(1)} %collective-permute-done.16.refs_1_), channel_id=1, source_target_pairs={{0,8},{1,3},{2,10},{3,5},{4,12},{5,7},{6,14},{7,1},{8,16},{9,11},{... | collective-permute-start | bytes 786440 | tf_op jit(solution)/shard_map/ppermute | solution.py:493
  22.9 37.3 %collective-permute-start = (bf16[4096,256]{1,0:T(8,128)(2,1)S(1)}, bf16[4096,256]{1,0:T(8,128)(2,1)S(1)}, u32[]{:S(2)}, u32[]{:S(2)}) collective-permute-start(bf16[4096,256]{1,0:T(8,128)(2,1)S(1)} %get-tuple-element.52), channel_id=1, source_target_pairs={{0,8},{1,3},{2,10},{3,5},{4,12},{5,7},{6,14},{7,1},{8,16},{9,11},{... | collective-permute-start | bytes 6291464 | tf_op jit(solution)/shard_map/ppermute | solution.py:493
  33.7 63.3 %collective-permute-start.1 = (bf16[4096,256]{1,0:T(8,128)(2,1)S(1)}, bf16[4096,256]{1,0:T(8,128)(2,1)S(1)}, u32[]{:S(2)}, u32[]{:S(2)}) collective-permute-start(bf16[4096,256]{1,0:T(8,128)(2,1)S(1)} %get-tuple-element.51), channel_id=1, source_target_pairs={{0,8},{1,3},{2,10},{3,5},{4,12},{5,7},{6,14},{7,1},{8,16},{9,11},{... | collective-permute-start | bytes 6291464 | tf_op jit(solution)/shard_map/ppermute | solution.py:493
  34.9 66.0 %collective-permute-start.2 = (bf16[4096,256]{1,0:T(8,128)(2,1)S(1)}, bf16[4096,256]{1,0:T(8,128)(2,1)S(1)}, u32[]{:S(2)}, u32[]{:S(2)}) collective-permute-start(bf16[4096,256]{1,0:T(8,128)(2,1)S(1)} %get-tuple-element.52), channel_id=1, source_target_pairs={{0,6},{1,25},{2,0},{3,27},{4,2},{5,29},{6,4},{7,31},{8,14},{9,1},{... | collective-permute-start | bytes 6291464 | tf_op jit(solution)/shard_map/ppermute | solution.py:493
  37.9 63.0 %collective-permute-start.12 = (bf16[4096,256]{1,0:T(8,128)(2,1)S(1)}, bf16[4096,256]{1,0:T(8,128)(2,1)S(1)}, u32[]{:S(2)}, u32[]{:S(2)}) collective-permute-start(bf16[4096,256]{1,0:T(8,128)(2,1)S(1)} %get-tuple-element.52), channel_id=1, source_target_pairs={{0,2},{1,9},{2,4},{3,11},{4,6},{5,13},{6,0},{7,15},{8,10},{9,17},{... | collective-permute-start | bytes 6291464 | tf_op jit(solution)/shard_map/ppermute | solution.py:493
  38.0 63.1 %collective-permute-start.9 = (bf16[4096,256]{1,0:T(8,128)(2,1)S(1)}, bf16[4096,256]{1,0:T(8,128)(2,1)S(1)}, u32[]{:S(2)}, u32[]{:S(2)}) collective-permute-start(bf16[4096,256]{1,0:T(8,128)(2,1)S(1)} %collective-permute-done.3.refs_4_), channel_id=1, source_target_pairs={{0,6},{1,25},{2,0},{3,27},{4,2},{5,29},{6,4},{7,31},{8,14},{9,1},{... | collective-permute-start | bytes 6291464 | tf_op jit(solution)/shard_map/ppermute | solution.py:493
  60.2 41.3 %collective-permute-start.4 = (bf16[4096,256]{1,0:T(8,128)(2,1)S(1)}, bf16[4096,256]{1,0:T(8,128)(2,1)S(1)}, u32[]{:S(2)}, u32[]{:S(2)}) collective-permute-start(bf16[4096,256]{1,0:T(8,128)(2,1)S(1)} %collective-permute-done.refs_1_), channel_id=1, source_target_pairs={{0,1},{1,0},{2,3},{3,2},{4,5},{5,4},{6,7},{7,6},{8,9},{9,8},{10,11... | collective-permute-start | bytes 6291464 | tf_op jit(solution)/shard_map/ppermute | solution.py:493
  97.0 7.7 %collective-permute-start.5 = (bf16[4096,256]{1,0:T(8,128)(2,1)S(1)}, bf16[4096,256]{1,0:T(8,128)(2,1)S(1)}, u32[]{:S(2)}, u32[]{:S(2)}) collective-permute-start(bf16[4096,256]{1,0:T(8,128)(2,1)S(1)} %collective-permute-done.1.refs_2_), channel_id=1, source_target_pairs={{0,1},{1,0},{2,3},{3,2},{4,5},{5,4},{6,7},{7,6},{8,9},{9,8},{10,11... | collective-permute-start | bytes 6291464 | tf_op jit(solution)/shard_map/ppermute | solution.py:493
  100.9 26.4 %collective-permute-start.6 = (bf16[4096,256]{1,0:T(8,128)(2,1)S(1)}, bf16[4096,256]{1,0:T(8,128)(2,1)S(1)}, u32[]{:S(2)}, u32[]{:S(2)}) collective-permute-start(bf16[4096,256]{1,0:T(8,128)(2,1)S(1)} %collective-permute-done.refs_1_), channel_id=1, source_target_pairs={{0,8},{1,3},{2,10},{3,5},{4,12},{5,7},{6,14},{7,1},{8,16},{9,11},{... | collective-permute-start | bytes 6291464 | tf_op jit(solution)/shard_map/ppermute | solution.py:493
  100.9 48.8 %collective-permute-start.7 = (bf16[4096,256]{1,0:T(8,128)(2,1)S(1)}, bf16[4096,256]{1,0:T(8,128)(2,1)S(1)}, u32[]{:S(2)}, u32[]{:S(2)}) collective-permute-start(bf16[4096,256]{1,0:T(8,128)(2,1)S(1)} %collective-permute-done.1.refs_2_), channel_id=1, source_target_pairs={{0,8},{1,3},{2,10},{3,5},{4,12},{5,7},{6,14},{7,1},{8,16},{9,11},{... | collective-permute-start | bytes 6291464 | tf_op jit(solution)/shard_map/ppermute | solution.py:493
  101.0 49.7 %collective-permute-start.13 = (bf16[4096,256]{1,0:T(8,128)(2,1)S(1)}, bf16[4096,256]{1,0:T(8,128)(2,1)}, u32[]{:S(2)}, u32[]{:S(2)}) collective-permute-start(bf16[4096,256]{1,0:T(8,128)(2,1)S(1)} %collective-permute-done.9.refs_10_), channel_id=1, source_target_pairs={{0,6},{1,25},{2,0},{3,27},{4,2},{5,29},{6,4},{7,31},{8,14},{9,1},{... | collective-permute-start | bytes 6291464 | tf_op jit(solution)/shard_map/ppermute | solution.py:493
  101.5 49.3 %collective-permute-start.8 = (bf16[4096,256]{1,0:T(8,128)(2,1)S(1)}, bf16[4096,256]{1,0:T(8,128)(2,1)S(1)}, u32[]{:S(2)}, u32[]{:S(2)}) collective-permute-start(bf16[4096,256]{1,0:T(8,128)(2,1)S(1)} %collective-permute-done.2.refs_3_), channel_id=1, source_target_pairs={{0,6},{1,25},{2,0},{3,27},{4,2},{5,29},{6,4},{7,31},{8,14},{9,1},{... | collective-permute-start | bytes 6291464 | tf_op jit(solution)/shard_map/ppermute | solution.py:493
  104.7 46.6 %collective-permute-start.14 = (bf16[4096,256]{1,0:T(8,128)(2,1)S(1)}, bf16[4096,256]{1,0:T(8,128)(2,1)S(1)}, u32[]{:S(2)}, u32[]{:S(2)}) collective-permute-start(bf16[4096,256]{1,0:T(8,128)(2,1)S(1)} %collective-permute-done.12.refs_13_), channel_id=1, source_target_pairs={{0,1},{1,0},{2,3},{3,2},{4,5},{5,4},{6,7},{7,6},{8,9},{9,8},{10,11... | collective-permute-start | bytes 6291464 | tf_op jit(solution)/shard_map/ppermute | solution.py:493
  127.3 25.4 %collective-permute-start.10 = (bf16[4096,256]{1,0:T(8,128)(2,1)S(1)}, bf16[4096,256]{1,0:T(8,128)(2,1)S(1)}, u32[]{:S(2)}, u32[]{:S(2)}) collective-permute-start(bf16[4096,256]{1,0:T(8,128)(2,1)S(1)} %collective-permute-done.6.refs_7_), channel_id=1, source_target_pairs={{0,1},{1,0},{2,3},{3,2},{4,5},{5,4},{6,7},{7,6},{8,9},{9,8},{10,11... | collective-permute-start | bytes 6291464 | tf_op jit(solution)/shard_map/ppermute | solution.py:493
  150.7 47.1 %collective-permute-start.15 = (bf16[4096,256]{1,0:T(8,128)(2,1)}, bf16[4096,256]{1,0:T(8,128)(2,1)}, u32[]{:S(2)}, u32[]{:S(2)}) collective-permute-start(bf16[4096,256]{1,0:T(8,128)(2,1)} %collective-permute-done.13.refs_14_), channel_id=1, source_target_pairs={{0,1},{1,0},{2,3},{3,2},{4,5},{5,4},{6,7},{7,6},{8,9},{9,8},{10,11... | collective-permute-start | bytes 6291464 | tf_op jit(solution)/shard_map/ppermute | solution.py:493
  150.8 58.0 %collective-permute-start.21 = (bf16[2,256,256]{2,1,0:T(8,128)(2,1)S(1)}, bf16[2,256,256]{2,1,0:T(8,128)(2,1)}, u32[]{:S(2)}, u32[]{:S(2)}) collective-permute-start(bf16[2,256,256]{2,1,0:T(8,128)(2,1)S(1)} %collective-permute-done.16.refs_1_), channel_id=1, source_target_pairs={{0,1},{1,0},{2,3},{3,2},{4,5},{5,4},{6,7},{7,6},{8,9},{9,8},{10,11... | collective-permute-start | bytes 786440 | tf_op jit(solution)/shard_map/ppermute | solution.py:493
  151.3 57.5 %collective-permute-start.20 = (bf16[2,256,256]{2,1,0:T(8,128)(2,1)S(1)}, bf16[2,256,256]{2,1,0:T(8,128)(2,1)}, u32[]{:S(2)}, u32[]{:S(2)}) collective-permute-start(bf16[2,256,256]{2,1,0:T(8,128)(2,1)S(1)} %collective-permute-done.19.refs_4_), channel_id=1, source_target_pairs={{0,6},{1,25},{2,0},{3,27},{4,2},{5,29},{6,4},{7,31},{8,14},{9,1},{... | collective-permute-start | bytes 786440 | tf_op jit(solution)/shard_map/ppermute | solution.py:493
  152.7 56.1 %collective-permute-start.23 = (bf16[2,256,256]{2,1,0:T(8,128)(2,1)S(1)}, bf16[2,256,256]{2,1,0:T(8,128)(2,1)}, u32[]{:S(2)}, u32[]{:S(2)}) collective-permute-start(bf16[2,256,256]{2,1,0:T(8,128)(2,1)S(1)} %collective-permute-done.18.refs_3_), channel_id=1, source_target_pairs={{0,1},{1,0},{2,3},{3,2},{4,5},{5,4},{6,7},{7,6},{8,9},{9,8},{10,11... | collective-permute-start | bytes 786440 | tf_op jit(solution)/shard_map/ppermute | solution.py:493
  154.5 54.3 %collective-permute-start.22 = (bf16[2,256,256]{2,1,0:T(8,128)(2,1)S(1)}, bf16[2,256,256]{2,1,0:T(8,128)(2,1)}, u32[]{:S(2)}, u32[]{:S(2)}) collective-permute-start(bf16[2,256,256]{2,1,0:T(8,128)(2,1)S(1)} %collective-permute-done.17.refs_2_), channel_id=1, source_target_pairs={{0,1},{1,0},{2,3},{3,2},{4,5},{5,4},{6,7},{7,6},{8,9},{9,8},{10,11... | collective-permute-start | bytes 786440 | tf_op jit(solution)/shard_map/ppermute | solution.py:493
  216.9 21.7 %collective-permute-start.24 = (f32[6,256,256]{2,1,0:T(8,128)}, f32[6,256,256]{2,1,0:T(8,128)S(1)}, u32[]{:S(2)}, u32[]{:S(2)}) collective-permute-start(f32[6,256,256]{2,1,0:T(8,128)} %get-tuple-element.33), channel_id=1, source_target_pairs={{0,1},{1,0},{2,3},{3,2},{4,5},{5,4},{6,7},{7,6},{8,9},{9,8},{10,11... | collective-permute-start | bytes 4718600 | tf_op jit(solution)/shard_map/ppermute | solution.py:493
  235.4 9.7 %collective-permute-start.26 = (f32[2,256,256]{2,1,0:T(8,128)}, f32[2,256,256]{2,1,0:T(8,128)S(1)}, u32[]{:S(2)}, u32[]{:S(2)}) collective-permute-start(f32[2,256,256]{2,1,0:T(8,128)} %get-tuple-element.35), channel_id=1, source_target_pairs={{6,0},{25,1},{0,2},{27,3},{2,4},{29,5},{4,6},{31,7},{14,8},{1,9},{... | collective-permute-start | bytes 1572872 | tf_op jit(solution)/shard_map/ppermute | solution.py:493
  239.7 8.4 %collective-permute-start.28 = (f32[2,256,256]{2,1,0:T(8,128)S(1)}, f32[2,256,256]{2,1,0:T(8,128)S(1)}, u32[]{:S(2)}, u32[]{:S(2)}) collective-permute-start(f32[2,256,256]{2,1,0:T(8,128)S(1)} %slice_add_fusion.3), channel_id=1, source_target_pairs={{8,0},{3,1},{10,2},{5,3},{12,4},{7,5},{14,6},{1,7},{16,8},{11,9},{... | collective-permute-start | bytes 1572872 | tf_op jit(solution)/shard_map/ppermute | solution.py:493
  246.2 9.6 %collective-permute-start.27 = (f32[2,256,256]{2,1,0:T(8,128)S(1)}, f32[2,256,256]{2,1,0:T(8,128)S(1)}, u32[]{:S(2)}, u32[]{:S(2)}) collective-permute-start(f32[2,256,256]{2,1,0:T(8,128)S(1)} %add.69), channel_id=1, source_target_pairs={{6,0},{25,1},{0,2},{27,3},{2,4},{29,5},{4,6},{31,7},{14,8},{1,9},{... | collective-permute-start | bytes 1572872 | tf_op jit(solution)/shard_map/ppermute | solution.py:493
  248.3 11.2 %collective-permute-start.25 = (f32[2,256,256]{2,1,0:T(8,128)S(1)}, f32[2,256,256]{2,1,0:T(8,128)S(1)}, u32[]{:S(2)}, u32[]{:S(2)}) collective-permute-start(f32[2,256,256]{2,1,0:T(8,128)S(1)} %get-tuple-element.56), channel_id=1, source_target_pairs={{2,0},{9,1},{4,2},{11,3},{6,4},{13,5},{0,6},{15,7},{10,8},{17,9},{... | collective-permute-start | bytes 1572872 | tf_op jit(solution)/shard_map/ppermute | solution.py:493
  249.3 13.1 %collective-permute-start.29 = (f32[2,256,256]{2,1,0:T(8,128)S(1)}, f32[2,256,256]{2,1,0:T(8,128)S(1)}, u32[]{:S(2)}, u32[]{:S(2)}) collective-permute-start(f32[2,256,256]{2,1,0:T(8,128)S(1)} %get-tuple-element.55), channel_id=1, source_target_pairs={{8,0},{3,1},{10,2},{5,3},{12,4},{7,5},{14,6},{1,7},{16,8},{11,9},{... | collective-permute-start | bytes 1572872 | tf_op jit(solution)/shard_map/ppermute | solution.py:493
  271.3 6.9 %collective-permute-start.30 = (bf16[2,256,256]{2,1,0:T(8,128)(2,1)}, bf16[2,256,256]{2,1,0:T(8,128)(2,1)S(1)}, u32[]{:S(2)}, u32[]{:S(2)}) collective-permute-start(bf16[2,256,256]{2,1,0:T(8,128)(2,1)} %get-tuple-element.39.refs_0_), channel_id=1, source_target_pairs={{0,8},{1,3},{2,10},{3,5},{4,12},{5,7},{6,14},{7,1},{8,16},{9,11},{... | collective-permute-start | bytes 786440 | tf_op jit(solution)/shard_map/ppermute | solution.py:493
  271.3 11.0 %collective-permute-start.33 = (bf16[2,256,256]{2,1,0:T(8,128)(2,1)}, bf16[2,256,256]{2,1,0:T(8,128)(2,1)S(1)}, u32[]{:S(2)}, u32[]{:S(2)}) collective-permute-start(bf16[2,256,256]{2,1,0:T(8,128)(2,1)} %get-tuple-element.39.refs_0_), channel_id=1, source_target_pairs={{0,6},{1,25},{2,0},{3,27},{4,2},{5,29},{6,4},{7,31},{8,14},{9,1},{... | collective-permute-start | bytes 786440 | tf_op jit(solution)/shard_map/ppermute | solution.py:493
  272.2 13.1 %collective-permute-start.32 = (bf16[2,256,256]{2,1,0:T(8,128)(2,1)}, bf16[2,256,256]{2,1,0:T(8,128)(2,1)S(1)}, u32[]{:S(2)}, u32[]{:S(2)}) collective-permute-start(bf16[2,256,256]{2,1,0:T(8,128)(2,1)} %get-tuple-element.39.refs_0_), channel_id=1, source_target_pairs={{0,2},{1,9},{2,4},{3,11},{4,6},{5,13},{6,0},{7,15},{8,10},{9,17},{... | collective-permute-start | bytes 786440 | tf_op jit(solution)/shard_map/ppermute | solution.py:493
  278.3 7.7 %collective-permute-start.31 = (bf16[2,256,256]{2,1,0:T(8,128)(2,1)S(1)}, bf16[2,256,256]{2,1,0:T(8,128)(2,1)S(1)}, u32[]{:S(2)}, u32[]{:S(2)}) collective-permute-start(bf16[2,256,256]{2,1,0:T(8,128)(2,1)S(1)} %collective-permute-done.30.refs_1_), channel_id=1, source_target_pairs={{0,8},{1,3},{2,10},{3,5},{4,12},{5,7},{6,14},{7,1},{8,16},{9,11},{... | collective-permute-start | bytes 786440 | tf_op jit(solution)/shard_map/ppermute | solution.py:493
  278.3 11.7 %collective-permute-start.35 = (bf16[2,256,256]{2,1,0:T(8,128)(2,1)S(1)}, bf16[2,256,256]{2,1,0:T(8,128)(2,1)S(1)}, u32[]{:S(2)}, u32[]{:S(2)}) collective-permute-start(bf16[2,256,256]{2,1,0:T(8,128)(2,1)S(1)} %collective-permute-done.30.refs_1_), channel_id=1, source_target_pairs={{0,1},{1,0},{2,3},{3,2},{4,5},{5,4},{6,7},{7,6},{8,9},{9,8},{10,11... | collective-permute-start | bytes 786440 | tf_op jit(solution)/shard_map/ppermute | solution.py:493
  282.4 7.6 %collective-permute-start.34 = (bf16[2,256,256]{2,1,0:T(8,128)(2,1)S(1)}, bf16[2,256,256]{2,1,0:T(8,128)(2,1)S(1)}, u32[]{:S(2)}, u32[]{:S(2)}) collective-permute-start(bf16[2,256,256]{2,1,0:T(8,128)(2,1)S(1)} %collective-permute-done.33.refs_4_), channel_id=1, source_target_pairs={{0,6},{1,25},{2,0},{3,27},{4,2},{5,29},{6,4},{7,31},{8,14},{9,1},{... | collective-permute-start | bytes 786440 | tf_op jit(solution)/shard_map/ppermute | solution.py:493
  301.9 9.7 %collective-permute-start.40 = (f32[2,256,256]{2,1,0:T(8,128)}, f32[2,256,256]{2,1,0:T(8,128)S(1)}, u32[]{:S(2)}, u32[]{:S(2)}) collective-permute-start(f32[2,256,256]{2,1,0:T(8,128)} %get-tuple-element.44), channel_id=1, source_target_pairs={{6,0},{25,1},{0,2},{27,3},{2,4},{29,5},{4,6},{31,7},{14,8},{1,9},{... | collective-permute-start | bytes 1572872 | tf_op jit(solution)/shard_map/ppermute | solution.py:493
  306.3 9.4 %collective-permute-start.42 = (f32[2,256,256]{2,1,0:T(8,128)S(1)}, f32[2,256,256]{2,1,0:T(8,128)S(1)}, u32[]{:S(2)}, u32[]{:S(2)}) collective-permute-start(f32[2,256,256]{2,1,0:T(8,128)S(1)} %slice_add_fusion), channel_id=1, source_target_pairs={{8,0},{3,1},{10,2},{5,3},{12,4},{7,5},{14,6},{1,7},{16,8},{11,9},{... | collective-permute-start | bytes 1572872 | tf_op jit(solution)/shard_map/ppermute | solution.py:493
  312.8 9.6 %collective-permute-start.41 = (f32[2,256,256]{2,1,0:T(8,128)S(1)}, f32[2,256,256]{2,1,0:T(8,128)S(1)}, u32[]{:S(2)}, u32[]{:S(2)}) collective-permute-start(f32[2,256,256]{2,1,0:T(8,128)S(1)} %add.74), channel_id=1, source_target_pairs={{6,0},{25,1},{0,2},{27,3},{2,4},{29,5},{4,6},{31,7},{14,8},{1,9},{... | collective-permute-start | bytes 1572872 | tf_op jit(solution)/shard_map/ppermute | solution.py:493
  315.9 9.8 %collective-permute-start.39 = (f32[2,256,256]{2,1,0:T(8,128)S(1)}, f32[2,256,256]{2,1,0:T(8,128)S(1)}, u32[]{:S(2)}, u32[]{:S(2)}) collective-permute-start(f32[2,256,256]{2,1,0:T(8,128)S(1)} %get-tuple-element.54), channel_id=1, source_target_pairs={{2,0},{9,1},{4,2},{11,3},{6,4},{13,5},{0,6},{15,7},{10,8},{17,9},{... | collective-permute-start | bytes 1572872 | tf_op jit(solution)/shard_map/ppermute | solution.py:493
  317.4 14.2 %collective-permute-start.43 = (f32[2,256,256]{2,1,0:T(8,128)S(1)}, f32[2,256,256]{2,1,0:T(8,128)S(1)}, u32[]{:S(2)}, u32[]{:S(2)}) collective-permute-start(f32[2,256,256]{2,1,0:T(8,128)S(1)} %get-tuple-element.53), channel_id=1, source_target_pairs={{8,0},{3,1},{10,2},{5,3},{12,4},{7,5},{14,6},{1,7},{16,8},{11,9},{... | collective-permute-start | bytes 1572872 | tf_op jit(solution)/shard_map/ppermute | solution.py:493
  343.9 6.2 %collective-permute-start.45 = (f32[128,256]{1,0:T(8,128)S(1)}, f32[128,256]{1,0:T(8,128)S(1)}, u32[]{:S(2)}, u32[]{:S(2)}) collective-permute-start(f32[128,256]{1,0:T(8,128)S(1)} %select_add_fusion), channel_id=1, source_target_pairs={{0,32},{32,64},{64,96},{96,0},{1,33},{33,65},{65,97},{97,1},{2,34}... | collective-permute-start | bytes 393224 | tf_op jit(solution)/shard_map/ppermute | solution.py:525
  344.0 7.8 %collective-permute-start.46 = (f32[128,256]{1,0:T(8,128)S(1)}, f32[128,256]{1,0:T(8,128)S(1)}, u32[]{:S(2)}, u32[]{:S(2)}) collective-permute-start(f32[128,256]{1,0:T(8,128)S(1)} %select_add_fusion), channel_id=1, source_target_pairs={{0,96},{32,0},{64,32},{96,64},{1,97},{33,1},{65,33},{97,65},{2,98}... | collective-permute-start | bytes 393224 | tf_op jit(solution)/shard_map/ppermute | solution.py:525
  346.7 5.9 %collective-permute-start.47 = (f32[128,256]{1,0:T(8,128)S(1)}, f32[128,256]{1,0:T(8,128)S(1)}, u32[]{:S(2)}, u32[]{:S(2)}) collective-permute-start(f32[128,256]{1,0:T(8,128)S(1)} %select_add_fusion), channel_id=1, source_target_pairs={{0,64},{32,96},{64,0},{96,32},{1,65},{33,97},{65,1},{97,33},{2,66}... | collective-permute-start | bytes 393224 | tf_op jit(solution)/shard_map/ppermute | solution.py:525
  352.7 6.0 %collective-permute-start.49 = (f32[128,256]{1,0:T(8,128)S(1)}, f32[128,256]{1,0:T(8,128)S(1)}, u32[]{:S(2)}, u32[]{:S(2)}) collective-permute-start(f32[128,256]{1,0:T(8,128)S(1)} %add_add_fusion.2), channel_id=1, source_target_pairs={{0,24},{8,0},{16,8},{24,16},{1,25},{9,1},{17,9},{25,17},{2,26},{10... | collective-permute-start | bytes 393224 | tf_op jit(solution)/shard_map/ppermute | solution.py:525
  355.3 5.7 %collective-permute-start.50 = (f32[128,256]{1,0:T(8,128)S(1)}, f32[128,256]{1,0:T(8,128)S(1)}, u32[]{:S(2)}, u32[]{:S(2)}) collective-permute-start(f32[128,256]{1,0:T(8,128)S(1)} %add_add_fusion.2), channel_id=1, source_target_pairs={{0,16},{8,24},{16,0},{24,8},{1,17},{9,25},{17,1},{25,9},{2,18},{10... | collective-permute-start | bytes 393224 | tf_op jit(solution)/shard_map/ppermute | solution.py:525
  361.0 5.7 %collective-permute-start.51 = (f32[128,256]{1,0:T(8,128)S(1)}, f32[128,256]{1,0:T(8,128)S(1)}, u32[]{:S(2)}, u32[]{:S(2)}) collective-permute-start(f32[128,256]{1,0:T(8,128)S(1)} %add_add_fusion.1), channel_id=1, source_target_pairs={{0,2},{2,4},{4,6},{6,0},{1,3},{3,5},{5,7},{7,1},{8,10},{10,12},{12... | collective-permute-start | bytes 393224 | tf_op jit(solution)/shard_map/ppermute | solution.py:525
  361.1 5.7 %collective-permute-start.52 = (f32[128,256]{1,0:T(8,128)S(1)}, f32[128,256]{1,0:T(8,128)S(1)}, u32[]{:S(2)}, u32[]{:S(2)}) collective-permute-start(f32[128,256]{1,0:T(8,128)S(1)} %add_add_fusion.1), channel_id=1, source_target_pairs={{0,6},{2,0},{4,2},{6,4},{1,7},{3,1},{5,3},{7,5},{8,14},{10,8},{12,... | collective-permute-start | bytes 393224 | tf_op jit(solution)/shard_map/ppermute | solution.py:525
  364.5 5.5 %collective-permute-start.53 = (f32[128,256]{1,0:T(8,128)S(1)}, f32[128,256]{1,0:T(8,128)S(1)}, u32[]{:S(2)}, u32[]{:S(2)}) collective-permute-start(f32[128,256]{1,0:T(8,128)S(1)} %add_add_fusion.1), channel_id=1, source_target_pairs={{0,4},{2,6},{4,0},{6,2},{1,5},{3,7},{5,1},{7,3},{8,12},{10,14},{12... | collective-permute-start | bytes 393224 | tf_op jit(solution)/shard_map/ppermute | solution.py:525
  (45 other events, 1605.8 us)

commit v3 on v2

--- a/solution.py
+++ b/solution.py
@@ -70,7 +70,7 @@
     return [same[m] + [same[m ^ 1][k] for k in CROSS] for m in range(DEVS)]
 
 
-READY = ((0, 0), (0, 0), (1, 1), (2, 2), (0, 0), (1, 1), (0, 0), (1, 1), (2, 2))
+READY = ((0, 0), (0, 0), (2, 1), (1, 2), (0, 0), (1, 1), (0, 0), (2, 1), (1, 2))
 CLASSES = 3
 CHOICES = 3
 
@@ -400,37 +400,42 @@
     )(info, count, rot, *lows)
 
 
-def update_kernel(frame_ref, *refs):
-    parts, (out_ref, low_ref, sum_ref) = refs[:-3], refs[-3:]
+def update_kernel(core_ref, frame_ref, *refs):
+    parts, (out_ref, *more) = refs[: OWN - 2], refs[OWN - 2 :]
     for p in range(PER):
         total = frame_ref[p]
         for part in parts:
             total = total + part[p]
         out_ref[p] = total
     newton_schulz(out_ref, PER)
-    low_ref[...] = out_ref[...].astype(BF16)
-    sum_ref[...] = out_ref[0] + out_ref[1]
-
-
-def make_update(frames, parts):
+    if len(more) == 1:
+        more[0][...] = out_ref[...].astype(BF16)
+    else:
+        for ref, half in zip(more, (core_ref[0], 1 - core_ref[0])):
+            rows = pl.ds(pl.multiple_of(half * (D // 2), D // 2), D // 2)
+            ref[...] = out_ref[0, rows] + out_ref[1, rows]
+
+
+def make_update(frames, parts, core=None):
+    more = [jax.ShapeDtypeStruct((PER, D, D), BF16)]
+    if core is not None:
+        more = [jax.ShapeDtypeStruct((D // 2, D), F32)] * 2
     return pl.pallas_call(
         update_kernel,
-        in_specs=[VM] * (1 + len(parts)),
-        out_specs=[VM] * 3,
-        out_shape=[
-            jax.ShapeDtypeStruct((PER, D, D), F32),
-            jax.ShapeDtypeStruct((PER, D, D), BF16),
-            jax.ShapeDtypeStruct((D, D), F32),
-        ],
+        in_specs=[SM] + [VM] * (1 + len(parts)),
+        out_specs=[VM] * (1 + len(more)),
+        out_shape=[jax.ShapeDtypeStruct((PER, D, D), F32)] + more,
         compiler_params=params(),
         name="update_frames",
-    )(frames, *parts)
+    )(jnp.zeros(1, jnp.int32) if core is None else core, frames, *parts)
 
 
 CHUNK = 1024
 
 
-def final_kernel(total_ref, frame_ref, patch_ref, aligned_ref, final_ref, gauge, rows, outs, low, in_sem, out_sem):
+def final_kernel(
+    core_ref, keep_ref, other_ref, frame_ref, patch_ref, aligned_ref, final_ref, total_ref, gauge, rows, outs, low, in_sem, out_sem
+):
     pieces = patch_ref.shape[1] // CHUNK
 
     def piece(n):
@@ -446,6 +451,8 @@
 
     for n in range(PER * pieces):
         copy_in(n).start()
+    for ref, half in ((keep_ref, core_ref[0]), (other_ref, 1 - core_ref[0])):
+        total_ref[pl.ds(pl.multiple_of(half * (D // 2), D // 2), D // 2)] = ref[...]
     gauge[0] = total_ref[...]
     newton_schulz(gauge, 1)
     g = halves(gauge[0])
@@ -466,15 +473,16 @@
         copy_out(n).wait()
 
 
-def make_final(total, frames, patches):
+def make_final(core, keep, other, frames, patches):
     pieces = PER * patches.shape[1] // CHUNK
     return pl.pallas_call(
         final_kernel,
-        in_specs=[VM, VM, HBM],
-        out_specs=[HBM, VM],
+        in_specs=[SM, VM, VM, VM, HBM],
+        out_specs=[HBM, VM, VM],
         out_shape=[
             jax.ShapeDtypeStruct(patches.shape, BF16),
             jax.ShapeDtypeStruct((PER, D, D), F32),
+            jax.ShapeDtypeStruct((D, D), F32),
         ],
         scratch_shapes=[
             pltpu.VMEM((1, D, D), F32),
@@ -486,7 +494,7 @@
         ],
         compiler_params=params(),
         name="aligned_rows",
-    )(total, frames, patches)
+    )(core, keep, other, frames, patches)
 
 
 def send(value, perm):
@@ -494,7 +502,7 @@
 
 
 LAYOUT = ((0, 0), (0, 1)) + tuple(
-    (n + p, None) for n in (1, 7, 13, 3, 9, 5, 11, 15) for p in range(PER)
+    (n, None) for n in (1, 2, 13, 7, 10, 14, 3, 4, 8, 9, 5, 6, 15, 11, 12, 16)
 )
 
 
@@ -512,7 +520,9 @@
     own, one, two, three, four, five, cross = parts
     cross = send(cross, SIBLING)
     five = send(five, back_perm(LEFT))
-    one, two, three = (v + cross[PER * n : PER * (n + 1)] for n, v in enumerate((one, two, three)))
+    one, two, three = (
+        lax.optimization_barrier(v + cross[PER * n : PER * (n + 1)]) for n, v in enumerate((one, two, three))
+    )
     two = send(two, back_perm(UP))
     three = send(three, back_perm(RIGHT))
     return [own, three, send(four + five, back_perm(LEFT)), send(one + two, back_perm(UP))]
@@ -528,31 +538,25 @@
     return (value + near[0]) + (near[1] + from_behind(2))
 
 
-def sum_over_all(value):
-    core = lax.axis_index("gy_2")
+def sum_over_all(keep, give):
     swap = [(0, 1), (1, 0)]
-    half = value.shape[0] // 2
-    low, high = value[:half], value[half:]
-    mine = jnp.where(core == 0, low, high) + lax.ppermute(jnp.where(core == 0, high, low), "gy_2", swap)
+    keep = keep + lax.ppermute(give, "gy_2", swap)
     for axis in ("gx", "gy_0", "gy_1"):
-        mine = axis_sum(mine, axis)
-    other = lax.ppermute(mine, "gy_2", swap)
-    return jnp.concatenate([jnp.where(core == 0, mine, other), jnp.where(core == 0, other, mine)])
+        keep = axis_sum(keep, axis)
+    return keep, lax.ppermute(keep, "gy_2", swap)
 
 
 def local(patches, start_frames, pair_ends, margin_blocks):
     me = lax.axis_index(GY).astype(jnp.int32)
     base = lax.axis_index("gx").astype(jnp.int32) * (DEVS * PER)
 
-    def hop(values, steps):
-        out = [None] * PER
-        for p in reversed(range(PER)):
-            out[p] = send(values[p], step_perm(steps) if steps else SIBLING)
-        return out
-
-    both = [patches[p] for p in range(PER)]
-    four = hop(both, LEFT)
-    one = hop(both, UP)
+    def move(value, steps=None):
+        return send(value, step_perm(steps) if steps else SIBLING)
+
+    upper = patches[1]
+    four_1, one_1 = move(upper, LEFT), move(upper, UP)
+    lower = lax.optimization_barrier(patches)[0]
+    four_0, one_0 = move(lower, LEFT), move(lower, UP)
     info, count = make_index(
         jnp.stack([me, base]),
         jnp.asarray(meeting_table()),
@@ -561,24 +565,27 @@
     )
     frames, low = make_start(start_frames)
     lows = spread_frames(low)
-    five = hop(four, LEFT)
-    two = hop(one, UP)
-    arrays = [patches, *one, *four, *hop(one, None)]
+    five_1, two_1 = move(four_1, LEFT), move(one_1, UP)
+    five_0, two_0 = move(four_0, LEFT), move(one_0, UP)
+    three_0 = move(lower, RIGHT)
+    arrays = [patches, one_0, one_1, four_0, four_1, move(one_0), move(one_1)]
     rot = make_rotations(info, count, arrays, LAYOUT, 0, BATCH)
-    three_0 = send(both[0], step_perm(RIGHT))
-    three_1 = send(five[1], step_perm(LEFT))
-    three = [three_0, three_1]
-    arrays += [*two, *five, *hop(two, None)]
+    three_1 = move(five_1, LEFT)
+    arrays += [two_1, five_0, five_1, three_0, move(two_1), move(three_0)]
     rot = make_rotations(info, count, arrays, LAYOUT, 1, BATCH, rot)
-    arrays += [*three, *hop(three, None)]
-    rot = make_rotations(info, count, arrays, LAYOUT, 2, 3, rot)
+    arrays += [two_0, three_1, move(two_0), move(three_1)]
+    rot = make_rotations(info, count, arrays, LAYOUT, 2, BATCH, rot)
+    core = lax.axis_index("gy_2").astype(jnp.int32).reshape(1)
     for sweep in range(SWEEPS):
         if sweep:
             lows = spread_frames(low)
         back = bring_back(make_estimates(info, count, rot, lows))
-        frames, low, frame_sum = make_update(frames, back)
-    total = sum_over_all(frame_sum)
-    aligned, final_frames = make_final(total, frames, patches)
+        if sweep < SWEEPS - 1:
+            frames, low = make_update(frames, back)
+        else:
+            frames, keep, give = make_update(frames, back, core)
+    keep, other = sum_over_all(keep, give)
+    aligned, final_frames, total = make_final(core, keep, other, frames, patches)
     return aligned, final_frames, total
 
 

time: 388 us -> 384 us (0.990)
    ppermute x44, starting transfers between devices: 80.7 us -> 72.8 us  [send(): return lax.ppermute(value, GY, perm)]
    ppermute x9, starting transfers between devices: 10 us -> 16.6 us  [from_behind(): lax.ppermute(value, axis, [(i, (i + hops) % size) for i in range(size)])]
  transfers between devices with their start and end apart: 55 -> 55, of which waited for: 32 -> 33; matrix products, arithmetic and copies ran while one was open for 2% -> 2% of each run, Pallas kernels for 15% -> 16%
where the time goes in v3:
time: 384 us; the launch traced here: 383 us
  waiting for transfers between devices  172 us (45%)
  Pallas kernels  103 us (27%)
  starting transfers between devices  91.8 us (24%)
  local copies, waits for them, and re-layouts  9.35 us (2%)
  other arithmetic  5.15 us (1%)
    ppermute x44, waiting for transfers between devices, send(): return lax.ppermute(value, GY, perm)  152 us
    ppermute x44, starting transfers between devices, send(): return lax.ppermute(value, GY, perm)  72.8 us
    pallas_call x3, Pallas kernels, make_rotations(): pl.pallas_call(functools.partial(rotation_kernel, layout, ready, size), i...  38.3 us
    ppermute x9, waiting for transfers between devices, from_behind(): lax.ppermute(value, axis, [(i, (i + hops) % size) for i in range(size)])  17.9 us
    ppermute x9, starting transfers between devices, from_behind(): lax.ppermute(value, axis, [(i, (i + hops) % size) for i in range(size)])  16.6 us
    pallas_call x2, Pallas kernels, make_update(): pl.pallas_call(update_kernel, in_specs=[SM] + [VM] * (1 + len(parts)), ou...  16.2 us
    pallas_call x2, Pallas kernels, make_estimates(): pl.pallas_call(estimate_kernel, in_specs=[SM, SM, HBM] + [HBM] * SLOTS, o...  16 us
    pallas_call x1, Pallas kernels, make_index(): pl.pallas_call(index_kernel, in_specs=[SM] * 4, out_specs=[SM] * 2, out_s...  14.4 us
  transfers between devices with their start and end apart: 55, of which 33 were waited for; matrix products, arithmetic and copies ran while one was open for 2% of the time, Pallas kernels for 16%

profile of v3, /device:TPU:1, one launch (start us, length us, event | category | flops | bytes accessed | tf_op | source)
XLA Modules:
  0.0 382.5 jit_solution(17643381823535155419)
XLA Ops:
  0.6 3.2 slice_bitcast_fusion.1
  3.8 4.6 %collective-permute-start.3 = (bf16[4096,256]{1,0:T(8,128)(2,1)}, bf16[4096,256]{1,0:T(8,128)(2,1)S(1)}, u32[]{:S(2)}, u32[]{:S(2)}) collective-permute-start(bf16[4096,256]{1,0:T(8,128)(2,1)} %slice_bitcast_fusion.1), channel_id=1, source_target_pairs={{0,6},{1,25},{2,0},{3,27},{4,2},{5,29},{6,4},{7,31},{8,14},{9,1},{... | collective-permute-start | bytes 6291464 | tf_op jit(solution)/shard_map/ppermute | solution.py:501
  8.4 7.4 %start_frames.1 = (f32[2,256,256]{2,1,0:T(8,128)}, bf16[2,256,256]{2,1,0:T(8,128)(2,1)}) custom-call(f32[2,256,256]{2,1,0:T(8,128)} %start_ref.1), custom_call_target="tpu_custom_call" | custom-call | tf_op jit(solution)/shard_map/start_frames/pallas_call | solution.py:298
  18.5 4.3 %collective-permute-done.16.refs_1_ = bf16[2,256,256]{2,1,0:T(8,128)(2,1)S(1)} collective-permute-done((bf16[2,256,256]{2,1,0:T(8,128)(2,1)}, bf16[2,256,256]{2,1,0:T(8,128)(2,1)S(1)}, u32[]{:S(2)}, u32[]{:S(2)}) %collective-permute-start.16) | collective-permute-done | bytes 262176 | tf_op jit(solution)/shard_map/ppermute | solution.py:501
  23.7 2.2 collective-permute-start
  25.8 8.7 %collective-permute-done.19.refs_4_ = bf16[2,256,256]{2,1,0:T(8,128)(2,1)S(1)} collective-permute-done((bf16[2,256,256]{2,1,0:T(8,128)(2,1)}, bf16[2,256,256]{2,1,0:T(8,128)(2,1)S(1)}, u32[]{:S(2)}, u32[]{:S(2)}) %collective-permute-start.19) | collective-permute-done | bytes 262176 | tf_op jit(solution)/shard_map/ppermute | solution.py:501
  35.7 3.0 collective-permute-start.2
  38.8 2.7 collective-permute-start.8
  41.4 19.3 %collective-permute-done.refs_1_ = bf16[4096,256]{1,0:T(8,128)(2,1)S(1)} collective-permute-done((bf16[4096,256]{1,0:T(8,128)(2,1)S(1)}, bf16[4096,256]{1,0:T(8,128)(2,1)S(1)}, u32[]{:S(2)}, u32[]{:S(2)}) %collective-permute-start) | collective-permute-done | bytes 2097184 | tf_op jit(solution)/shard_map/ppermute | solution.py:501
  60.7 9.3 %collective-permute-start.4 = (bf16[4096,256]{1,0:T(8,128)(2,1)S(1)}, bf16[4096,256]{1,0:T(8,128)(2,1)S(1)}, u32[]{:S(2)}, u32[]{:S(2)}) collective-permute-start(bf16[4096,256]{1,0:T(8,128)(2,1)S(1)} %collective-permute-done.refs_1_), channel_id=1, source_target_pairs={{0,1},{1,0},{2,3},{3,2},{4,5},{5,4},{6,7},{7,6},{8,9},{9,8},{10,11... | collective-permute-start | bytes 6291464 | tf_op jit(solution)/shard_map/ppermute | solution.py:501
  70.0 27.6 %collective-permute-done.1.refs_2_ = bf16[4096,256]{1,0:T(8,128)(2,1)S(1)} collective-permute-done((bf16[4096,256]{1,0:T(8,128)(2,1)}, bf16[4096,256]{1,0:T(8,128)(2,1)S(1)}, u32[]{:S(2)}, u32[]{:S(2)}) %collective-permute-start.1) | collective-permute-done | bytes 2097184 | tf_op jit(solution)/shard_map/ppermute | solution.py:501
  97.6 3.9 %collective-permute-start.5 = (bf16[4096,256]{1,0:T(8,128)(2,1)S(1)}, bf16[4096,256]{1,0:T(8,128)(2,1)S(1)}, u32[]{:S(2)}, u32[]{:S(2)}) collective-permute-start(bf16[4096,256]{1,0:T(8,128)(2,1)S(1)} %collective-permute-done.1.refs_2_), channel_id=1, source_target_pairs={{0,1},{1,0},{2,3},{3,2},{4,5},{5,4},{6,7},{7,6},{8,9},{9,8},{10,11... | collective-permute-start | bytes 6291464 | tf_op jit(solution)/shard_map/ppermute | solution.py:501
  102.2 3.1 collective-permute-done.5.refs_6_
  105.7 22.2 %collective-permute-done.6.refs_7_ = bf16[4096,256]{1,0:T(8,128)(2,1)S(1)} collective-permute-done((bf16[4096,256]{1,0:T(8,128)(2,1)S(1)}, bf16[4096,256]{1,0:T(8,128)(2,1)S(1)}, u32[]{:S(2)}, u32[]{:S(2)}) %collective-permute-start.6) | collective-permute-done | bytes 2097184 | tf_op jit(solution)/shard_map/ppermute | solution.py:501
  128.8 21.5 %collective-permute-done.12.refs_13_ = bf16[4096,256]{1,0:T(8,128)(2,1)S(1)} collective-permute-done((bf16[4096,256]{1,0:T(8,128)(2,1)S(1)}, bf16[4096,256]{1,0:T(8,128)(2,1)S(1)}, u32[]{:S(2)}, u32[]{:S(2)}) %collective-permute-start.12) | collective-permute-done | bytes 2097184 | tf_op jit(solution)/shard_map/ppermute | solution.py:501
  159.1 14.4 %pair_index.1 = (s32[4320]{0:T(1024)}, s32[3]{0:T(128)}) custom-call(s32[2]{0:T(128)} %pad_add_fusion.me_ref, s32[12288]{0:T(1024)} %constant.25.clone.table_ref, s32[512]{0:T(512)} %reshape.16.ends_ref, s32[2048]{0:T(1024)} %reshape.17.blocks_ref), custom_call_target="tpu_custom_call" | custom-call | tf_op jit(solution)/shard_map/pair_index/pallas_call | solution.py:188
  173.4 12.2 %shard_map.76.refs_13_ = f32[148,256,256]{2,1,0:T(8,128)} custom-call(s32[4320]{0:T(1024)} %get-tuple-element.27.info_ref, s32[3]{0:T(128)} %get-tuple-element.28.count_ref, bf16[2,4096,256]{2,1,0:T(8,128)(2,1)} %patch_ref.1, bf16[4096,256]{1,0:T(8,128)(2,1)} %copy-done.2, bf16[4096,256]{1,0:T(8,128)(2,1)} %copy-done.3, bf16[4096,256]{1,0:T(8,128)(2,1)} %copy-done.4, ...), custom_call_target="tpu_custom_call" | custom-call | tf_op jit(solution)/shard_map/pallas_call | solution.py:273
  185.7 12.9 %shard_map.77.refs_17_ = f32[148,256,256]{2,1,0:T(8,128)} custom-call(s32[4320]{0:T(1024)} %get-tuple-element.27.info_ref, s32[3]{0:T(128)} %get-tuple-element.28.count_ref, bf16[2,4096,256]{2,1,0:T(8,128)(2,1)} %patch_ref.1, bf16[4096,256]{1,0:T(8,128)(2,1)} %copy-done.2, bf16[4096,256]{1,0:T(8,128)(2,1)} %copy-done.3, ...), custom_call_target="tpu_custom_call", output_to_operand_aliasing={{}: (15, {})} | custom-call | tf_op jit(solution)/shard_map/pallas_call | solution.py:273
  198.6 13.2 %shard_map.78.rot_ref = f32[148,256,256]{2,1,0:T(8,128)} custom-call(s32[4320]{0:T(1024)} %get-tuple-element.27.info_ref, s32[3]{0:T(128)} %get-tuple-element.28.count_ref, bf16[2,4096,256]{2,1,0:T(8,128)(2,1)} %patch_ref.1, bf16[4096,256]{1,0:T(8,128)(2,1)} %copy-done.2, bf16[4096,256]{1,0:T(8,128)(2,1)} %copy-done.3, ...), custom_call_target="tpu_custom_call", output_to_operand_aliasing={{}: (19, {})} | custom-call | tf_op jit(solution)/shard_map/pallas_call | solution.py:273
  211.9 8.0 %estimates.2 = (f32[2,256,256]{2,1,0:T(8,128)}, f32[2,256,256]{2,1,0:T(8,128)}, f32[2,256,256]{2,1,0:T(8,128)}, f32[2,256,256]{2,1,0:T(8,128)}, f32[2,256,256]{2...) custom-call(s32[4320]{0:T(1024)} %get-tuple-element.27.info_ref, s32[3]{0:T(128)} %get-tuple-element.28.count_ref, ...), custom_call_target="tpu_custom_call" | custom-call | tf_op jit(solution)/shard_map/estimates/pallas_call | solution.py:384
  219.9 11.1 %collective-permute-start.24 = (f32[6,256,256]{2,1,0:T(8,128)}, f32[6,256,256]{2,1,0:T(8,128)S(1)}, u32[]{:S(2)}, u32[]{:S(2)}) collective-permute-start(f32[6,256,256]{2,1,0:T(8,128)} %get-tuple-element.32), channel_id=1, source_target_pairs={{0,1},{1,0},{2,3},{3,2},{4,5},{5,4},{6,7},{7,6},{8,9},{9,8},{10,11... | collective-permute-start | bytes 4718600 | tf_op jit(solution)/shard_map/ppermute | solution.py:501
  231.0 3.2 collective-permute-done.24
  235.9 4.8 %collective-permute-done.26 = f32[2,256,256]{2,1,0:T(8,128)S(1)} collective-permute-done((f32[2,256,256]{2,1,0:T(8,128)}, f32[2,256,256]{2,1,0:T(8,128)S(1)}, u32[]{:S(2)}, u32[]{:S(2)}) %collective-permute-start.26) | collective-permute-done | bytes 524320 | tf_op jit(solution)/shard_map/ppermute | solution.py:501
  240.9 2.7 collective-permute-start.25
  245.5 4.9 %collective-permute-done.27.refs_2_ = f32[2,256,256]{2,1,0:T(8,128)S(1)} collective-permute-done((f32[2,256,256]{2,1,0:T(8,128)S(1)}, f32[2,256,256]{2,1,0:T(8,128)S(1)}, u32[]{:S(2)}, u32[]{:S(2)}) %collective-permute-start.27) | collective-permute-done | bytes 524320 | tf_op jit(solution)/shard_map/ppermute | solution.py:501
  251.4 5.6 %collective-permute-done.29.refs_3_ = f32[2,256,256]{2,1,0:T(8,128)S(1)} collective-permute-done((f32[2,256,256]{2,1,0:T(8,128)S(1)}, f32[2,256,256]{2,1,0:T(8,128)S(1)}, u32[]{:S(2)}, u32[]{:S(2)}) %collective-permute-start.29) | collective-permute-done | bytes 524320 | tf_op jit(solution)/shard_map/ppermute | solution.py:501
  257.8 8.1 %update_frames.2 = (f32[2,256,256]{2,1,0:T(8,128)}, bf16[2,256,256]{2,1,0:T(8,128)(2,1)}) custom-call(s32[1]{0:T(128)} %constant.9.clone.1.core_ref, f32[2,256,256]{2,1,0:T(8,128)} %get-tuple-element.26.frame_ref, f32[2,256,256]{2,1,0:T(8,128)} %get-tuple-element.30.refs_0_, f32[2,256,256]{2,1,0:T(8,128)} %copy-done.20, f32[2,256,256]{2,1,0:T(8,128)} %copy-done.18, ...), custom_call_target="tpu_custom_call" | custom-call | tf_op jit(solution)/shard_map/update_frames/pallas_call | solution.py:423
  267.3 5.9 %collective-permute-done.30.refs_1_ = bf16[2,256,256]{2,1,0:T(8,128)(2,1)S(1)} collective-permute-done((bf16[2,256,256]{2,1,0:T(8,128)(2,1)}, bf16[2,256,256]{2,1,0:T(8,128)(2,1)S(1)}, u32[]{:S(2)}, u32[]{:S(2)}) %collective-permute-start.30) | collective-permute-done | bytes 262176 | tf_op jit(solution)/shard_map/ppermute | solution.py:501
  273.2 2.9 collective-permute-start.35
  276.1 3.0 collective-permute-start.34
  280.5 3.2 collective-permute-start.36
  285.6 8.0 %estimates.3 = (f32[2,256,256]{2,1,0:T(8,128)}, f32[2,256,256]{2,1,0:T(8,128)}, f32[2,256,256]{2,1,0:T(8,128)}, f32[2,256,256]{2,1,0:T(8,128)}, f32[2,256,256]{2...) custom-call(s32[4320]{0:T(1024)} %get-tuple-element.27.info_ref, s32[3]{0:T(128)} %get-tuple-element.28.count_ref, ...), custom_call_target="tpu_custom_call" | custom-call | tf_op jit(solution)/shard_map/estimates/pallas_call | solution.py:384
  293.6 2.1 collective-permute-start.38
  295.7 3.2 collective-permute-done.38
  300.6 3.1 collective-permute-start.42
  305.6 2.7 collective-permute-start.39
  309.9 3.2 collective-permute-start.43
  313.1 2.0 collective-permute-done.41.refs_2_
  315.9 5.9 %collective-permute-done.43.refs_3_ = f32[2,256,256]{2,1,0:T(8,128)S(1)} collective-permute-done((f32[2,256,256]{2,1,0:T(8,128)S(1)}, f32[2,256,256]{2,1,0:T(8,128)S(1)}, u32[]{:S(2)}, u32[]{:S(2)}) %collective-permute-start.43) | collective-permute-done | bytes 524320 | tf_op jit(solution)/shard_map/ppermute | solution.py:501
  322.6 8.1 %update_frames.3 = (f32[2,256,256]{2,1,0:T(8,128)}, f32[128,256]{1,0:T(8,128)}, f32[128,256]{1,0:T(8,128)}) custom-call(s32[1]{0:T(128)} %bitcast.core_ref, f32[2,256,256]{2,1,0:T(8,128)} %get-tuple-element.37.frame_ref, f32[2,256,256]{2,1,0:T(8,128)} %get-tuple-element.39.refs_0_, f32[2,256,256]{2,1,0:T(8,128)} %copy-done.21, f32[2,256,256]{2,1,0:T(8,128)} %copy-done.19, ...), custom_call_target="tpu_custom_call" | custom-call | tf_op jit(solution)/shard_map/update_frames/pallas_call | solution.py:423
  333.2 8.1 %collective-permute-start.46 = (f32[128,256]{1,0:T(8,128)S(1)}, f32[128,256]{1,0:T(8,128)S(1)}, u32[]{:S(2)}, u32[]{:S(2)}) collective-permute-start(f32[128,256]{1,0:T(8,128)S(1)} %add.78), channel_id=1, source_target_pairs={{0,96},{32,0},{64,32},{96,64},{1,97},{33,1},{65,33},{97,65},{2,98}... | collective-permute-start | bytes 393224 | tf_op jit(solution)/shard_map/ppermute | solution.py:535
  342.4 2.5 collective-permute-done.45
  346.7 2.0 collective-permute-done.47
  353.8 4.6 %collective-permute-done.50 = f32[128,256]{1,0:T(8,128)S(1)} collective-permute-done((f32[128,256]{1,0:T(8,128)S(1)}, f32[128,256]{1,0:T(8,128)S(1)}, u32[]{:S(2)}, u32[]{:S(2)}) %collective-permute-start.50) | collective-permute-done | bytes 131104 | tf_op jit(solution)/shard_map/ppermute | solution.py:535
  361.3 2.2 collective-permute-done.51
  364.7 3.0 collective-permute-done.53
  367.8 2.3 collective-permute-start.54
  371.7 10.6 %aligned_rows.1 = (bf16[2,4096,256]{2,1,0:T(8,128)(2,1)}, f32[2,256,256]{2,1,0:T(8,128)}, f32[256,256]{1,0:T(8,128)}) custom-call(s32[1]{0:T(128)} %bitcast.core_ref, f32[128,256]{1,0:T(8,128)} %copy-done.17, f32[128,256]{1,0:T(8,128)} %copy-done.36, f32[2,256,256]{2,1,0:T(8,128)} %get-tuple-element.48.frame_ref, bf16[2,4096,256]{2,1,0:T(8,128)(2,1)} %patch_ref.1), custom_call_target="tpu_custom_call" | custom-call | tf_op jit(solution)/shard_map/aligned_rows/pallas_call | solution.py:478
  (167 shorter events, 48.8 us)
Async XLA Ops:
  3.8 34.9 %collective-permute-start.3 = (bf16[4096,256]{1,0:T(8,128)(2,1)}, bf16[4096,256]{1,0:T(8,128)(2,1)S(1)}, u32[]{:S(2)}, u32[]{:S(2)}) collective-permute-start(bf16[4096,256]{1,0:T(8,128)(2,1)} %slice_bitcast_fusion.1), channel_id=1, source_target_pairs={{0,6},{1,25},{2,0},{3,27},{4,2},{5,29},{6,4},{7,31},{8,14},{9,1},{... | collective-permute-start | bytes 6291464 | tf_op jit(solution)/shard_map/ppermute | solution.py:501
  15.8 6.9 %collective-permute-start.16 = (bf16[2,256,256]{2,1,0:T(8,128)(2,1)}, bf16[2,256,256]{2,1,0:T(8,128)(2,1)S(1)}, u32[]{:S(2)}, u32[]{:S(2)}) collective-permute-start(bf16[2,256,256]{2,1,0:T(8,128)(2,1)} %get-tuple-element.29.refs_0_), channel_id=1, source_target_pairs={{0,8},{1,3},{2,10},{3,5},{4,12},{5,7},{6,14},{7,1},{8,16},{9,11},{... | collective-permute-start | bytes 786440 | tf_op jit(solution)/shard_map/ppermute | solution.py:501
  17.0 17.5 %collective-permute-start.19 = (bf16[2,256,256]{2,1,0:T(8,128)(2,1)}, bf16[2,256,256]{2,1,0:T(8,128)(2,1)S(1)}, u32[]{:S(2)}, u32[]{:S(2)}) collective-permute-start(bf16[2,256,256]{2,1,0:T(8,128)(2,1)} %get-tuple-element.29.refs_0_), channel_id=1, source_target_pairs={{0,6},{1,25},{2,0},{3,27},{4,2},{5,29},{6,4},{7,31},{8,14},{9,1},{... | collective-permute-start | bytes 786440 | tf_op jit(solution)/shard_map/ppermute | solution.py:501
  17.1 18.6 %collective-permute-start.18 = (bf16[2,256,256]{2,1,0:T(8,128)(2,1)}, bf16[2,256,256]{2,1,0:T(8,128)(2,1)S(1)}, u32[]{:S(2)}, u32[]{:S(2)}) collective-permute-start(bf16[2,256,256]{2,1,0:T(8,128)(2,1)} %get-tuple-element.29.refs_0_), channel_id=1, source_target_pairs={{0,2},{1,9},{2,4},{3,11},{4,6},{5,13},{6,0},{7,15},{8,10},{9,17},{... | collective-permute-start | bytes 786440 | tf_op jit(solution)/shard_map/ppermute | solution.py:501
  22.8 16.0 %collective-permute-start.17 = (bf16[2,256,256]{2,1,0:T(8,128)(2,1)S(1)}, bf16[2,256,256]{2,1,0:T(8,128)(2,1)S(1)}, u32[]{:S(2)}, u32[]{:S(2)}) collective-permute-start(bf16[2,256,256]{2,1,0:T(8,128)(2,1)S(1)} %collective-permute-done.16.refs_1_), channel_id=1, source_target_pairs={{0,8},{1,3},{2,10},{3,5},{4,12},{5,7},{6,14},{7,1},{8,16},{9,11},{... | collective-permute-start | bytes 786440 | tf_op jit(solution)/shard_map/ppermute | solution.py:501
  23.7 37.1 %collective-permute-start = (bf16[4096,256]{1,0:T(8,128)(2,1)S(1)}, bf16[4096,256]{1,0:T(8,128)(2,1)S(1)}, u32[]{:S(2)}, u32[]{:S(2)}) collective-permute-start(bf16[4096,256]{1,0:T(8,128)(2,1)S(1)} %slice_bitcast_fusion), channel_id=1, source_target_pairs={{0,8},{1,3},{2,10},{3,5},{4,12},{5,7},{6,14},{7,1},{8,16},{9,11},{... | collective-permute-start | bytes 6291464 | tf_op jit(solution)/shard_map/ppermute | solution.py:501
  34.5 63.1 %collective-permute-start.1 = (bf16[4096,256]{1,0:T(8,128)(2,1)}, bf16[4096,256]{1,0:T(8,128)(2,1)S(1)}, u32[]{:S(2)}, u32[]{:S(2)}) collective-permute-start(bf16[4096,256]{1,0:T(8,128)(2,1)} %slice_bitcast_fusion.1), channel_id=1, source_target_pairs={{0,8},{1,3},{2,10},{3,5},{4,12},{5,7},{6,14},{7,1},{8,16},{9,11},{... | collective-permute-start | bytes 6291464 | tf_op jit(solution)/shard_map/ppermute | solution.py:501
  35.7 65.8 %collective-permute-start.2 = (bf16[4096,256]{1,0:T(8,128)(2,1)S(1)}, bf16[4096,256]{1,0:T(8,128)(2,1)S(1)}, u32[]{:S(2)}, u32[]{:S(2)}) collective-permute-start(bf16[4096,256]{1,0:T(8,128)(2,1)S(1)} %slice_bitcast_fusion), channel_id=1, source_target_pairs={{0,6},{1,25},{2,0},{3,27},{4,2},{5,29},{6,4},{7,31},{8,14},{9,1},{... | collective-permute-start | bytes 6291464 | tf_op jit(solution)/shard_map/ppermute | solution.py:501
  38.7 62.8 %collective-permute-start.9 = (bf16[4096,256]{1,0:T(8,128)(2,1)S(1)}, bf16[4096,256]{1,0:T(8,128)(2,1)S(1)}, u32[]{:S(2)}, u32[]{:S(2)}) collective-permute-start(bf16[4096,256]{1,0:T(8,128)(2,1)S(1)} %slice_bitcast_fusion), channel_id=1, source_target_pairs={{0,2},{1,9},{2,4},{3,11},{4,6},{5,13},{6,0},{7,15},{8,10},{9,17},{... | collective-permute-start | bytes 6291464 | tf_op jit(solution)/shard_map/ppermute | solution.py:501
  38.8 62.8 %collective-permute-start.8 = (bf16[4096,256]{1,0:T(8,128)(2,1)S(1)}, bf16[4096,256]{1,0:T(8,128)(2,1)S(1)}, u32[]{:S(2)}, u32[]{:S(2)}) collective-permute-start(bf16[4096,256]{1,0:T(8,128)(2,1)S(1)} %collective-permute-done.3.refs_4_), channel_id=1, source_target_pairs={{0,6},{1,25},{2,0},{3,27},{4,2},{5,29},{6,4},{7,31},{8,14},{9,1},{... | collective-permute-start | bytes 6291464 | tf_op jit(solution)/shard_map/ppermute | solution.py:501
  60.7 41.4 %collective-permute-start.4 = (bf16[4096,256]{1,0:T(8,128)(2,1)S(1)}, bf16[4096,256]{1,0:T(8,128)(2,1)S(1)}, u32[]{:S(2)}, u32[]{:S(2)}) collective-permute-start(bf16[4096,256]{1,0:T(8,128)(2,1)S(1)} %collective-permute-done.refs_1_), channel_id=1, source_target_pairs={{0,1},{1,0},{2,3},{3,2},{4,5},{5,4},{6,7},{7,6},{8,9},{9,8},{10,11... | collective-permute-start | bytes 6291464 | tf_op jit(solution)/shard_map/ppermute | solution.py:501
  97.6 7.7 %collective-permute-start.5 = (bf16[4096,256]{1,0:T(8,128)(2,1)S(1)}, bf16[4096,256]{1,0:T(8,128)(2,1)S(1)}, u32[]{:S(2)}, u32[]{:S(2)}) collective-permute-start(bf16[4096,256]{1,0:T(8,128)(2,1)S(1)} %collective-permute-done.1.refs_2_), channel_id=1, source_target_pairs={{0,1},{1,0},{2,3},{3,2},{4,5},{5,4},{6,7},{7,6},{8,9},{9,8},{10,11... | collective-permute-start | bytes 6291464 | tf_op jit(solution)/shard_map/ppermute | solution.py:501
  101.5 26.4 %collective-permute-start.6 = (bf16[4096,256]{1,0:T(8,128)(2,1)S(1)}, bf16[4096,256]{1,0:T(8,128)(2,1)S(1)}, u32[]{:S(2)}, u32[]{:S(2)}) collective-permute-start(bf16[4096,256]{1,0:T(8,128)(2,1)S(1)} %collective-permute-done.1.refs_2_), channel_id=1, source_target_pairs={{0,8},{1,3},{2,10},{3,5},{4,12},{5,7},{6,14},{7,1},{8,16},{9,11},{... | collective-permute-start | bytes 6291464 | tf_op jit(solution)/shard_map/ppermute | solution.py:501
  101.5 48.8 %collective-permute-start.12 = (bf16[4096,256]{1,0:T(8,128)(2,1)S(1)}, bf16[4096,256]{1,0:T(8,128)(2,1)S(1)}, u32[]{:S(2)}, u32[]{:S(2)}) collective-permute-start(bf16[4096,256]{1,0:T(8,128)(2,1)S(1)} %collective-permute-done.refs_1_), channel_id=1, source_target_pairs={{0,8},{1,3},{2,10},{3,5},{4,12},{5,7},{6,14},{7,1},{8,16},{9,11},{... | collective-permute-start | bytes 6291464 | tf_op jit(solution)/shard_map/ppermute | solution.py:501
  101.6 49.7 %collective-permute-start.13 = (bf16[4096,256]{1,0:T(8,128)(2,1)S(1)}, bf16[4096,256]{1,0:T(8,128)(2,1)}, u32[]{:S(2)}, u32[]{:S(2)}) collective-permute-start(bf16[4096,256]{1,0:T(8,128)(2,1)S(1)} %collective-permute-done.8.refs_9_), channel_id=1, source_target_pairs={{0,6},{1,25},{2,0},{3,27},{4,2},{5,29},{6,4},{7,31},{8,14},{9,1},{... | collective-permute-start | bytes 6291464 | tf_op jit(solution)/shard_map/ppermute | solution.py:501
  102.1 49.3 %collective-permute-start.7 = (bf16[4096,256]{1,0:T(8,128)(2,1)S(1)}, bf16[4096,256]{1,0:T(8,128)(2,1)S(1)}, u32[]{:S(2)}, u32[]{:S(2)}) collective-permute-start(bf16[4096,256]{1,0:T(8,128)(2,1)S(1)} %collective-permute-done.2.refs_3_), channel_id=1, source_target_pairs={{0,6},{1,25},{2,0},{3,27},{4,2},{5,29},{6,4},{7,31},{8,14},{9,1},{... | collective-permute-start | bytes 6291464 | tf_op jit(solution)/shard_map/ppermute | solution.py:501
  105.3 46.6 %collective-permute-start.11 = (bf16[4096,256]{1,0:T(8,128)(2,1)S(1)}, bf16[4096,256]{1,0:T(8,128)(2,1)S(1)}, u32[]{:S(2)}, u32[]{:S(2)}) collective-permute-start(bf16[4096,256]{1,0:T(8,128)(2,1)S(1)} %collective-permute-done.9.refs_10_), channel_id=1, source_target_pairs={{0,1},{1,0},{2,3},{3,2},{4,5},{5,4},{6,7},{7,6},{8,9},{9,8},{10,11... | collective-permute-start | bytes 6291464 | tf_op jit(solution)/shard_map/ppermute | solution.py:501
  127.9 25.5 %collective-permute-start.10 = (bf16[4096,256]{1,0:T(8,128)(2,1)S(1)}, bf16[4096,256]{1,0:T(8,128)(2,1)S(1)}, u32[]{:S(2)}, u32[]{:S(2)}) collective-permute-start(bf16[4096,256]{1,0:T(8,128)(2,1)S(1)} %collective-permute-done.6.refs_7_), channel_id=1, source_target_pairs={{0,1},{1,0},{2,3},{3,2},{4,5},{5,4},{6,7},{7,6},{8,9},{9,8},{10,11... | collective-permute-start | bytes 6291464 | tf_op jit(solution)/shard_map/ppermute | solution.py:501
  151.3 47.3 %collective-permute-start.15 = (bf16[4096,256]{1,0:T(8,128)(2,1)}, bf16[4096,256]{1,0:T(8,128)(2,1)}, u32[]{:S(2)}, u32[]{:S(2)}) collective-permute-start(bf16[4096,256]{1,0:T(8,128)(2,1)} %collective-permute-done.13.refs_14_), channel_id=1, source_target_pairs={{0,1},{1,0},{2,3},{3,2},{4,5},{5,4},{6,7},{7,6},{8,9},{9,8},{10,11... | collective-permute-start | bytes 6291464 | tf_op jit(solution)/shard_map/ppermute | solution.py:501
  151.4 60.4 %collective-permute-start.21 = (bf16[2,256,256]{2,1,0:T(8,128)(2,1)S(1)}, bf16[2,256,256]{2,1,0:T(8,128)(2,1)}, u32[]{:S(2)}, u32[]{:S(2)}) collective-permute-start(bf16[2,256,256]{2,1,0:T(8,128)(2,1)S(1)} %collective-permute-done.16.refs_1_), channel_id=1, source_target_pairs={{0,1},{1,0},{2,3},{3,2},{4,5},{5,4},{6,7},{7,6},{8,9},{9,8},{10,11... | collective-permute-start | bytes 786440 | tf_op jit(solution)/shard_map/ppermute | solution.py:501
  151.9 59.9 %collective-permute-start.20 = (bf16[2,256,256]{2,1,0:T(8,128)(2,1)S(1)}, bf16[2,256,256]{2,1,0:T(8,128)(2,1)}, u32[]{:S(2)}, u32[]{:S(2)}) collective-permute-start(bf16[2,256,256]{2,1,0:T(8,128)(2,1)S(1)} %collective-permute-done.19.refs_4_), channel_id=1, source_target_pairs={{0,6},{1,25},{2,0},{3,27},{4,2},{5,29},{6,4},{7,31},{8,14},{9,1},{... | collective-permute-start | bytes 786440 | tf_op jit(solution)/shard_map/ppermute | solution.py:501
  153.4 58.4 %collective-permute-start.23 = (bf16[2,256,256]{2,1,0:T(8,128)(2,1)S(1)}, bf16[2,256,256]{2,1,0:T(8,128)(2,1)}, u32[]{:S(2)}, u32[]{:S(2)}) collective-permute-start(bf16[2,256,256]{2,1,0:T(8,128)(2,1)S(1)} %collective-permute-done.18.refs_3_), channel_id=1, source_target_pairs={{0,1},{1,0},{2,3},{3,2},{4,5},{5,4},{6,7},{7,6},{8,9},{9,8},{10,11... | collective-permute-start | bytes 786440 | tf_op jit(solution)/shard_map/ppermute | solution.py:501
  155.1 56.8 %collective-permute-start.22 = (bf16[2,256,256]{2,1,0:T(8,128)(2,1)S(1)}, bf16[2,256,256]{2,1,0:T(8,128)(2,1)}, u32[]{:S(2)}, u32[]{:S(2)}) collective-permute-start(bf16[2,256,256]{2,1,0:T(8,128)(2,1)S(1)} %collective-permute-done.17.refs_2_), channel_id=1, source_target_pairs={{0,1},{1,0},{2,3},{3,2},{4,5},{5,4},{6,7},{7,6},{8,9},{9,8},{10,11... | collective-permute-start | bytes 786440 | tf_op jit(solution)/shard_map/ppermute | solution.py:501
  219.9 14.3 %collective-permute-start.24 = (f32[6,256,256]{2,1,0:T(8,128)}, f32[6,256,256]{2,1,0:T(8,128)S(1)}, u32[]{:S(2)}, u32[]{:S(2)}) collective-permute-start(f32[6,256,256]{2,1,0:T(8,128)} %get-tuple-element.32), channel_id=1, source_target_pairs={{0,1},{1,0},{2,3},{3,2},{4,5},{5,4},{6,7},{7,6},{8,9},{9,8},{10,11... | collective-permute-start | bytes 4718600 | tf_op jit(solution)/shard_map/ppermute | solution.py:501
  231.0 9.7 %collective-permute-start.26 = (f32[2,256,256]{2,1,0:T(8,128)}, f32[2,256,256]{2,1,0:T(8,128)S(1)}, u32[]{:S(2)}, u32[]{:S(2)}) collective-permute-start(f32[2,256,256]{2,1,0:T(8,128)} %get-tuple-element.34), channel_id=1, source_target_pairs={{6,0},{25,1},{0,2},{27,3},{2,4},{29,5},{4,6},{31,7},{14,8},{1,9},{... | collective-permute-start | bytes 1572872 | tf_op jit(solution)/shard_map/ppermute | solution.py:501
  235.9 8.4 %collective-permute-start.28 = (f32[2,256,256]{2,1,0:T(8,128)S(1)}, f32[2,256,256]{2,1,0:T(8,128)S(1)}, u32[]{:S(2)}, u32[]{:S(2)}) collective-permute-start(f32[2,256,256]{2,1,0:T(8,128)S(1)} %get-tuple-element.52), channel_id=1, source_target_pairs={{8,0},{3,1},{10,2},{5,3},{12,4},{7,5},{14,6},{1,7},{16,8},{11,9},{... | collective-permute-start | bytes 1572872 | tf_op jit(solution)/shard_map/ppermute | solution.py:501
  240.8 9.6 %collective-permute-start.27 = (f32[2,256,256]{2,1,0:T(8,128)S(1)}, f32[2,256,256]{2,1,0:T(8,128)S(1)}, u32[]{:S(2)}, u32[]{:S(2)}) collective-permute-start(f32[2,256,256]{2,1,0:T(8,128)S(1)} %add.69), channel_id=1, source_target_pairs={{6,0},{25,1},{0,2},{27,3},{2,4},{29,5},{4,6},{31,7},{14,8},{1,9},{... | collective-permute-start | bytes 1572872 | tf_op jit(solution)/shard_map/ppermute | solution.py:501
  240.9 10.5 %collective-permute-start.25 = (f32[2,256,256]{2,1,0:T(8,128)S(1)}, f32[2,256,256]{2,1,0:T(8,128)S(1)}, u32[]{:S(2)}, u32[]{:S(2)}) collective-permute-start(f32[2,256,256]{2,1,0:T(8,128)S(1)} %get-tuple-element.54), channel_id=1, source_target_pairs={{2,0},{9,1},{4,2},{11,3},{6,4},{13,5},{0,6},{15,7},{10,8},{17,9},{... | collective-permute-start | bytes 1572872 | tf_op jit(solution)/shard_map/ppermute | solution.py:501
  244.3 12.6 %collective-permute-start.29 = (f32[2,256,256]{2,1,0:T(8,128)S(1)}, f32[2,256,256]{2,1,0:T(8,128)S(1)}, u32[]{:S(2)}, u32[]{:S(2)}) collective-permute-start(f32[2,256,256]{2,1,0:T(8,128)S(1)} %add.72), channel_id=1, source_target_pairs={{8,0},{3,1},{10,2},{5,3},{12,4},{7,5},{14,6},{1,7},{16,8},{11,9},{... | collective-permute-start | bytes 1572872 | tf_op jit(solution)/shard_map/ppermute | solution.py:501
  265.9 7.4 %collective-permute-start.30 = (bf16[2,256,256]{2,1,0:T(8,128)(2,1)}, bf16[2,256,256]{2,1,0:T(8,128)(2,1)S(1)}, u32[]{:S(2)}, u32[]{:S(2)}) collective-permute-start(bf16[2,256,256]{2,1,0:T(8,128)(2,1)} %get-tuple-element.38.refs_0_), channel_id=1, source_target_pairs={{0,8},{1,3},{2,10},{3,5},{4,12},{5,7},{6,14},{7,1},{8,16},{9,11},{... | collective-permute-start | bytes 786440 | tf_op jit(solution)/shard_map/ppermute | solution.py:501
  265.9 10.2 %collective-permute-start.33 = (bf16[2,256,256]{2,1,0:T(8,128)(2,1)}, bf16[2,256,256]{2,1,0:T(8,128)(2,1)S(1)}, u32[]{:S(2)}, u32[]{:S(2)}) collective-permute-start(bf16[2,256,256]{2,1,0:T(8,128)(2,1)} %get-tuple-element.38.refs_0_), channel_id=1, source_target_pairs={{0,6},{1,25},{2,0},{3,27},{4,2},{5,29},{6,4},{7,31},{8,14},{9,1},{... | collective-permute-start | bytes 786440 | tf_op jit(solution)/shard_map/ppermute | solution.py:501
  265.9 13.2 %collective-permute-start.32 = (bf16[2,256,256]{2,1,0:T(8,128)(2,1)}, bf16[2,256,256]{2,1,0:T(8,128)(2,1)S(1)}, u32[]{:S(2)}, u32[]{:S(2)}) collective-permute-start(bf16[2,256,256]{2,1,0:T(8,128)(2,1)} %get-tuple-element.38.refs_0_), channel_id=1, source_target_pairs={{0,2},{1,9},{2,4},{3,11},{4,6},{5,13},{6,0},{7,15},{8,10},{9,17},{... | collective-permute-start | bytes 786440 | tf_op jit(solution)/shard_map/ppermute | solution.py:501
  273.2 7.2 %collective-permute-start.31 = (bf16[2,256,256]{2,1,0:T(8,128)(2,1)S(1)}, bf16[2,256,256]{2,1,0:T(8,128)(2,1)S(1)}, u32[]{:S(2)}, u32[]{:S(2)}) collective-permute-start(bf16[2,256,256]{2,1,0:T(8,128)(2,1)S(1)} %collective-permute-done.30.refs_1_), channel_id=1, source_target_pairs={{0,8},{1,3},{2,10},{3,5},{4,12},{5,7},{6,14},{7,1},{8,16},{9,11},{... | collective-permute-start | bytes 786440 | tf_op jit(solution)/shard_map/ppermute | solution.py:501
  273.2 10.5 %collective-permute-start.35 = (bf16[2,256,256]{2,1,0:T(8,128)(2,1)S(1)}, bf16[2,256,256]{2,1,0:T(8,128)(2,1)S(1)}, u32[]{:S(2)}, u32[]{:S(2)}) collective-permute-start(bf16[2,256,256]{2,1,0:T(8,128)(2,1)S(1)} %collective-permute-done.30.refs_1_), channel_id=1, source_target_pairs={{0,1},{1,0},{2,3},{3,2},{4,5},{5,4},{6,7},{7,6},{8,9},{9,8},{10,11... | collective-permute-start | bytes 786440 | tf_op jit(solution)/shard_map/ppermute | solution.py:501
  276.1 7.6 %collective-permute-start.34 = (bf16[2,256,256]{2,1,0:T(8,128)(2,1)S(1)}, bf16[2,256,256]{2,1,0:T(8,128)(2,1)S(1)}, u32[]{:S(2)}, u32[]{:S(2)}) collective-permute-start(bf16[2,256,256]{2,1,0:T(8,128)(2,1)S(1)} %collective-permute-done.33.refs_4_), channel_id=1, source_target_pairs={{0,6},{1,25},{2,0},{3,27},{4,2},{5,29},{6,4},{7,31},{8,14},{9,1},{... | collective-permute-start | bytes 786440 | tf_op jit(solution)/shard_map/ppermute | solution.py:501
  293.6 5.3 %collective-permute-start.38 = (f32[6,256,256]{2,1,0:T(8,128)}, f32[6,256,256]{2,1,0:T(8,128)S(1)}, u32[]{:S(2)}, u32[]{:S(2)}) collective-permute-start(f32[6,256,256]{2,1,0:T(8,128)} %get-tuple-element.41), channel_id=1, source_target_pairs={{0,1},{1,0},{2,3},{3,2},{4,5},{5,4},{6,7},{7,6},{8,9},{9,8},{10,11... | collective-permute-start | bytes 4718600 | tf_op jit(solution)/shard_map/ppermute | solution.py:501
  295.7 9.7 %collective-permute-start.40 = (f32[2,256,256]{2,1,0:T(8,128)}, f32[2,256,256]{2,1,0:T(8,128)S(1)}, u32[]{:S(2)}, u32[]{:S(2)}) collective-permute-start(f32[2,256,256]{2,1,0:T(8,128)} %get-tuple-element.43), channel_id=1, source_target_pairs={{6,0},{25,1},{0,2},{27,3},{2,4},{29,5},{4,6},{31,7},{14,8},{1,9},{... | collective-permute-start | bytes 1572872 | tf_op jit(solution)/shard_map/ppermute | solution.py:501
  300.6 9.3 %collective-permute-start.42 = (f32[2,256,256]{2,1,0:T(8,128)S(1)}, f32[2,256,256]{2,1,0:T(8,128)S(1)}, u32[]{:S(2)}, u32[]{:S(2)}) collective-permute-start(f32[2,256,256]{2,1,0:T(8,128)S(1)} %get-tuple-element.49), channel_id=1, source_target_pairs={{8,0},{3,1},{10,2},{5,3},{12,4},{7,5},{14,6},{1,7},{16,8},{11,9},{... | collective-permute-start | bytes 1572872 | tf_op jit(solution)/shard_map/ppermute | solution.py:501
  305.5 9.6 %collective-permute-start.41 = (f32[2,256,256]{2,1,0:T(8,128)S(1)}, f32[2,256,256]{2,1,0:T(8,128)S(1)}, u32[]{:S(2)}, u32[]{:S(2)}) collective-permute-start(f32[2,256,256]{2,1,0:T(8,128)S(1)} %add.74), channel_id=1, source_target_pairs={{6,0},{25,1},{0,2},{27,3},{2,4},{29,5},{4,6},{31,7},{14,8},{1,9},{... | collective-permute-start | bytes 1572872 | tf_op jit(solution)/shard_map/ppermute | solution.py:501
  305.6 10.3 %collective-permute-start.39 = (f32[2,256,256]{2,1,0:T(8,128)S(1)}, f32[2,256,256]{2,1,0:T(8,128)S(1)}, u32[]{:S(2)}, u32[]{:S(2)}) collective-permute-start(f32[2,256,256]{2,1,0:T(8,128)S(1)} %get-tuple-element.51), channel_id=1, source_target_pairs={{2,0},{9,1},{4,2},{11,3},{6,4},{13,5},{0,6},{15,7},{10,8},{17,9},{... | collective-permute-start | bytes 1572872 | tf_op jit(solution)/shard_map/ppermute | solution.py:501
  309.9 11.9 %collective-permute-start.43 = (f32[2,256,256]{2,1,0:T(8,128)S(1)}, f32[2,256,256]{2,1,0:T(8,128)S(1)}, u32[]{:S(2)}, u32[]{:S(2)}) collective-permute-start(f32[2,256,256]{2,1,0:T(8,128)S(1)} %add.77), channel_id=1, source_target_pairs={{8,0},{3,1},{10,2},{5,3},{12,4},{7,5},{14,6},{1,7},{16,8},{11,9},{... | collective-permute-start | bytes 1572872 | tf_op jit(solution)/shard_map/ppermute | solution.py:501
  333.2 11.8 %collective-permute-start.45 = (f32[128,256]{1,0:T(8,128)S(1)}, f32[128,256]{1,0:T(8,128)S(1)}, u32[]{:S(2)}, u32[]{:S(2)}) collective-permute-start(f32[128,256]{1,0:T(8,128)S(1)} %add.78), channel_id=1, source_target_pairs={{0,32},{32,64},{64,96},{96,0},{1,33},{33,65},{65,97},{97,1},{2,34}... | collective-permute-start | bytes 393224 | tf_op jit(solution)/shard_map/ppermute | solution.py:535
  333.2 13.4 %collective-permute-start.46 = (f32[128,256]{1,0:T(8,128)S(1)}, f32[128,256]{1,0:T(8,128)S(1)}, u32[]{:S(2)}, u32[]{:S(2)}) collective-permute-start(f32[128,256]{1,0:T(8,128)S(1)} %add.78), channel_id=1, source_target_pairs={{0,96},{32,0},{64,32},{96,64},{1,97},{33,1},{65,33},{97,65},{2,98}... | collective-permute-start | bytes 393224 | tf_op jit(solution)/shard_map/ppermute | solution.py:535
  341.3 7.4 %collective-permute-start.47 = (f32[128,256]{1,0:T(8,128)S(1)}, f32[128,256]{1,0:T(8,128)S(1)}, u32[]{:S(2)}, u32[]{:S(2)}) collective-permute-start(f32[128,256]{1,0:T(8,128)S(1)} %add.78), channel_id=1, source_target_pairs={{0,64},{32,96},{64,0},{96,32},{1,65},{33,97},{65,1},{97,33},{2,66}... | collective-permute-start | bytes 393224 | tf_op jit(solution)/shard_map/ppermute | solution.py:535
  348.7 5.1 %collective-permute-start.48 = (f32[128,256]{1,0:T(8,128)S(1)}, f32[128,256]{1,0:T(8,128)S(1)}, u32[]{:S(2)}, u32[]{:S(2)}) collective-permute-start(f32[128,256]{1,0:T(8,128)S(1)} %add_add_fusion.2), channel_id=1, source_target_pairs={{0,8},{8,16},{16,24},{24,0},{1,9},{9,17},{17,25},{25,1},{2,10},{10... | collective-permute-start | bytes 393224 | tf_op jit(solution)/shard_map/ppermute | solution.py:535
  351.4 7.0 %collective-permute-start.50 = (f32[128,256]{1,0:T(8,128)S(1)}, f32[128,256]{1,0:T(8,128)S(1)}, u32[]{:S(2)}, u32[]{:S(2)}) collective-permute-start(f32[128,256]{1,0:T(8,128)S(1)} %add_add_fusion.2), channel_id=1, source_target_pairs={{0,16},{8,24},{16,0},{24,8},{1,17},{9,25},{17,1},{25,9},{2,18},{10... | collective-permute-start | bytes 393224 | tf_op jit(solution)/shard_map/ppermute | solution.py:535
  359.4 5.4 %collective-permute-start.52 = (f32[128,256]{1,0:T(8,128)S(1)}, f32[128,256]{1,0:T(8,128)S(1)}, u32[]{:S(2)}, u32[]{:S(2)}) collective-permute-start(f32[128,256]{1,0:T(8,128)S(1)} %add_add_fusion.1), channel_id=1, source_target_pairs={{0,6},{2,0},{4,2},{6,4},{1,7},{3,1},{5,3},{7,5},{8,14},{10,8},{12,... | collective-permute-start | bytes 393224 | tf_op jit(solution)/shard_map/ppermute | solution.py:535
  361.2 6.6 %collective-permute-start.53 = (f32[128,256]{1,0:T(8,128)S(1)}, f32[128,256]{1,0:T(8,128)S(1)}, u32[]{:S(2)}, u32[]{:S(2)}) collective-permute-start(f32[128,256]{1,0:T(8,128)S(1)} %add_add_fusion.1), channel_id=1, source_target_pairs={{0,4},{2,6},{4,0},{6,2},{1,5},{3,7},{5,1},{7,3},{8,12},{10,14},{12... | collective-permute-start | bytes 393224 | tf_op jit(solution)/shard_map/ppermute | solution.py:535
  (46 other events, 1503.2 us)

commit v4 on v3

--- a/solution.py
+++ b/solution.py
@@ -17,7 +17,6 @@
 NS_STEPS = 5
 PER = 2
 DEVS = 32
-BATCH = 4
 GY = ("gy_0", "gy_1", "gy_2")
 GX_GY = ("gx", "gy_0", "gy_1", "gy_2")
 F32, BF16 = jnp.float32, jnp.bfloat16
@@ -33,7 +32,7 @@
 CROSS = (1, 2, 3)
 OWN = len(OFFS[0])
 SLOTS = OWN + len(CROSS)
-MAX_PAIRS = -(-(SLOTS * DEVS // 2) // BATCH) * BATCH
+MAX_PAIRS = SLOTS * DEVS // 2
 
 
 def device_at(z, x, c):
@@ -213,39 +212,30 @@
         return ref.at[lines] if part is None else ref.at[part, lines]
 
     def load(batch, buf):
-        def one(i, carry):
+        def one(n, carry):
+            i, e = n >> 1, n & 1
             line = (ready * MAX_PAIRS + jnp.minimum(batch * size + i, count - 1)) * INFO
-            for e in range(2):
-                slot = info_ref[line + e]
-                for s in layout:
-
-                    @pl.when(slot == s)
-                    def _():
-                        for k in range(OVB):
-                            pltpu.make_async_copy(
-                                block_ref(s, info_ref[line + 2 + e * OVB + k]),
-                                rows.at[buf, i, e, pl.ds(k * BLOCK, BLOCK)],
-                                load_sem.at[buf],
-                            ).start()
+            slot = info_ref[line + e]
+            for s in layout:
+
+                @pl.when(slot == s)
+                def _():
+                    for k in range(OVB):
+                        pltpu.make_async_copy(
+                            block_ref(s, info_ref[line + 2 + e * OVB + k]),
+                            rows.at[buf, i, e, pl.ds(k * BLOCK, BLOCK)],
+                            load_sem.at[buf],
+                        ).start()
 
             return carry
 
-        lax.fori_loop(0, size, one, 0)
+        lax.fori_loop(0, 2 * size, one, 0)
 
     def out_copy(batch):
         return pltpu.make_async_copy(outs, rot_ref.at[pl.ds(first + batch * size, size)], out_sem)
 
-    @pl.when(batches > 0)
-    def _():
-        load(0, 0)
-
-    def step(batch, carry):
+    def work(batch):
         buf = batch & 1
-
-        @pl.when(batch + 1 < batches)
-        def _():
-            load(batch + 1, 1 - buf)
-
         pltpu.make_async_copy(rows.at[buf], rows.at[buf], load_sem.at[buf]).wait()
         for i in range(size):
             mats[i] = dot(rows[buf, i, 1], rows[buf, i, 0], 0, 0)
@@ -258,9 +248,19 @@
         for i in range(size):
             outs[i] = mats[i]
         out_copy(batch).start()
+
+    def step(n, carry):
+        @pl.when(n < batches)
+        def _():
+            load(n, n & 1)
+
+        @pl.when(n > 0)
+        def _():
+            work(n - 1)
+
         return carry
 
-    lax.fori_loop(0, batches, step, 0)
+    lax.fori_loop(0, batches + 1, step, 0)
 
     @pl.when(batches > 0)
     def _():
@@ -274,7 +274,7 @@
         functools.partial(rotation_kernel, layout, ready, size),
         in_specs=[SM, SM] + [HBM] * (len(arrays) + len(more)),
         out_specs=HBM,
-        out_shape=jax.ShapeDtypeStruct((MAX_PAIRS + BATCH, D, D), F32),
+        out_shape=jax.ShapeDtypeStruct((MAX_PAIRS + 8, D, D), F32),
         input_output_aliases={2 + len(arrays): 0} if more else {},
         scratch_shapes=[
             pltpu.VMEM((2, size, 2, OVB * BLOCK, D), BF16),
@@ -284,6 +284,7 @@
             pltpu.SemaphoreType.DMA,
         ],
         compiler_params=params(60),
+        name="rotations",
     )(info, count, *arrays, *more)
 
 
@@ -430,7 +431,7 @@
     )(jnp.zeros(1, jnp.int32) if core is None else core, frames, *parts)
 
 
-CHUNK = 1024
+CHUNK = 512
 
 
 def final_kernel(
@@ -438,19 +439,18 @@
 ):
     pieces = patch_ref.shape[1] // CHUNK
 
-    def piece(n):
-        return n // pieces, pl.ds(pl.multiple_of(n % pieces * CHUNK, CHUNK), CHUNK)
-
-    def copy_in(n):
-        p, r = piece(n)
-        return pltpu.make_async_copy(patch_ref.at[p, r], rows.at[p, r], in_sem.at[n])
-
-    def copy_out(n):
-        p, r = piece(n)
-        return pltpu.make_async_copy(outs.at[p, r], aligned_ref.at[p, r], out_sem.at[n])
-
-    for n in range(PER * pieces):
-        copy_in(n).start()
+    def lines(n):
+        return pl.ds(pl.multiple_of(n * CHUNK, CHUNK), CHUNK)
+
+    def copy_in(p, n):
+        return pltpu.make_async_copy(patch_ref.at[p, lines(n)], rows.at[p, lines(n)], in_sem.at[p, n])
+
+    def copy_out(p, n):
+        return pltpu.make_async_copy(outs.at[p, lines(n)], aligned_ref.at[p, lines(n)], out_sem.at[p, n])
+
+    every = [(p, n) for n in range(pieces) for p in range(PER)]
+    for at in every:
+        copy_in(*at).start()
     for ref, half in ((keep_ref, core_ref[0]), (other_ref, 1 - core_ref[0])):
         total_ref[pl.ds(pl.multiple_of(half * (D // 2), D // 2), D // 2)] = ref[...]
     gauge[0] = total_ref[...]
@@ -462,19 +462,21 @@
         low[p] = final.astype(BF16)
 
     def step(n, carry):
-        p, r = piece(n)
-        copy_in(n).wait()
-        outs[p, r] = dot(rows[p, r], low[p]).astype(BF16)
-        copy_out(n).start()
+        for p in range(PER):
+            copy_in(p, n).wait()
+        found = [dot(rows[p, lines(n)], low[p]).astype(BF16) for p in range(PER)]
+        for p in range(PER):
+            outs[p, lines(n)] = found[p]
+            copy_out(p, n).start()
         return carry
 
-    lax.fori_loop(0, PER * pieces, step, 0)
-    for n in range(PER * pieces):
-        copy_out(n).wait()
+    lax.fori_loop(0, pieces, step, 0)
+    for at in every:
+        copy_out(*at).wait()
 
 
 def make_final(core, keep, other, frames, patches):
-    pieces = PER * patches.shape[1] // CHUNK
+    pieces = patches.shape[1] // CHUNK
     return pl.pallas_call(
         final_kernel,
         in_specs=[SM, VM, VM, VM, HBM],
@@ -489,8 +491,8 @@
             pltpu.VMEM(patches.shape, BF16),
             pltpu.VMEM(patches.shape, BF16),
             pltpu.VMEM((PER, D, D), BF16),
-            pltpu.SemaphoreType.DMA((pieces,)),
-            pltpu.SemaphoreType.DMA((pieces,)),
+            pltpu.SemaphoreType.DMA((PER, pieces)),
+            pltpu.SemaphoreType.DMA((PER, pieces)),
         ],
         compiler_params=params(),
         name="aligned_rows",
@@ -511,7 +513,8 @@
 
 
 def spread_frames(low):
-    one, four, three = send(low, step_perm(UP)), send(low, step_perm(LEFT)), send(low, step_perm(RIGHT))
+    one, four = send(low, step_perm(UP)), send(low, step_perm(LEFT))
+    three = send(low, step_perm(RIGHT))
     two, five = send(one, step_perm(UP)), send(four, step_perm(LEFT))
     return [low, one, two, three, four, five] + [send(v, SIBLING) for v in (one, two, three)]
 
@@ -525,7 +528,8 @@
     )
     two = send(two, back_perm(UP))
     three = send(three, back_perm(RIGHT))
-    return [own, three, send(four + five, back_perm(LEFT)), send(one + two, back_perm(UP))]
+    four = send(four + five, back_perm(LEFT))
+    return [own, three, four, send(one + two, back_perm(UP))]
 
 
 def axis_sum(value, axis):
@@ -569,12 +573,12 @@
     five_0, two_0 = move(four_0, LEFT), move(one_0, UP)
     three_0 = move(lower, RIGHT)
     arrays = [patches, one_0, one_1, four_0, four_1, move(one_0), move(one_1)]
-    rot = make_rotations(info, count, arrays, LAYOUT, 0, BATCH)
+    rot = make_rotations(info, count, arrays, LAYOUT, 0, 3)
     three_1 = move(five_1, LEFT)
     arrays += [two_1, five_0, five_1, three_0, move(two_1), move(three_0)]
-    rot = make_rotations(info, count, arrays, LAYOUT, 1, BATCH, rot)
+    rot = make_rotations(info, count, arrays, LAYOUT, 1, 7, rot)
     arrays += [two_0, three_1, move(two_0), move(three_1)]
-    rot = make_rotations(info, count, arrays, LAYOUT, 2, BATCH, rot)
+    rot = make_rotations(info, count, arrays, LAYOUT, 2, 5, rot)
     core = lax.axis_index("gy_2").astype(jnp.int32).reshape(1)
     for sweep in range(SWEEPS):
         if sweep:

time: 384 us -> 390 us (1.016)
  Pallas kernels: 103 us -> 110 us
    pallas_call x3, Pallas kernels: 38.3 us -> 45.2 us  [make_rotations(): pl.pallas_call(functools.partial(rotation_kernel, layout, ready, size), i...]
    ppermute x9, starting transfers between devices: 16.6 us -> 10.1 us  [from_behind(): lax.ppermute(value, axis, [(i, (i + hops) % size) for i in range(size)])]
    ppermute x44, starting transfers between devices: 72.8 us -> 79.2 us  [send(): return lax.ppermute(value, GY, perm)]
  transfers between devices with their start and end apart: 55 -> 55, of which waited for: 33 -> 33; matrix products, arithmetic and copies ran while one was open for 2% -> 2% of each run, Pallas kernels for 16% -> 17%
where the time goes in v4:
time: 390 us; the launch traced here: 389 us
  waiting for transfers between devices  171 us (44%)
  Pallas kernels  110 us (28%)
  starting transfers between devices  92.8 us (24%)
  local copies, waits for them, and re-layouts  9.35 us (2%)
  other arithmetic  5.15 us (1%)
    ppermute x44, waiting for transfers between devices, send(): return lax.ppermute(value, GY, perm)  152 us
    ppermute x44, starting transfers between devices, send(): return lax.ppermute(value, GY, perm)  79.2 us
    pallas_call x3, Pallas kernels, make_rotations(): pl.pallas_call(functools.partial(rotation_kernel, layout, ready, size), i...  45.2 us
    ppermute x9, waiting for transfers between devices, from_behind(): lax.ppermute(value, axis, [(i, (i + hops) % size) for i in range(size)])  16.5 us
    pallas_call x2, Pallas kernels, make_update(): pl.pallas_call(update_kernel, in_specs=[SM] + [VM] * (1 + len(parts)), ou...  16.1 us
    pallas_call x2, Pallas kernels, make_estimates(): pl.pallas_call(estimate_kernel, in_specs=[SM, SM, HBM] + [HBM] * SLOTS, o...  16 us
    pallas_call x1, Pallas kernels, make_index(): pl.pallas_call(index_kernel, in_specs=[SM] * 4, out_specs=[SM] * 2, out_s...  14.4 us
    pallas_call x1, Pallas kernels, make_final(): pl.pallas_call(final_kernel, in_specs=[SM, VM, VM, VM, HBM], out_specs=[H...  10.9 us
  transfers between devices with their start and end apart: 55, of which 33 were waited for; matrix products, arithmetic and copies ran while one was open for 2% of the time, Pallas kernels for 17%

profile of v4, /device:TPU:1, one launch (start us, length us, event | category | flops | bytes accessed | tf_op | source)
XLA Modules:
  0.0 389.2 jit_solution(9916210547842232349)
XLA Ops:
  0.6 3.2 slice_bitcast_fusion.1
  3.8 4.6 %collective-permute-start.3 = (bf16[4096,256]{1,0:T(8,128)(2,1)}, bf16[4096,256]{1,0:T(8,128)(2,1)S(1)}, u32[]{:S(2)}, u32[]{:S(2)}) collective-permute-start(bf16[4096,256]{1,0:T(8,128)(2,1)} %slice_bitcast_fusion.1), channel_id=1, source_target_pairs={{0,6},{1,25},{2,0},{3,27},{4,2},{5,29},{6,4},{7,31},{8,14},{9,1},{... | collective-permute-start | bytes 6291464 | tf_op jit(solution)/shard_map/ppermute | solution.py:503
  8.4 7.4 %start_frames.1 = (f32[2,256,256]{2,1,0:T(8,128)}, bf16[2,256,256]{2,1,0:T(8,128)(2,1)}) custom-call(f32[2,256,256]{2,1,0:T(8,128)} %start_ref.1), custom_call_target="tpu_custom_call" | custom-call | tf_op jit(solution)/shard_map/start_frames/pallas_call | solution.py:299
  18.5 4.3 %collective-permute-done.16.refs_1_ = bf16[2,256,256]{2,1,0:T(8,128)(2,1)S(1)} collective-permute-done((bf16[2,256,256]{2,1,0:T(8,128)(2,1)}, bf16[2,256,256]{2,1,0:T(8,128)(2,1)S(1)}, u32[]{:S(2)}, u32[]{:S(2)}) %collective-permute-start.16) | collective-permute-done | bytes 262176 | tf_op jit(solution)/shard_map/ppermute | solution.py:503
  23.7 2.2 collective-permute-start
  25.8 8.7 %collective-permute-done.19.refs_4_ = bf16[2,256,256]{2,1,0:T(8,128)(2,1)S(1)} collective-permute-done((bf16[2,256,256]{2,1,0:T(8,128)(2,1)}, bf16[2,256,256]{2,1,0:T(8,128)(2,1)S(1)}, u32[]{:S(2)}, u32[]{:S(2)}) %collective-permute-start.19) | collective-permute-done | bytes 262176 | tf_op jit(solution)/shard_map/ppermute | solution.py:503
  35.7 3.0 collective-permute-start.2
  38.8 2.7 collective-permute-start.8
  41.4 19.3 %collective-permute-done.refs_1_ = bf16[4096,256]{1,0:T(8,128)(2,1)S(1)} collective-permute-done((bf16[4096,256]{1,0:T(8,128)(2,1)S(1)}, bf16[4096,256]{1,0:T(8,128)(2,1)S(1)}, u32[]{:S(2)}, u32[]{:S(2)}) %collective-permute-start) | collective-permute-done | bytes 2097184 | tf_op jit(solution)/shard_map/ppermute | solution.py:503
  60.7 9.3 %collective-permute-start.4 = (bf16[4096,256]{1,0:T(8,128)(2,1)S(1)}, bf16[4096,256]{1,0:T(8,128)(2,1)S(1)}, u32[]{:S(2)}, u32[]{:S(2)}) collective-permute-start(bf16[4096,256]{1,0:T(8,128)(2,1)S(1)} %collective-permute-done.refs_1_), channel_id=1, source_target_pairs={{0,1},{1,0},{2,3},{3,2},{4,5},{5,4},{6,7},{7,6},{8,9},{9,8},{10,11... | collective-permute-start | bytes 6291464 | tf_op jit(solution)/shard_map/ppermute | solution.py:503
  70.0 27.6 %collective-permute-done.1.refs_2_ = bf16[4096,256]{1,0:T(8,128)(2,1)S(1)} collective-permute-done((bf16[4096,256]{1,0:T(8,128)(2,1)}, bf16[4096,256]{1,0:T(8,128)(2,1)S(1)}, u32[]{:S(2)}, u32[]{:S(2)}) %collective-permute-start.1) | collective-permute-done | bytes 2097184 | tf_op jit(solution)/shard_map/ppermute | solution.py:503
  97.6 3.9 collective-permute-start.5
  102.2 3.1 collective-permute-done.5.refs_6_
  105.7 22.2 %collective-permute-done.6.refs_7_ = bf16[4096,256]{1,0:T(8,128)(2,1)S(1)} collective-permute-done((bf16[4096,256]{1,0:T(8,128)(2,1)S(1)}, bf16[4096,256]{1,0:T(8,128)(2,1)S(1)}, u32[]{:S(2)}, u32[]{:S(2)}) %collective-permute-start.6) | collective-permute-done | bytes 2097184 | tf_op jit(solution)/shard_map/ppermute | solution.py:503
  128.8 21.5 %collective-permute-done.12.refs_13_ = bf16[4096,256]{1,0:T(8,128)(2,1)S(1)} collective-permute-done((bf16[4096,256]{1,0:T(8,128)(2,1)S(1)}, bf16[4096,256]{1,0:T(8,128)(2,1)S(1)}, u32[]{:S(2)}, u32[]{:S(2)}) %collective-permute-start.12) | collective-permute-done | bytes 2097184 | tf_op jit(solution)/shard_map/ppermute | solution.py:503
  159.1 14.4 %pair_index.1 = (s32[4320]{0:T(1024)}, s32[3]{0:T(128)}) custom-call(s32[2]{0:T(128)} %pad_add_fusion.me_ref, s32[12288]{0:T(1024)} %constant.25.clone.table_ref, s32[512]{0:T(512)} %reshape.16.ends_ref, s32[2048]{0:T(1024)} %reshape.17.blocks_ref), custom_call_target="tpu_custom_call" | custom-call | tf_op jit(solution)/shard_map/pair_index/pallas_call | solution.py:187
  173.5 10.4 %rotations.3.refs_13_ = f32[152,256,256]{2,1,0:T(8,128)} custom-call(s32[4320]{0:T(1024)} %get-tuple-element.27.info_ref, s32[3]{0:T(128)} %get-tuple-element.28.count_ref, bf16[2,4096,256]{2,1,0:T(8,128)(2,1)} %patch_ref.1, bf16[4096,256]{1,0:T(8,128)(2,1)} %copy-done.2, bf16[4096,256]{1,0:T(8,128)(2,1)} %copy-done.3, bf16[4096,256]{1,0:T(8,128)(2,1)} %copy-done.4, ...), custom_call_target="tpu_custom_call" | custom-call | tf_op jit(solution)/shard_map/rotations/pallas_call | solution.py:273
  183.9 19.3 %rotations.4.refs_17_ = f32[152,256,256]{2,1,0:T(8,128)} custom-call(s32[4320]{0:T(1024)} %get-tuple-element.27.info_ref, s32[3]{0:T(128)} %get-tuple-element.28.count_ref, bf16[2,4096,256]{2,1,0:T(8,128)(2,1)} %patch_ref.1, bf16[4096,256]{1,0:T(8,128)(2,1)} %copy-done.2, bf16[4096,256]{1,0:T(8,128)(2,1)} %copy-done.3, ...), custom_call_target="tpu_custom_call", output_to_operand_aliasing={{}: (15, {})} | custom-call | tf_op jit(solution)/shard_map/rotations/pallas_call | solution.py:273
  203.2 15.4 %rotations.5.rot_ref = f32[152,256,256]{2,1,0:T(8,128)} custom-call(s32[4320]{0:T(1024)} %get-tuple-element.27.info_ref, s32[3]{0:T(128)} %get-tuple-element.28.count_ref, bf16[2,4096,256]{2,1,0:T(8,128)(2,1)} %patch_ref.1, bf16[4096,256]{1,0:T(8,128)(2,1)} %copy-done.2, bf16[4096,256]{1,0:T(8,128)(2,1)} %copy-done.3, ...), custom_call_target="tpu_custom_call", output_to_operand_aliasing={{}: (19, {})} | custom-call | tf_op jit(solution)/shard_map/rotations/pallas_call | solution.py:273
  218.7 8.0 %estimates.2 = (f32[2,256,256]{2,1,0:T(8,128)}, f32[2,256,256]{2,1,0:T(8,128)}, f32[2,256,256]{2,1,0:T(8,128)}, f32[2,256,256]{2,1,0:T(8,128)}, f32[2,256,256]{2...) custom-call(s32[4320]{0:T(1024)} %get-tuple-element.27.info_ref, s32[3]{0:T(128)} %get-tuple-element.28.count_ref, ...), custom_call_target="tpu_custom_call" | custom-call | tf_op jit(solution)/shard_map/estimates/pallas_call | solution.py:385
  226.7 17.5 %collective-permute-start.24 = (f32[6,256,256]{2,1,0:T(8,128)}, f32[6,256,256]{2,1,0:T(8,128)S(1)}, u32[]{:S(2)}, u32[]{:S(2)}) collective-permute-start(f32[6,256,256]{2,1,0:T(8,128)} %get-tuple-element.32), channel_id=1, source_target_pairs={{0,1},{1,0},{2,3},{3,2},{4,5},{5,4},{6,7},{7,6},{8,9},{9,8},{10,11... | collective-permute-start | bytes 4718600 | tf_op jit(solution)/shard_map/ppermute | solution.py:503
  244.2 3.2 collective-permute-done.24
  249.2 4.8 %collective-permute-done.26 = f32[2,256,256]{2,1,0:T(8,128)S(1)} collective-permute-done((f32[2,256,256]{2,1,0:T(8,128)}, f32[2,256,256]{2,1,0:T(8,128)S(1)}, u32[]{:S(2)}, u32[]{:S(2)}) %collective-permute-start.26) | collective-permute-done | bytes 524320 | tf_op jit(solution)/shard_map/ppermute | solution.py:503
  254.1 2.7 collective-permute-start.25
  258.8 4.9 %collective-permute-done.27.refs_2_ = f32[2,256,256]{2,1,0:T(8,128)S(1)} collective-permute-done((f32[2,256,256]{2,1,0:T(8,128)S(1)}, f32[2,256,256]{2,1,0:T(8,128)S(1)}, u32[]{:S(2)}, u32[]{:S(2)}) %collective-permute-start.27) | collective-permute-done | bytes 524320 | tf_op jit(solution)/shard_map/ppermute | solution.py:503
  264.6 5.6 %collective-permute-done.29.refs_3_ = f32[2,256,256]{2,1,0:T(8,128)S(1)} collective-permute-done((f32[2,256,256]{2,1,0:T(8,128)S(1)}, f32[2,256,256]{2,1,0:T(8,128)S(1)}, u32[]{:S(2)}, u32[]{:S(2)}) %collective-permute-start.29) | collective-permute-done | bytes 524320 | tf_op jit(solution)/shard_map/ppermute | solution.py:503
  271.0 8.1 %update_frames.2 = (f32[2,256,256]{2,1,0:T(8,128)}, bf16[2,256,256]{2,1,0:T(8,128)(2,1)}) custom-call(s32[1]{0:T(128)} %constant.9.clone.1.core_ref, f32[2,256,256]{2,1,0:T(8,128)} %get-tuple-element.26.frame_ref, f32[2,256,256]{2,1,0:T(8,128)} %get-tuple-element.30.refs_0_, f32[2,256,256]{2,1,0:T(8,128)} %copy-done.20, f32[2,256,256]{2,1,0:T(8,128)} %copy-done.18, ...), custom_call_target="tpu_custom_call" | custom-call | tf_op jit(solution)/shard_map/update_frames/pallas_call | solution.py:424
  280.5 5.9 %collective-permute-done.30.refs_1_ = bf16[2,256,256]{2,1,0:T(8,128)(2,1)S(1)} collective-permute-done((bf16[2,256,256]{2,1,0:T(8,128)(2,1)}, bf16[2,256,256]{2,1,0:T(8,128)(2,1)S(1)}, u32[]{:S(2)}, u32[]{:S(2)}) %collective-permute-start.30) | collective-permute-done | bytes 262176 | tf_op jit(solution)/shard_map/ppermute | solution.py:503
  286.5 2.8 collective-permute-start.35
  289.3 3.0 collective-permute-start.34
  293.7 3.2 collective-permute-start.36
  298.8 8.0 %estimates.3 = (f32[2,256,256]{2,1,0:T(8,128)}, f32[2,256,256]{2,1,0:T(8,128)}, f32[2,256,256]{2,1,0:T(8,128)}, f32[2,256,256]{2,1,0:T(8,128)}, f32[2,256,256]{2...) custom-call(s32[4320]{0:T(1024)} %get-tuple-element.27.info_ref, s32[3]{0:T(128)} %get-tuple-element.28.count_ref, ...), custom_call_target="tpu_custom_call" | custom-call | tf_op jit(solution)/shard_map/estimates/pallas_call | solution.py:385
  306.8 2.1 collective-permute-start.38
  308.9 3.2 collective-permute-done.38
  313.8 3.2 collective-permute-start.42
  318.8 2.7 collective-permute-start.39
  323.1 3.2 collective-permute-start.43
  329.1 5.9 %collective-permute-done.43.refs_3_ = f32[2,256,256]{2,1,0:T(8,128)S(1)} collective-permute-done((f32[2,256,256]{2,1,0:T(8,128)S(1)}, f32[2,256,256]{2,1,0:T(8,128)S(1)}, u32[]{:S(2)}, u32[]{:S(2)}) %collective-permute-start.43) | collective-permute-done | bytes 524320 | tf_op jit(solution)/shard_map/ppermute | solution.py:503
  335.8 8.1 %update_frames.3 = (f32[2,256,256]{2,1,0:T(8,128)}, f32[128,256]{1,0:T(8,128)}, f32[128,256]{1,0:T(8,128)}) custom-call(s32[1]{0:T(128)} %bitcast.core_ref, f32[2,256,256]{2,1,0:T(8,128)} %get-tuple-element.37.frame_ref, f32[2,256,256]{2,1,0:T(8,128)} %get-tuple-element.39.refs_0_, f32[2,256,256]{2,1,0:T(8,128)} %copy-done.21, f32[2,256,256]{2,1,0:T(8,128)} %copy-done.19, ...), custom_call_target="tpu_custom_call" | custom-call | tf_op jit(solution)/shard_map/update_frames/pallas_call | solution.py:424
  346.5 2.7 collective-permute-start.46
  349.1 3.4 collective-permute-done.45
  355.1 2.7 collective-permute-start.49
  357.8 2.3 collective-permute-done.48
  360.6 3.1 collective-permute-done.50
  363.8 3.5 collective-permute-start.52
  369.5 3.5 collective-permute-done.53
  373.1 3.4 collective-permute-start.54
  378.2 10.9 %aligned_rows.1 = (bf16[2,4096,256]{2,1,0:T(8,128)(2,1)}, f32[2,256,256]{2,1,0:T(8,128)}, f32[256,256]{1,0:T(8,128)}) custom-call(s32[1]{0:T(128)} %bitcast.core_ref, f32[128,256]{1,0:T(8,128)} %copy-done.17, f32[128,256]{1,0:T(8,128)} %copy-done.36, f32[2,256,256]{2,1,0:T(8,128)} %get-tuple-element.48.frame_ref, bf16[2,4096,256]{2,1,0:T(8,128)(2,1)} %patch_ref.1), custom_call_target="tpu_custom_call" | custom-call | tf_op jit(solution)/shard_map/aligned_rows/pallas_call | solution.py:480
  (167 shorter events, 44.1 us)
Async XLA Ops:
  3.8 34.9 %collective-permute-start.3 = (bf16[4096,256]{1,0:T(8,128)(2,1)}, bf16[4096,256]{1,0:T(8,128)(2,1)S(1)}, u32[]{:S(2)}, u32[]{:S(2)}) collective-permute-start(bf16[4096,256]{1,0:T(8,128)(2,1)} %slice_bitcast_fusion.1), channel_id=1, source_target_pairs={{0,6},{1,25},{2,0},{3,27},{4,2},{5,29},{6,4},{7,31},{8,14},{9,1},{... | collective-permute-start | bytes 6291464 | tf_op jit(solution)/shard_map/ppermute | solution.py:503
  15.8 6.9 %collective-permute-start.16 = (bf16[2,256,256]{2,1,0:T(8,128)(2,1)}, bf16[2,256,256]{2,1,0:T(8,128)(2,1)S(1)}, u32[]{:S(2)}, u32[]{:S(2)}) collective-permute-start(bf16[2,256,256]{2,1,0:T(8,128)(2,1)} %get-tuple-element.29.refs_0_), channel_id=1, source_target_pairs={{0,8},{1,3},{2,10},{3,5},{4,12},{5,7},{6,14},{7,1},{8,16},{9,11},{... | collective-permute-start | bytes 786440 | tf_op jit(solution)/shard_map/ppermute | solution.py:503
  17.0 17.5 %collective-permute-start.19 = (bf16[2,256,256]{2,1,0:T(8,128)(2,1)}, bf16[2,256,256]{2,1,0:T(8,128)(2,1)S(1)}, u32[]{:S(2)}, u32[]{:S(2)}) collective-permute-start(bf16[2,256,256]{2,1,0:T(8,128)(2,1)} %get-tuple-element.29.refs_0_), channel_id=1, source_target_pairs={{0,6},{1,25},{2,0},{3,27},{4,2},{5,29},{6,4},{7,31},{8,14},{9,1},{... | collective-permute-start | bytes 786440 | tf_op jit(solution)/shard_map/ppermute | solution.py:503
  17.1 18.6 %collective-permute-start.18 = (bf16[2,256,256]{2,1,0:T(8,128)(2,1)}, bf16[2,256,256]{2,1,0:T(8,128)(2,1)S(1)}, u32[]{:S(2)}, u32[]{:S(2)}) collective-permute-start(bf16[2,256,256]{2,1,0:T(8,128)(2,1)} %get-tuple-element.29.refs_0_), channel_id=1, source_target_pairs={{0,2},{1,9},{2,4},{3,11},{4,6},{5,13},{6,0},{7,15},{8,10},{9,17},{... | collective-permute-start | bytes 786440 | tf_op jit(solution)/shard_map/ppermute | solution.py:503
  22.8 16.0 %collective-permute-start.17 = (bf16[2,256,256]{2,1,0:T(8,128)(2,1)S(1)}, bf16[2,256,256]{2,1,0:T(8,128)(2,1)S(1)}, u32[]{:S(2)}, u32[]{:S(2)}) collective-permute-start(bf16[2,256,256]{2,1,0:T(8,128)(2,1)S(1)} %collective-permute-done.16.refs_1_), channel_id=1, source_target_pairs={{0,8},{1,3},{2,10},{3,5},{4,12},{5,7},{6,14},{7,1},{8,16},{9,11},{... | collective-permute-start | bytes 786440 | tf_op jit(solution)/shard_map/ppermute | solution.py:503
  23.7 37.1 %collective-permute-start = (bf16[4096,256]{1,0:T(8,128)(2,1)S(1)}, bf16[4096,256]{1,0:T(8,128)(2,1)S(1)}, u32[]{:S(2)}, u32[]{:S(2)}) collective-permute-start(bf16[4096,256]{1,0:T(8,128)(2,1)S(1)} %slice_bitcast_fusion), channel_id=1, source_target_pairs={{0,8},{1,3},{2,10},{3,5},{4,12},{5,7},{6,14},{7,1},{8,16},{9,11},{... | collective-permute-start | bytes 6291464 | tf_op jit(solution)/shard_map/ppermute | solution.py:503
  34.5 63.1 %collective-permute-start.1 = (bf16[4096,256]{1,0:T(8,128)(2,1)}, bf16[4096,256]{1,0:T(8,128)(2,1)S(1)}, u32[]{:S(2)}, u32[]{:S(2)}) collective-permute-start(bf16[4096,256]{1,0:T(8,128)(2,1)} %slice_bitcast_fusion.1), channel_id=1, source_target_pairs={{0,8},{1,3},{2,10},{3,5},{4,12},{5,7},{6,14},{7,1},{8,16},{9,11},{... | collective-permute-start | bytes 6291464 | tf_op jit(solution)/shard_map/ppermute | solution.py:503
  35.7 65.8 %collective-permute-start.2 = (bf16[4096,256]{1,0:T(8,128)(2,1)S(1)}, bf16[4096,256]{1,0:T(8,128)(2,1)S(1)}, u32[]{:S(2)}, u32[]{:S(2)}) collective-permute-start(bf16[4096,256]{1,0:T(8,128)(2,1)S(1)} %slice_bitcast_fusion), channel_id=1, source_target_pairs={{0,6},{1,25},{2,0},{3,27},{4,2},{5,29},{6,4},{7,31},{8,14},{9,1},{... | collective-permute-start | bytes 6291464 | tf_op jit(solution)/shard_map/ppermute | solution.py:503
  38.7 62.8 %collective-permute-start.9 = (bf16[4096,256]{1,0:T(8,128)(2,1)S(1)}, bf16[4096,256]{1,0:T(8,128)(2,1)S(1)}, u32[]{:S(2)}, u32[]{:S(2)}) collective-permute-start(bf16[4096,256]{1,0:T(8,128)(2,1)S(1)} %slice_bitcast_fusion), channel_id=1, source_target_pairs={{0,2},{1,9},{2,4},{3,11},{4,6},{5,13},{6,0},{7,15},{8,10},{9,17},{... | collective-permute-start | bytes 6291464 | tf_op jit(solution)/shard_map/ppermute | solution.py:503
  38.8 62.8 %collective-permute-start.8 = (bf16[4096,256]{1,0:T(8,128)(2,1)S(1)}, bf16[4096,256]{1,0:T(8,128)(2,1)S(1)}, u32[]{:S(2)}, u32[]{:S(2)}) collective-permute-start(bf16[4096,256]{1,0:T(8,128)(2,1)S(1)} %collective-permute-done.3.refs_4_), channel_id=1, source_target_pairs={{0,6},{1,25},{2,0},{3,27},{4,2},{5,29},{6,4},{7,31},{8,14},{9,1},{... | collective-permute-start | bytes 6291464 | tf_op jit(solution)/shard_map/ppermute | solution.py:503
  60.7 41.4 %collective-permute-start.4 = (bf16[4096,256]{1,0:T(8,128)(2,1)S(1)}, bf16[4096,256]{1,0:T(8,128)(2,1)S(1)}, u32[]{:S(2)}, u32[]{:S(2)}) collective-permute-start(bf16[4096,256]{1,0:T(8,128)(2,1)S(1)} %collective-permute-done.refs_1_), channel_id=1, source_target_pairs={{0,1},{1,0},{2,3},{3,2},{4,5},{5,4},{6,7},{7,6},{8,9},{9,8},{10,11... | collective-permute-start | bytes 6291464 | tf_op jit(solution)/shard_map/ppermute | solution.py:503
  97.6 7.7 %collective-permute-start.5 = (bf16[4096,256]{1,0:T(8,128)(2,1)S(1)}, bf16[4096,256]{1,0:T(8,128)(2,1)S(1)}, u32[]{:S(2)}, u32[]{:S(2)}) collective-permute-start(bf16[4096,256]{1,0:T(8,128)(2,1)S(1)} %collective-permute-done.1.refs_2_), channel_id=1, source_target_pairs={{0,1},{1,0},{2,3},{3,2},{4,5},{5,4},{6,7},{7,6},{8,9},{9,8},{10,11... | collective-permute-start | bytes 6291464 | tf_op jit(solution)/shard_map/ppermute | solution.py:503
  101.5 26.4 %collective-permute-start.6 = (bf16[4096,256]{1,0:T(8,128)(2,1)S(1)}, bf16[4096,256]{1,0:T(8,128)(2,1)S(1)}, u32[]{:S(2)}, u32[]{:S(2)}) collective-permute-start(bf16[4096,256]{1,0:T(8,128)(2,1)S(1)} %collective-permute-done.1.refs_2_), channel_id=1, source_target_pairs={{0,8},{1,3},{2,10},{3,5},{4,12},{5,7},{6,14},{7,1},{8,16},{9,11},{... | collective-permute-start | bytes 6291464 | tf_op jit(solution)/shard_map/ppermute | solution.py:503
  101.5 48.8 %collective-permute-start.12 = (bf16[4096,256]{1,0:T(8,128)(2,1)S(1)}, bf16[4096,256]{1,0:T(8,128)(2,1)S(1)}, u32[]{:S(2)}, u32[]{:S(2)}) collective-permute-start(bf16[4096,256]{1,0:T(8,128)(2,1)S(1)} %collective-permute-done.refs_1_), channel_id=1, source_target_pairs={{0,8},{1,3},{2,10},{3,5},{4,12},{5,7},{6,14},{7,1},{8,16},{9,11},{... | collective-permute-start | bytes 6291464 | tf_op jit(solution)/shard_map/ppermute | solution.py:503
  101.6 49.7 %collective-permute-start.13 = (bf16[4096,256]{1,0:T(8,128)(2,1)S(1)}, bf16[4096,256]{1,0:T(8,128)(2,1)}, u32[]{:S(2)}, u32[]{:S(2)}) collective-permute-start(bf16[4096,256]{1,0:T(8,128)(2,1)S(1)} %collective-permute-done.8.refs_9_), channel_id=1, source_target_pairs={{0,6},{1,25},{2,0},{3,27},{4,2},{5,29},{6,4},{7,31},{8,14},{9,1},{... | collective-permute-start | bytes 6291464 | tf_op jit(solution)/shard_map/ppermute | solution.py:503
  102.1 49.3 %collective-permute-start.7 = (bf16[4096,256]{1,0:T(8,128)(2,1)S(1)}, bf16[4096,256]{1,0:T(8,128)(2,1)S(1)}, u32[]{:S(2)}, u32[]{:S(2)}) collective-permute-start(bf16[4096,256]{1,0:T(8,128)(2,1)S(1)} %collective-permute-done.2.refs_3_), channel_id=1, source_target_pairs={{0,6},{1,25},{2,0},{3,27},{4,2},{5,29},{6,4},{7,31},{8,14},{9,1},{... | collective-permute-start | bytes 6291464 | tf_op jit(solution)/shard_map/ppermute | solution.py:503
  105.3 46.6 %collective-permute-start.11 = (bf16[4096,256]{1,0:T(8,128)(2,1)S(1)}, bf16[4096,256]{1,0:T(8,128)(2,1)S(1)}, u32[]{:S(2)}, u32[]{:S(2)}) collective-permute-start(bf16[4096,256]{1,0:T(8,128)(2,1)S(1)} %collective-permute-done.9.refs_10_), channel_id=1, source_target_pairs={{0,1},{1,0},{2,3},{3,2},{4,5},{5,4},{6,7},{7,6},{8,9},{9,8},{10,11... | collective-permute-start | bytes 6291464 | tf_op jit(solution)/shard_map/ppermute | solution.py:503
  127.9 25.5 %collective-permute-start.10 = (bf16[4096,256]{1,0:T(8,128)(2,1)S(1)}, bf16[4096,256]{1,0:T(8,128)(2,1)S(1)}, u32[]{:S(2)}, u32[]{:S(2)}) collective-permute-start(bf16[4096,256]{1,0:T(8,128)(2,1)S(1)} %collective-permute-done.6.refs_7_), channel_id=1, source_target_pairs={{0,1},{1,0},{2,3},{3,2},{4,5},{5,4},{6,7},{7,6},{8,9},{9,8},{10,11... | collective-permute-start | bytes 6291464 | tf_op jit(solution)/shard_map/ppermute | solution.py:503
  151.3 51.9 %collective-permute-start.15 = (bf16[4096,256]{1,0:T(8,128)(2,1)}, bf16[4096,256]{1,0:T(8,128)(2,1)}, u32[]{:S(2)}, u32[]{:S(2)}) collective-permute-start(bf16[4096,256]{1,0:T(8,128)(2,1)} %collective-permute-done.13.refs_14_), channel_id=1, source_target_pairs={{0,1},{1,0},{2,3},{3,2},{4,5},{5,4},{6,7},{7,6},{8,9},{9,8},{10,11... | collective-permute-start | bytes 6291464 | tf_op jit(solution)/shard_map/ppermute | solution.py:503
  151.4 67.2 %collective-permute-start.21 = (bf16[2,256,256]{2,1,0:T(8,128)(2,1)S(1)}, bf16[2,256,256]{2,1,0:T(8,128)(2,1)}, u32[]{:S(2)}, u32[]{:S(2)}) collective-permute-start(bf16[2,256,256]{2,1,0:T(8,128)(2,1)S(1)} %collective-permute-done.16.refs_1_), channel_id=1, source_target_pairs={{0,1},{1,0},{2,3},{3,2},{4,5},{5,4},{6,7},{7,6},{8,9},{9,8},{10,11... | collective-permute-start | bytes 786440 | tf_op jit(solution)/shard_map/ppermute | solution.py:503
  151.9 66.7 %collective-permute-start.20 = (bf16[2,256,256]{2,1,0:T(8,128)(2,1)S(1)}, bf16[2,256,256]{2,1,0:T(8,128)(2,1)}, u32[]{:S(2)}, u32[]{:S(2)}) collective-permute-start(bf16[2,256,256]{2,1,0:T(8,128)(2,1)S(1)} %collective-permute-done.19.refs_4_), channel_id=1, source_target_pairs={{0,6},{1,25},{2,0},{3,27},{4,2},{5,29},{6,4},{7,31},{8,14},{9,1},{... | collective-permute-start | bytes 786440 | tf_op jit(solution)/shard_map/ppermute | solution.py:503
  153.4 65.3 %collective-permute-start.23 = (bf16[2,256,256]{2,1,0:T(8,128)(2,1)S(1)}, bf16[2,256,256]{2,1,0:T(8,128)(2,1)}, u32[]{:S(2)}, u32[]{:S(2)}) collective-permute-start(bf16[2,256,256]{2,1,0:T(8,128)(2,1)S(1)} %collective-permute-done.18.refs_3_), channel_id=1, source_target_pairs={{0,1},{1,0},{2,3},{3,2},{4,5},{5,4},{6,7},{7,6},{8,9},{9,8},{10,11... | collective-permute-start | bytes 786440 | tf_op jit(solution)/shard_map/ppermute | solution.py:503
  155.1 63.6 %collective-permute-start.22 = (bf16[2,256,256]{2,1,0:T(8,128)(2,1)S(1)}, bf16[2,256,256]{2,1,0:T(8,128)(2,1)}, u32[]{:S(2)}, u32[]{:S(2)}) collective-permute-start(bf16[2,256,256]{2,1,0:T(8,128)(2,1)S(1)} %collective-permute-done.17.refs_2_), channel_id=1, source_target_pairs={{0,1},{1,0},{2,3},{3,2},{4,5},{5,4},{6,7},{7,6},{8,9},{9,8},{10,11... | collective-permute-start | bytes 786440 | tf_op jit(solution)/shard_map/ppermute | solution.py:503
  226.7 20.7 %collective-permute-start.24 = (f32[6,256,256]{2,1,0:T(8,128)}, f32[6,256,256]{2,1,0:T(8,128)S(1)}, u32[]{:S(2)}, u32[]{:S(2)}) collective-permute-start(f32[6,256,256]{2,1,0:T(8,128)} %get-tuple-element.32), channel_id=1, source_target_pairs={{0,1},{1,0},{2,3},{3,2},{4,5},{5,4},{6,7},{7,6},{8,9},{9,8},{10,11... | collective-permute-start | bytes 4718600 | tf_op jit(solution)/shard_map/ppermute | solution.py:503
  244.2 9.7 %collective-permute-start.26 = (f32[2,256,256]{2,1,0:T(8,128)}, f32[2,256,256]{2,1,0:T(8,128)S(1)}, u32[]{:S(2)}, u32[]{:S(2)}) collective-permute-start(f32[2,256,256]{2,1,0:T(8,128)} %get-tuple-element.34), channel_id=1, source_target_pairs={{6,0},{25,1},{0,2},{27,3},{2,4},{29,5},{4,6},{31,7},{14,8},{1,9},{... | collective-permute-start | bytes 1572872 | tf_op jit(solution)/shard_map/ppermute | solution.py:503
  249.1 8.4 %collective-permute-start.28 = (f32[2,256,256]{2,1,0:T(8,128)S(1)}, f32[2,256,256]{2,1,0:T(8,128)S(1)}, u32[]{:S(2)}, u32[]{:S(2)}) collective-permute-start(f32[2,256,256]{2,1,0:T(8,128)S(1)} %get-tuple-element.52), channel_id=1, source_target_pairs={{8,0},{3,1},{10,2},{5,3},{12,4},{7,5},{14,6},{1,7},{16,8},{11,9},{... | collective-permute-start | bytes 1572872 | tf_op jit(solution)/shard_map/ppermute | solution.py:503
  254.0 9.6 %collective-permute-start.27 = (f32[2,256,256]{2,1,0:T(8,128)S(1)}, f32[2,256,256]{2,1,0:T(8,128)S(1)}, u32[]{:S(2)}, u32[]{:S(2)}) collective-permute-start(f32[2,256,256]{2,1,0:T(8,128)S(1)} %add.69), channel_id=1, source_target_pairs={{6,0},{25,1},{0,2},{27,3},{2,4},{29,5},{4,6},{31,7},{14,8},{1,9},{... | collective-permute-start | bytes 1572872 | tf_op jit(solution)/shard_map/ppermute | solution.py:503
  254.1 10.5 %collective-permute-start.25 = (f32[2,256,256]{2,1,0:T(8,128)S(1)}, f32[2,256,256]{2,1,0:T(8,128)S(1)}, u32[]{:S(2)}, u32[]{:S(2)}) collective-permute-start(f32[2,256,256]{2,1,0:T(8,128)S(1)} %get-tuple-element.54), channel_id=1, source_target_pairs={{2,0},{9,1},{4,2},{11,3},{6,4},{13,5},{0,6},{15,7},{10,8},{17,9},{... | collective-permute-start | bytes 1572872 | tf_op jit(solution)/shard_map/ppermute | solution.py:503
  257.5 12.6 %collective-permute-start.29 = (f32[2,256,256]{2,1,0:T(8,128)S(1)}, f32[2,256,256]{2,1,0:T(8,128)S(1)}, u32[]{:S(2)}, u32[]{:S(2)}) collective-permute-start(f32[2,256,256]{2,1,0:T(8,128)S(1)} %add.72), channel_id=1, source_target_pairs={{8,0},{3,1},{10,2},{5,3},{12,4},{7,5},{14,6},{1,7},{16,8},{11,9},{... | collective-permute-start | bytes 1572872 | tf_op jit(solution)/shard_map/ppermute | solution.py:503
  279.1 7.4 %collective-permute-start.30 = (bf16[2,256,256]{2,1,0:T(8,128)(2,1)}, bf16[2,256,256]{2,1,0:T(8,128)(2,1)S(1)}, u32[]{:S(2)}, u32[]{:S(2)}) collective-permute-start(bf16[2,256,256]{2,1,0:T(8,128)(2,1)} %get-tuple-element.38.refs_0_), channel_id=1, source_target_pairs={{0,8},{1,3},{2,10},{3,5},{4,12},{5,7},{6,14},{7,1},{8,16},{9,11},{... | collective-permute-start | bytes 786440 | tf_op jit(solution)/shard_map/ppermute | solution.py:503
  279.1 10.2 %collective-permute-start.33 = (bf16[2,256,256]{2,1,0:T(8,128)(2,1)}, bf16[2,256,256]{2,1,0:T(8,128)(2,1)S(1)}, u32[]{:S(2)}, u32[]{:S(2)}) collective-permute-start(bf16[2,256,256]{2,1,0:T(8,128)(2,1)} %get-tuple-element.38.refs_0_), channel_id=1, source_target_pairs={{0,6},{1,25},{2,0},{3,27},{4,2},{5,29},{6,4},{7,31},{8,14},{9,1},{... | collective-permute-start | bytes 786440 | tf_op jit(solution)/shard_map/ppermute | solution.py:503
  279.1 13.2 %collective-permute-start.32 = (bf16[2,256,256]{2,1,0:T(8,128)(2,1)}, bf16[2,256,256]{2,1,0:T(8,128)(2,1)S(1)}, u32[]{:S(2)}, u32[]{:S(2)}) collective-permute-start(bf16[2,256,256]{2,1,0:T(8,128)(2,1)} %get-tuple-element.38.refs_0_), channel_id=1, source_target_pairs={{0,2},{1,9},{2,4},{3,11},{4,6},{5,13},{6,0},{7,15},{8,10},{9,17},{... | collective-permute-start | bytes 786440 | tf_op jit(solution)/shard_map/ppermute | solution.py:503
  286.5 7.2 %collective-permute-start.31 = (bf16[2,256,256]{2,1,0:T(8,128)(2,1)S(1)}, bf16[2,256,256]{2,1,0:T(8,128)(2,1)S(1)}, u32[]{:S(2)}, u32[]{:S(2)}) collective-permute-start(bf16[2,256,256]{2,1,0:T(8,128)(2,1)S(1)} %collective-permute-done.30.refs_1_), channel_id=1, source_target_pairs={{0,8},{1,3},{2,10},{3,5},{4,12},{5,7},{6,14},{7,1},{8,16},{9,11},{... | collective-permute-start | bytes 786440 | tf_op jit(solution)/shard_map/ppermute | solution.py:503
  286.5 10.4 %collective-permute-start.35 = (bf16[2,256,256]{2,1,0:T(8,128)(2,1)S(1)}, bf16[2,256,256]{2,1,0:T(8,128)(2,1)S(1)}, u32[]{:S(2)}, u32[]{:S(2)}) collective-permute-start(bf16[2,256,256]{2,1,0:T(8,128)(2,1)S(1)} %collective-permute-done.30.refs_1_), channel_id=1, source_target_pairs={{0,1},{1,0},{2,3},{3,2},{4,5},{5,4},{6,7},{7,6},{8,9},{9,8},{10,11... | collective-permute-start | bytes 786440 | tf_op jit(solution)/shard_map/ppermute | solution.py:503
  289.3 7.6 %collective-permute-start.34 = (bf16[2,256,256]{2,1,0:T(8,128)(2,1)S(1)}, bf16[2,256,256]{2,1,0:T(8,128)(2,1)S(1)}, u32[]{:S(2)}, u32[]{:S(2)}) collective-permute-start(bf16[2,256,256]{2,1,0:T(8,128)(2,1)S(1)} %collective-permute-done.33.refs_4_), channel_id=1, source_target_pairs={{0,6},{1,25},{2,0},{3,27},{4,2},{5,29},{6,4},{7,31},{8,14},{9,1},{... | collective-permute-start | bytes 786440 | tf_op jit(solution)/shard_map/ppermute | solution.py:503
  308.9 9.7 %collective-permute-start.40 = (f32[2,256,256]{2,1,0:T(8,128)}, f32[2,256,256]{2,1,0:T(8,128)S(1)}, u32[]{:S(2)}, u32[]{:S(2)}) collective-permute-start(f32[2,256,256]{2,1,0:T(8,128)} %get-tuple-element.43), channel_id=1, source_target_pairs={{6,0},{25,1},{0,2},{27,3},{2,4},{29,5},{4,6},{31,7},{14,8},{1,9},{... | collective-permute-start | bytes 1572872 | tf_op jit(solution)/shard_map/ppermute | solution.py:503
  313.8 9.3 %collective-permute-start.42 = (f32[2,256,256]{2,1,0:T(8,128)S(1)}, f32[2,256,256]{2,1,0:T(8,128)S(1)}, u32[]{:S(2)}, u32[]{:S(2)}) collective-permute-start(f32[2,256,256]{2,1,0:T(8,128)S(1)} %get-tuple-element.49), channel_id=1, source_target_pairs={{8,0},{3,1},{10,2},{5,3},{12,4},{7,5},{14,6},{1,7},{16,8},{11,9},{... | collective-permute-start | bytes 1572872 | tf_op jit(solution)/shard_map/ppermute | solution.py:503
  318.7 9.6 %collective-permute-start.41 = (f32[2,256,256]{2,1,0:T(8,128)S(1)}, f32[2,256,256]{2,1,0:T(8,128)S(1)}, u32[]{:S(2)}, u32[]{:S(2)}) collective-permute-start(f32[2,256,256]{2,1,0:T(8,128)S(1)} %add.74), channel_id=1, source_target_pairs={{6,0},{25,1},{0,2},{27,3},{2,4},{29,5},{4,6},{31,7},{14,8},{1,9},{... | collective-permute-start | bytes 1572872 | tf_op jit(solution)/shard_map/ppermute | solution.py:503
  318.8 10.3 %collective-permute-start.39 = (f32[2,256,256]{2,1,0:T(8,128)S(1)}, f32[2,256,256]{2,1,0:T(8,128)S(1)}, u32[]{:S(2)}, u32[]{:S(2)}) collective-permute-start(f32[2,256,256]{2,1,0:T(8,128)S(1)} %get-tuple-element.51), channel_id=1, source_target_pairs={{2,0},{9,1},{4,2},{11,3},{6,4},{13,5},{0,6},{15,7},{10,8},{17,9},{... | collective-permute-start | bytes 1572872 | tf_op jit(solution)/shard_map/ppermute | solution.py:503
  323.1 11.9 %collective-permute-start.43 = (f32[2,256,256]{2,1,0:T(8,128)S(1)}, f32[2,256,256]{2,1,0:T(8,128)S(1)}, u32[]{:S(2)}, u32[]{:S(2)}) collective-permute-start(f32[2,256,256]{2,1,0:T(8,128)S(1)} %add.77), channel_id=1, source_target_pairs={{8,0},{3,1},{10,2},{5,3},{12,4},{7,5},{14,6},{1,7},{16,8},{11,9},{... | collective-permute-start | bytes 1572872 | tf_op jit(solution)/shard_map/ppermute | solution.py:503
  346.4 6.2 %collective-permute-start.45 = (f32[128,256]{1,0:T(8,128)S(1)}, f32[128,256]{1,0:T(8,128)S(1)}, u32[]{:S(2)}, u32[]{:S(2)}) collective-permute-start(f32[128,256]{1,0:T(8,128)S(1)} %add.78), channel_id=1, source_target_pairs={{0,32},{32,64},{64,96},{96,0},{1,33},{33,65},{65,97},{97,1},{2,34}... | collective-permute-start | bytes 393224 | tf_op jit(solution)/shard_map/ppermute | solution.py:539
  346.5 7.8 %collective-permute-start.46 = (f32[128,256]{1,0:T(8,128)S(1)}, f32[128,256]{1,0:T(8,128)S(1)}, u32[]{:S(2)}, u32[]{:S(2)}) collective-permute-start(f32[128,256]{1,0:T(8,128)S(1)} %add.78), channel_id=1, source_target_pairs={{0,96},{32,0},{64,32},{96,64},{1,97},{33,1},{65,33},{97,65},{2,98}... | collective-permute-start | bytes 393224 | tf_op jit(solution)/shard_map/ppermute | solution.py:539
  349.1 5.9 %collective-permute-start.47 = (f32[128,256]{1,0:T(8,128)S(1)}, f32[128,256]{1,0:T(8,128)S(1)}, u32[]{:S(2)}, u32[]{:S(2)}) collective-permute-start(f32[128,256]{1,0:T(8,128)S(1)} %add.78), channel_id=1, source_target_pairs={{0,64},{32,96},{64,0},{96,32},{1,65},{33,97},{65,1},{97,33},{2,66}... | collective-permute-start | bytes 393224 | tf_op jit(solution)/shard_map/ppermute | solution.py:539
  355.1 5.5 %collective-permute-start.49 = (f32[128,256]{1,0:T(8,128)S(1)}, f32[128,256]{1,0:T(8,128)S(1)}, u32[]{:S(2)}, u32[]{:S(2)}) collective-permute-start(f32[128,256]{1,0:T(8,128)S(1)} %add_add_fusion.2), channel_id=1, source_target_pairs={{0,24},{8,0},{16,8},{24,16},{1,25},{9,1},{17,9},{25,17},{2,26},{10... | collective-permute-start | bytes 393224 | tf_op jit(solution)/shard_map/ppermute | solution.py:539
  357.8 5.9 %collective-permute-start.50 = (f32[128,256]{1,0:T(8,128)S(1)}, f32[128,256]{1,0:T(8,128)S(1)}, u32[]{:S(2)}, u32[]{:S(2)}) collective-permute-start(f32[128,256]{1,0:T(8,128)S(1)} %add_add_fusion.2), channel_id=1, source_target_pairs={{0,16},{8,24},{16,0},{24,8},{1,17},{9,25},{17,1},{25,9},{2,18},{10... | collective-permute-start | bytes 393224 | tf_op jit(solution)/shard_map/ppermute | solution.py:539
  363.7 5.8 %collective-permute-start.51 = (f32[128,256]{1,0:T(8,128)S(1)}, f32[128,256]{1,0:T(8,128)S(1)}, u32[]{:S(2)}, u32[]{:S(2)}) collective-permute-start(f32[128,256]{1,0:T(8,128)S(1)} %add_add_fusion.1), channel_id=1, source_target_pairs={{0,2},{2,4},{4,6},{6,0},{1,3},{3,5},{5,7},{7,1},{8,10},{10,12},{12... | collective-permute-start | bytes 393224 | tf_op jit(solution)/shard_map/ppermute | solution.py:539
  363.8 5.7 %collective-permute-start.52 = (f32[128,256]{1,0:T(8,128)S(1)}, f32[128,256]{1,0:T(8,128)S(1)}, u32[]{:S(2)}, u32[]{:S(2)}) collective-permute-start(f32[128,256]{1,0:T(8,128)S(1)} %add_add_fusion.1), channel_id=1, source_target_pairs={{0,6},{2,0},{4,2},{6,4},{1,7},{3,1},{5,3},{7,5},{8,14},{10,8},{12,... | collective-permute-start | bytes 393224 | tf_op jit(solution)/shard_map/ppermute | solution.py:539
  367.3 5.8 %collective-permute-start.53 = (f32[128,256]{1,0:T(8,128)S(1)}, f32[128,256]{1,0:T(8,128)S(1)}, u32[]{:S(2)}, u32[]{:S(2)}) collective-permute-start(f32[128,256]{1,0:T(8,128)S(1)} %add_add_fusion.1), channel_id=1, source_target_pairs={{0,4},{2,6},{4,0},{6,2},{1,5},{3,7},{5,1},{7,3},{8,12},{10,14},{12... | collective-permute-start | bytes 393224 | tf_op jit(solution)/shard_map/ppermute | solution.py:539
  (46 other events, 1501.5 us)

commit v5 on v4

--- a/solution.py
+++ b/solution.py
@@ -431,7 +431,7 @@
     )(jnp.zeros(1, jnp.int32) if core is None else core, frames, *parts)
 
 
-CHUNK = 512
+CHUNK = 1024
 
 
 def final_kernel(
@@ -439,18 +439,19 @@
 ):
     pieces = patch_ref.shape[1] // CHUNK
 
-    def lines(n):
-        return pl.ds(pl.multiple_of(n * CHUNK, CHUNK), CHUNK)
-
-    def copy_in(p, n):
-        return pltpu.make_async_copy(patch_ref.at[p, lines(n)], rows.at[p, lines(n)], in_sem.at[p, n])
-
-    def copy_out(p, n):
-        return pltpu.make_async_copy(outs.at[p, lines(n)], aligned_ref.at[p, lines(n)], out_sem.at[p, n])
-
-    every = [(p, n) for n in range(pieces) for p in range(PER)]
-    for at in every:
-        copy_in(*at).start()
+    def piece(n):
+        return n // pieces, pl.ds(pl.multiple_of(n % pieces * CHUNK, CHUNK), CHUNK)
+
+    def copy_in(n):
+        p, r = piece(n)
+        return pltpu.make_async_copy(patch_ref.at[p, r], rows.at[p, r], in_sem.at[n])
+
+    def copy_out(n):
+        p, r = piece(n)
+        return pltpu.make_async_copy(outs.at[p, r], aligned_ref.at[p, r], out_sem.at[n])
+
+    for n in range(PER * pieces):
+        copy_in(n).start()
     for ref, half in ((keep_ref, core_ref[0]), (other_ref, 1 - core_ref[0])):
         total_ref[pl.ds(pl.multiple_of(half * (D // 2), D // 2), D // 2)] = ref[...]
     gauge[0] = total_ref[...]
@@ -462,21 +463,19 @@
         low[p] = final.astype(BF16)
 
     def step(n, carry):
-        for p in range(PER):
-            copy_in(p, n).wait()
-        found = [dot(rows[p, lines(n)], low[p]).astype(BF16) for p in range(PER)]
-        for p in range(PER):
-            outs[p, lines(n)] = found[p]
-            copy_out(p, n).start()
+        p, r = piece(n)
+        copy_in(n).wait()
+        outs[p, r] = dot(rows[p, r], low[p]).astype(BF16)
+        copy_out(n).start()
         return carry
 
-    lax.fori_loop(0, pieces, step, 0)
-    for at in every:
-        copy_out(*at).wait()
+    lax.fori_loop(0, PER * pieces, step, 0)
+    for n in range(PER * pieces):
+        copy_out(n).wait()
 
 
 def make_final(core, keep, other, frames, patches):
-    pieces = patches.shape[1] // CHUNK
+    pieces = PER * patches.shape[1] // CHUNK
     return pl.pallas_call(
         final_kernel,
         in_specs=[SM, VM, VM, VM, HBM],
@@ -491,8 +490,8 @@
             pltpu.VMEM(patches.shape, BF16),
             pltpu.VMEM(patches.shape, BF16),
             pltpu.VMEM((PER, D, D), BF16),
-            pltpu.SemaphoreType.DMA((PER, pieces)),
-            pltpu.SemaphoreType.DMA((PER, pieces)),
+            pltpu.SemaphoreType.DMA((pieces,)),
+            pltpu.SemaphoreType.DMA((pieces,)),
         ],
         compiler_params=params(),
         name="aligned_rows",
@@ -513,8 +512,7 @@
 
 
 def spread_frames(low):
-    one, four = send(low, step_perm(UP)), send(low, step_perm(LEFT))
-    three = send(low, step_perm(RIGHT))
+    one, four, three = send(low, step_perm(UP)), send(low, step_perm(LEFT)), send(low, step_perm(RIGHT))
     two, five = send(one, step_perm(UP)), send(four, step_perm(LEFT))
     return [low, one, two, three, four, five] + [send(v, SIBLING) for v in (one, two, three)]
 
@@ -528,8 +526,7 @@
     )
     two = send(two, back_perm(UP))
     three = send(three, back_perm(RIGHT))
-    four = send(four + five, back_perm(LEFT))
-    return [own, three, four, send(one + two, back_perm(UP))]
+    return [own, three, send(four + five, back_perm(LEFT)), send(one + two, back_perm(UP))]
 
 
 def axis_sum(value, axis):
@@ -576,7 +573,7 @@
     rot = make_rotations(info, count, arrays, LAYOUT, 0, 3)
     three_1 = move(five_1, LEFT)
     arrays += [two_1, five_0, five_1, three_0, move(two_1), move(three_0)]
-    rot = make_rotations(info, count, arrays, LAYOUT, 1, 7, rot)
+    rot = make_rotations(info, count, arrays, LAYOUT, 1, 4, rot)
     arrays += [two_0, three_1, move(two_0), move(three_1)]
     rot = make_rotations(info, count, arrays, LAYOUT, 2, 5, rot)
     core = lax.axis_index("gy_2").astype(jnp.int32).reshape(1)

time: 390 us -> 382 us (0.979)
  Pallas kernels: 110 us -> 103 us
  starting transfers between devices: 92.8 us -> 87.3 us
  waiting for transfers between devices: 171 us -> 175 us
    ppermute x44, starting transfers between devices: 79.2 us -> 69.1 us  [send(): return lax.ppermute(value, GY, perm)]
    pallas_call x3, Pallas kernels: 45.2 us -> 38.8 us  [make_rotations(): pl.pallas_call(functools.partial(rotation_kernel, layout, ready, size), i...]
    ppermute x44, waiting for transfers between devices: 152 us -> 157 us  [send(): return lax.ppermute(value, GY, perm)]
    ppermute x9, starting transfers between devices: 10.1 us -> 14.2 us  [from_behind(): lax.ppermute(value, axis, [(i, (i + hops) % size) for i in range(size)])]
  transfers between devices with their start and end apart: 55 -> 55, of which waited for: 33 -> 34; matrix products, arithmetic and copies ran while one was open for 2% -> 2% of each run, Pallas kernels for 17% -> 16%
where the time goes in v5:
time: 382 us; the launch traced here: 381 us
  waiting for transfers between devices  175 us (46%)
  Pallas kernels  103 us (27%)
  starting transfers between devices  87.3 us (23%)
  local copies, waits for them, and re-layouts  9.35 us (2%)
  other arithmetic  5.15 us (1%)
    ppermute x44, waiting for transfers between devices, send(): return lax.ppermute(value, GY, perm)  157 us
    ppermute x44, starting transfers between devices, send(): return lax.ppermute(value, GY, perm)  69.1 us
    pallas_call x3, Pallas kernels, make_rotations(): pl.pallas_call(functools.partial(rotation_kernel, layout, ready, size), i...  38.8 us
    pallas_call x2, Pallas kernels, make_update(): pl.pallas_call(update_kernel, in_specs=[SM] + [VM] * (1 + len(parts)), ou...  16.1 us
    pallas_call x2, Pallas kernels, make_estimates(): pl.pallas_call(estimate_kernel, in_specs=[SM, SM, HBM] + [HBM] * SLOTS, o...  16 us
    ppermute x9, waiting for transfers between devices, from_behind(): lax.ppermute(value, axis, [(i, (i + hops) % size) for i in range(size)])  15.1 us
    pallas_call x1, Pallas kernels, make_index(): pl.pallas_call(index_kernel, in_specs=[SM] * 4, out_specs=[SM] * 2, out_s...  14.4 us
    ppermute x9, starting transfers between devices, from_behind(): lax.ppermute(value, axis, [(i, (i + hops) % size) for i in range(size)])  14.2 us
  transfers between devices with their start and end apart: 55, of which 34 were waited for; matrix products, arithmetic and copies ran while one was open for 2% of the time, Pallas kernels for 16%

profile of v5, /device:TPU:1, one launch (start us, length us, event | category | flops | bytes accessed | tf_op | source)
XLA Modules:
  0.0 381.0 jit_solution(385038968172125360)
XLA Ops:
  0.6 3.2 slice_bitcast_fusion.1
  3.8 4.6 %collective-permute-start.3 = (bf16[4096,256]{1,0:T(8,128)(2,1)}, bf16[4096,256]{1,0:T(8,128)(2,1)S(1)}, u32[]{:S(2)}, u32[]{:S(2)}) collective-permute-start(bf16[4096,256]{1,0:T(8,128)(2,1)} %slice_bitcast_fusion.1), channel_id=1, source_target_pairs={{0,6},{1,25},{2,0},{3,27},{4,2},{5,29},{6,4},{7,31},{8,14},{9,1},{... | collective-permute-start | bytes 6291464 | tf_op jit(solution)/shard_map/ppermute | solution.py:502
  8.4 7.4 %start_frames.1 = (f32[2,256,256]{2,1,0:T(8,128)}, bf16[2,256,256]{2,1,0:T(8,128)(2,1)}) custom-call(f32[2,256,256]{2,1,0:T(8,128)} %start_ref.1), custom_call_target="tpu_custom_call" | custom-call | tf_op jit(solution)/shard_map/start_frames/pallas_call | solution.py:299
  18.5 4.3 %collective-permute-done.16.refs_1_ = bf16[2,256,256]{2,1,0:T(8,128)(2,1)S(1)} collective-permute-done((bf16[2,256,256]{2,1,0:T(8,128)(2,1)}, bf16[2,256,256]{2,1,0:T(8,128)(2,1)S(1)}, u32[]{:S(2)}, u32[]{:S(2)}) %collective-permute-start.16) | collective-permute-done | bytes 262176 | tf_op jit(solution)/shard_map/ppermute | solution.py:502
  23.7 2.2 collective-permute-start
  25.8 8.7 %collective-permute-done.19.refs_4_ = bf16[2,256,256]{2,1,0:T(8,128)(2,1)S(1)} collective-permute-done((bf16[2,256,256]{2,1,0:T(8,128)(2,1)}, bf16[2,256,256]{2,1,0:T(8,128)(2,1)S(1)}, u32[]{:S(2)}, u32[]{:S(2)}) %collective-permute-start.19) | collective-permute-done | bytes 262176 | tf_op jit(solution)/shard_map/ppermute | solution.py:502
  35.7 3.0 collective-permute-start.2
  38.8 2.7 collective-permute-start.8
  41.4 19.3 %collective-permute-done.refs_1_ = bf16[4096,256]{1,0:T(8,128)(2,1)S(1)} collective-permute-done((bf16[4096,256]{1,0:T(8,128)(2,1)S(1)}, bf16[4096,256]{1,0:T(8,128)(2,1)S(1)}, u32[]{:S(2)}, u32[]{:S(2)}) %collective-permute-start) | collective-permute-done | bytes 2097184 | tf_op jit(solution)/shard_map/ppermute | solution.py:502
  60.7 9.3 %collective-permute-start.4 = (bf16[4096,256]{1,0:T(8,128)(2,1)S(1)}, bf16[4096,256]{1,0:T(8,128)(2,1)S(1)}, u32[]{:S(2)}, u32[]{:S(2)}) collective-permute-start(bf16[4096,256]{1,0:T(8,128)(2,1)S(1)} %collective-permute-done.refs_1_), channel_id=1, source_target_pairs={{0,1},{1,0},{2,3},{3,2},{4,5},{5,4},{6,7},{7,6},{8,9},{9,8},{10,11... | collective-permute-start | bytes 6291464 | tf_op jit(solution)/shard_map/ppermute | solution.py:502
  70.0 27.6 %collective-permute-done.1.refs_2_ = bf16[4096,256]{1,0:T(8,128)(2,1)S(1)} collective-permute-done((bf16[4096,256]{1,0:T(8,128)(2,1)}, bf16[4096,256]{1,0:T(8,128)(2,1)S(1)}, u32[]{:S(2)}, u32[]{:S(2)}) %collective-permute-start.1) | collective-permute-done | bytes 2097184 | tf_op jit(solution)/shard_map/ppermute | solution.py:502
  97.6 3.9 %collective-permute-start.5 = (bf16[4096,256]{1,0:T(8,128)(2,1)S(1)}, bf16[4096,256]{1,0:T(8,128)(2,1)S(1)}, u32[]{:S(2)}, u32[]{:S(2)}) collective-permute-start(bf16[4096,256]{1,0:T(8,128)(2,1)S(1)} %collective-permute-done.1.refs_2_), channel_id=1, source_target_pairs={{0,1},{1,0},{2,3},{3,2},{4,5},{5,4},{6,7},{7,6},{8,9},{9,8},{10,11... | collective-permute-start | bytes 6291464 | tf_op jit(solution)/shard_map/ppermute | solution.py:502
  102.2 3.1 collective-permute-done.5.refs_6_
  105.7 22.2 %collective-permute-done.6.refs_7_ = bf16[4096,256]{1,0:T(8,128)(2,1)S(1)} collective-permute-done((bf16[4096,256]{1,0:T(8,128)(2,1)S(1)}, bf16[4096,256]{1,0:T(8,128)(2,1)S(1)}, u32[]{:S(2)}, u32[]{:S(2)}) %collective-permute-start.6) | collective-permute-done | bytes 2097184 | tf_op jit(solution)/shard_map/ppermute | solution.py:502
  128.8 21.5 %collective-permute-done.12.refs_13_ = bf16[4096,256]{1,0:T(8,128)(2,1)S(1)} collective-permute-done((bf16[4096,256]{1,0:T(8,128)(2,1)S(1)}, bf16[4096,256]{1,0:T(8,128)(2,1)S(1)}, u32[]{:S(2)}, u32[]{:S(2)}) %collective-permute-start.12) | collective-permute-done | bytes 2097184 | tf_op jit(solution)/shard_map/ppermute | solution.py:502
  159.1 14.4 %pair_index.1 = (s32[4320]{0:T(1024)}, s32[3]{0:T(128)}) custom-call(s32[2]{0:T(128)} %pad_add_fusion.me_ref, s32[12288]{0:T(1024)} %constant.25.clone.table_ref, s32[512]{0:T(512)} %reshape.16.ends_ref, s32[2048]{0:T(1024)} %reshape.17.blocks_ref), custom_call_target="tpu_custom_call" | custom-call | tf_op jit(solution)/shard_map/pair_index/pallas_call | solution.py:187
  173.5 10.4 %rotations.3.refs_13_ = f32[152,256,256]{2,1,0:T(8,128)} custom-call(s32[4320]{0:T(1024)} %get-tuple-element.27.info_ref, s32[3]{0:T(128)} %get-tuple-element.28.count_ref, bf16[2,4096,256]{2,1,0:T(8,128)(2,1)} %patch_ref.1, bf16[4096,256]{1,0:T(8,128)(2,1)} %copy-done.2, bf16[4096,256]{1,0:T(8,128)(2,1)} %copy-done.3, bf16[4096,256]{1,0:T(8,128)(2,1)} %copy-done.4, ...), custom_call_target="tpu_custom_call" | custom-call | tf_op jit(solution)/shard_map/rotations/pallas_call | solution.py:273
  183.9 13.0 %rotations.4.refs_17_ = f32[152,256,256]{2,1,0:T(8,128)} custom-call(s32[4320]{0:T(1024)} %get-tuple-element.27.info_ref, s32[3]{0:T(128)} %get-tuple-element.28.count_ref, bf16[2,4096,256]{2,1,0:T(8,128)(2,1)} %patch_ref.1, bf16[4096,256]{1,0:T(8,128)(2,1)} %copy-done.2, bf16[4096,256]{1,0:T(8,128)(2,1)} %copy-done.3, ...), custom_call_target="tpu_custom_call", output_to_operand_aliasing={{}: (15, {})} | custom-call | tf_op jit(solution)/shard_map/rotations/pallas_call | solution.py:273
  196.9 15.4 %rotations.5.rot_ref = f32[152,256,256]{2,1,0:T(8,128)} custom-call(s32[4320]{0:T(1024)} %get-tuple-element.27.info_ref, s32[3]{0:T(128)} %get-tuple-element.28.count_ref, bf16[2,4096,256]{2,1,0:T(8,128)(2,1)} %patch_ref.1, bf16[4096,256]{1,0:T(8,128)(2,1)} %copy-done.2, bf16[4096,256]{1,0:T(8,128)(2,1)} %copy-done.3, ...), custom_call_target="tpu_custom_call", output_to_operand_aliasing={{}: (19, {})} | custom-call | tf_op jit(solution)/shard_map/rotations/pallas_call | solution.py:273
  212.3 8.0 %estimates.2 = (f32[2,256,256]{2,1,0:T(8,128)}, f32[2,256,256]{2,1,0:T(8,128)}, f32[2,256,256]{2,1,0:T(8,128)}, f32[2,256,256]{2,1,0:T(8,128)}, f32[2,256,256]{2...) custom-call(s32[4320]{0:T(1024)} %get-tuple-element.27.info_ref, s32[3]{0:T(128)} %get-tuple-element.28.count_ref, ...), custom_call_target="tpu_custom_call" | custom-call | tf_op jit(solution)/shard_map/estimates/pallas_call | solution.py:385
  220.4 11.2 %collective-permute-start.24 = (f32[6,256,256]{2,1,0:T(8,128)}, f32[6,256,256]{2,1,0:T(8,128)S(1)}, u32[]{:S(2)}, u32[]{:S(2)}) collective-permute-start(f32[6,256,256]{2,1,0:T(8,128)} %get-tuple-element.32), channel_id=1, source_target_pairs={{0,1},{1,0},{2,3},{3,2},{4,5},{5,4},{6,7},{7,6},{8,9},{9,8},{10,11... | collective-permute-start | bytes 4718600 | tf_op jit(solution)/shard_map/ppermute | solution.py:502
  231.6 3.2 collective-permute-done.24
  236.6 4.8 %collective-permute-done.26 = f32[2,256,256]{2,1,0:T(8,128)S(1)} collective-permute-done((f32[2,256,256]{2,1,0:T(8,128)}, f32[2,256,256]{2,1,0:T(8,128)S(1)}, u32[]{:S(2)}, u32[]{:S(2)}) %collective-permute-start.26) | collective-permute-done | bytes 524320 | tf_op jit(solution)/shard_map/ppermute | solution.py:502
  241.5 2.7 collective-permute-start.25
  244.2 3.9 %collective-permute-done.28 = f32[2,256,256]{2,1,0:T(8,128)S(1)} collective-permute-done((f32[2,256,256]{2,1,0:T(8,128)S(1)}, f32[2,256,256]{2,1,0:T(8,128)S(1)}, u32[]{:S(2)}, u32[]{:S(2)}) %collective-permute-start.28) | collective-permute-done | bytes 524320 | tf_op jit(solution)/shard_map/ppermute | solution.py:502
  248.2 2.9 collective-permute-done.27.refs_2_
  252.7 7.5 %collective-permute-done.29.refs_3_ = f32[2,256,256]{2,1,0:T(8,128)S(1)} collective-permute-done((f32[2,256,256]{2,1,0:T(8,128)S(1)}, f32[2,256,256]{2,1,0:T(8,128)S(1)}, u32[]{:S(2)}, u32[]{:S(2)}) %collective-permute-start.29) | collective-permute-done | bytes 524320 | tf_op jit(solution)/shard_map/ppermute | solution.py:502
  261.1 8.1 %update_frames.2 = (f32[2,256,256]{2,1,0:T(8,128)}, bf16[2,256,256]{2,1,0:T(8,128)(2,1)}) custom-call(s32[1]{0:T(128)} %constant.9.clone.1.core_ref, f32[2,256,256]{2,1,0:T(8,128)} %get-tuple-element.26.frame_ref, f32[2,256,256]{2,1,0:T(8,128)} %get-tuple-element.30.refs_0_, f32[2,256,256]{2,1,0:T(8,128)} %copy-done.20, f32[2,256,256]{2,1,0:T(8,128)} %copy-done.18, ...), custom_call_target="tpu_custom_call" | custom-call | tf_op jit(solution)/shard_map/update_frames/pallas_call | solution.py:424
  271.1 5.3 %collective-permute-done.30.refs_1_ = bf16[2,256,256]{2,1,0:T(8,128)(2,1)S(1)} collective-permute-done((bf16[2,256,256]{2,1,0:T(8,128)(2,1)}, bf16[2,256,256]{2,1,0:T(8,128)(2,1)S(1)}, u32[]{:S(2)}, u32[]{:S(2)}) %collective-permute-start.30) | collective-permute-done | bytes 262176 | tf_op jit(solution)/shard_map/ppermute | solution.py:502
  278.1 3.0 collective-permute-start.34
  281.1 2.1 collective-permute-done.31.refs_2_
  283.2 2.5 collective-permute-start.36
  287.6 8.0 %estimates.3 = (f32[2,256,256]{2,1,0:T(8,128)}, f32[2,256,256]{2,1,0:T(8,128)}, f32[2,256,256]{2,1,0:T(8,128)}, f32[2,256,256]{2,1,0:T(8,128)}, f32[2,256,256]{2...) custom-call(s32[4320]{0:T(1024)} %get-tuple-element.27.info_ref, s32[3]{0:T(128)} %get-tuple-element.28.count_ref, ...), custom_call_target="tpu_custom_call" | custom-call | tf_op jit(solution)/shard_map/estimates/pallas_call | solution.py:385
  295.6 2.1 collective-permute-start.38
  297.7 3.2 collective-permute-done.38
  302.6 2.6 collective-permute-start.42
  305.2 2.3 collective-permute-done.40
  307.6 2.7 collective-permute-start.39
  311.7 2.9 collective-permute-start.43
  314.6 2.6 collective-permute-done.41.refs_2_
  318.3 5.5 %collective-permute-done.43.refs_3_ = f32[2,256,256]{2,1,0:T(8,128)S(1)} collective-permute-done((f32[2,256,256]{2,1,0:T(8,128)S(1)}, f32[2,256,256]{2,1,0:T(8,128)S(1)}, u32[]{:S(2)}, u32[]{:S(2)}) %collective-permute-start.43) | collective-permute-done | bytes 524320 | tf_op jit(solution)/shard_map/ppermute | solution.py:502
  324.6 8.1 %update_frames.3 = (f32[2,256,256]{2,1,0:T(8,128)}, f32[128,256]{1,0:T(8,128)}, f32[128,256]{1,0:T(8,128)}) custom-call(s32[1]{0:T(128)} %bitcast.core_ref, f32[2,256,256]{2,1,0:T(8,128)} %get-tuple-element.37.frame_ref, f32[2,256,256]{2,1,0:T(8,128)} %get-tuple-element.39.refs_0_, f32[2,256,256]{2,1,0:T(8,128)} %copy-done.21, f32[2,256,256]{2,1,0:T(8,128)} %copy-done.19, ...), custom_call_target="tpu_custom_call" | custom-call | tf_op jit(solution)/shard_map/update_frames/pallas_call | solution.py:424
  336.4 3.8 collective-permute-start.46
  341.3 2.5 collective-permute-done.45
  353.4 2.7 collective-permute-done.50
  361.5 3.0 collective-permute-done.53
  364.6 4.0 %collective-permute-start.54 = (f32[128,256]{1,0:T(8,128)S(1)}, f32[128,256]{1,0:T(8,128)S(1)}, u32[]{:S(2)}, u32[]{:S(2)}) collective-permute-start(f32[128,256]{1,0:T(8,128)S(1)} %add_add_fusion.keep_ref), channel_id=1, source_target_pairs={{0,1},{1,0},{2,3},{3,2},{4,5},{5,4},{6,7},{7,6},{8,9},{9,8},{10,11... | collective-permute-start | bytes 393224 | tf_op jit(solution)/shard_map/ppermute | solution.py:547
  370.2 10.6 %aligned_rows.1 = (bf16[2,4096,256]{2,1,0:T(8,128)(2,1)}, f32[2,256,256]{2,1,0:T(8,128)}, f32[256,256]{1,0:T(8,128)}) custom-call(s32[1]{0:T(128)} %bitcast.core_ref, f32[128,256]{1,0:T(8,128)} %copy-done.17, f32[128,256]{1,0:T(8,128)} %copy-done.36, f32[2,256,256]{2,1,0:T(8,128)} %get-tuple-element.48.frame_ref, bf16[2,4096,256]{2,1,0:T(8,128)(2,1)} %patch_ref.1), custom_call_target="tpu_custom_call" | custom-call | tf_op jit(solution)/shard_map/aligned_rows/pallas_call | solution.py:479
  (167 shorter events, 51.9 us)
Async XLA Ops:
  3.8 34.9 %collective-permute-start.3 = (bf16[4096,256]{1,0:T(8,128)(2,1)}, bf16[4096,256]{1,0:T(8,128)(2,1)S(1)}, u32[]{:S(2)}, u32[]{:S(2)}) collective-permute-start(bf16[4096,256]{1,0:T(8,128)(2,1)} %slice_bitcast_fusion.1), channel_id=1, source_target_pairs={{0,6},{1,25},{2,0},{3,27},{4,2},{5,29},{6,4},{7,31},{8,14},{9,1},{... | collective-permute-start | bytes 6291464 | tf_op jit(solution)/shard_map/ppermute | solution.py:502
  15.8 6.9 %collective-permute-start.16 = (bf16[2,256,256]{2,1,0:T(8,128)(2,1)}, bf16[2,256,256]{2,1,0:T(8,128)(2,1)S(1)}, u32[]{:S(2)}, u32[]{:S(2)}) collective-permute-start(bf16[2,256,256]{2,1,0:T(8,128)(2,1)} %get-tuple-element.29.refs_0_), channel_id=1, source_target_pairs={{0,8},{1,3},{2,10},{3,5},{4,12},{5,7},{6,14},{7,1},{8,16},{9,11},{... | collective-permute-start | bytes 786440 | tf_op jit(solution)/shard_map/ppermute | solution.py:502
  17.0 17.5 %collective-permute-start.19 = (bf16[2,256,256]{2,1,0:T(8,128)(2,1)}, bf16[2,256,256]{2,1,0:T(8,128)(2,1)S(1)}, u32[]{:S(2)}, u32[]{:S(2)}) collective-permute-start(bf16[2,256,256]{2,1,0:T(8,128)(2,1)} %get-tuple-element.29.refs_0_), channel_id=1, source_target_pairs={{0,6},{1,25},{2,0},{3,27},{4,2},{5,29},{6,4},{7,31},{8,14},{9,1},{... | collective-permute-start | bytes 786440 | tf_op jit(solution)/shard_map/ppermute | solution.py:502
  17.1 18.6 %collective-permute-start.18 = (bf16[2,256,256]{2,1,0:T(8,128)(2,1)}, bf16[2,256,256]{2,1,0:T(8,128)(2,1)S(1)}, u32[]{:S(2)}, u32[]{:S(2)}) collective-permute-start(bf16[2,256,256]{2,1,0:T(8,128)(2,1)} %get-tuple-element.29.refs_0_), channel_id=1, source_target_pairs={{0,2},{1,9},{2,4},{3,11},{4,6},{5,13},{6,0},{7,15},{8,10},{9,17},{... | collective-permute-start | bytes 786440 | tf_op jit(solution)/shard_map/ppermute | solution.py:502
  22.8 16.0 %collective-permute-start.17 = (bf16[2,256,256]{2,1,0:T(8,128)(2,1)S(1)}, bf16[2,256,256]{2,1,0:T(8,128)(2,1)S(1)}, u32[]{:S(2)}, u32[]{:S(2)}) collective-permute-start(bf16[2,256,256]{2,1,0:T(8,128)(2,1)S(1)} %collective-permute-done.16.refs_1_), channel_id=1, source_target_pairs={{0,8},{1,3},{2,10},{3,5},{4,12},{5,7},{6,14},{7,1},{8,16},{9,11},{... | collective-permute-start | bytes 786440 | tf_op jit(solution)/shard_map/ppermute | solution.py:502
  23.7 37.1 %collective-permute-start = (bf16[4096,256]{1,0:T(8,128)(2,1)S(1)}, bf16[4096,256]{1,0:T(8,128)(2,1)S(1)}, u32[]{:S(2)}, u32[]{:S(2)}) collective-permute-start(bf16[4096,256]{1,0:T(8,128)(2,1)S(1)} %slice_bitcast_fusion), channel_id=1, source_target_pairs={{0,8},{1,3},{2,10},{3,5},{4,12},{5,7},{6,14},{7,1},{8,16},{9,11},{... | collective-permute-start | bytes 6291464 | tf_op jit(solution)/shard_map/ppermute | solution.py:502
  34.5 63.1 %collective-permute-start.1 = (bf16[4096,256]{1,0:T(8,128)(2,1)}, bf16[4096,256]{1,0:T(8,128)(2,1)S(1)}, u32[]{:S(2)}, u32[]{:S(2)}) collective-permute-start(bf16[4096,256]{1,0:T(8,128)(2,1)} %slice_bitcast_fusion.1), channel_id=1, source_target_pairs={{0,8},{1,3},{2,10},{3,5},{4,12},{5,7},{6,14},{7,1},{8,16},{9,11},{... | collective-permute-start | bytes 6291464 | tf_op jit(solution)/shard_map/ppermute | solution.py:502
  35.7 65.8 %collective-permute-start.2 = (bf16[4096,256]{1,0:T(8,128)(2,1)S(1)}, bf16[4096,256]{1,0:T(8,128)(2,1)S(1)}, u32[]{:S(2)}, u32[]{:S(2)}) collective-permute-start(bf16[4096,256]{1,0:T(8,128)(2,1)S(1)} %slice_bitcast_fusion), channel_id=1, source_target_pairs={{0,6},{1,25},{2,0},{3,27},{4,2},{5,29},{6,4},{7,31},{8,14},{9,1},{... | collective-permute-start | bytes 6291464 | tf_op jit(solution)/shard_map/ppermute | solution.py:502
  38.7 62.8 %collective-permute-start.9 = (bf16[4096,256]{1,0:T(8,128)(2,1)S(1)}, bf16[4096,256]{1,0:T(8,128)(2,1)S(1)}, u32[]{:S(2)}, u32[]{:S(2)}) collective-permute-start(bf16[4096,256]{1,0:T(8,128)(2,1)S(1)} %slice_bitcast_fusion), channel_id=1, source_target_pairs={{0,2},{1,9},{2,4},{3,11},{4,6},{5,13},{6,0},{7,15},{8,10},{9,17},{... | collective-permute-start | bytes 6291464 | tf_op jit(solution)/shard_map/ppermute | solution.py:502
  38.8 62.8 %collective-permute-start.8 = (bf16[4096,256]{1,0:T(8,128)(2,1)S(1)}, bf16[4096,256]{1,0:T(8,128)(2,1)S(1)}, u32[]{:S(2)}, u32[]{:S(2)}) collective-permute-start(bf16[4096,256]{1,0:T(8,128)(2,1)S(1)} %collective-permute-done.3.refs_4_), channel_id=1, source_target_pairs={{0,6},{1,25},{2,0},{3,27},{4,2},{5,29},{6,4},{7,31},{8,14},{9,1},{... | collective-permute-start | bytes 6291464 | tf_op jit(solution)/shard_map/ppermute | solution.py:502
  60.7 41.4 %collective-permute-start.4 = (bf16[4096,256]{1,0:T(8,128)(2,1)S(1)}, bf16[4096,256]{1,0:T(8,128)(2,1)S(1)}, u32[]{:S(2)}, u32[]{:S(2)}) collective-permute-start(bf16[4096,256]{1,0:T(8,128)(2,1)S(1)} %collective-permute-done.refs_1_), channel_id=1, source_target_pairs={{0,1},{1,0},{2,3},{3,2},{4,5},{5,4},{6,7},{7,6},{8,9},{9,8},{10,11... | collective-permute-start | bytes 6291464 | tf_op jit(solution)/shard_map/ppermute | solution.py:502
  97.6 7.7 %collective-permute-start.5 = (bf16[4096,256]{1,0:T(8,128)(2,1)S(1)}, bf16[4096,256]{1,0:T(8,128)(2,1)S(1)}, u32[]{:S(2)}, u32[]{:S(2)}) collective-permute-start(bf16[4096,256]{1,0:T(8,128)(2,1)S(1)} %collective-permute-done.1.refs_2_), channel_id=1, source_target_pairs={{0,1},{1,0},{2,3},{3,2},{4,5},{5,4},{6,7},{7,6},{8,9},{9,8},{10,11... | collective-permute-start | bytes 6291464 | tf_op jit(solution)/shard_map/ppermute | solution.py:502
  101.5 26.4 %collective-permute-start.6 = (bf16[4096,256]{1,0:T(8,128)(2,1)S(1)}, bf16[4096,256]{1,0:T(8,128)(2,1)S(1)}, u32[]{:S(2)}, u32[]{:S(2)}) collective-permute-start(bf16[4096,256]{1,0:T(8,128)(2,1)S(1)} %collective-permute-done.1.refs_2_), channel_id=1, source_target_pairs={{0,8},{1,3},{2,10},{3,5},{4,12},{5,7},{6,14},{7,1},{8,16},{9,11},{... | collective-permute-start | bytes 6291464 | tf_op jit(solution)/shard_map/ppermute | solution.py:502
  101.5 48.8 %collective-permute-start.12 = (bf16[4096,256]{1,0:T(8,128)(2,1)S(1)}, bf16[4096,256]{1,0:T(8,128)(2,1)S(1)}, u32[]{:S(2)}, u32[]{:S(2)}) collective-permute-start(bf16[4096,256]{1,0:T(8,128)(2,1)S(1)} %collective-permute-done.refs_1_), channel_id=1, source_target_pairs={{0,8},{1,3},{2,10},{3,5},{4,12},{5,7},{6,14},{7,1},{8,16},{9,11},{... | collective-permute-start | bytes 6291464 | tf_op jit(solution)/shard_map/ppermute | solution.py:502
  101.6 49.7 %collective-permute-start.13 = (bf16[4096,256]{1,0:T(8,128)(2,1)S(1)}, bf16[4096,256]{1,0:T(8,128)(2,1)}, u32[]{:S(2)}, u32[]{:S(2)}) collective-permute-start(bf16[4096,256]{1,0:T(8,128)(2,1)S(1)} %collective-permute-done.8.refs_9_), channel_id=1, source_target_pairs={{0,6},{1,25},{2,0},{3,27},{4,2},{5,29},{6,4},{7,31},{8,14},{9,1},{... | collective-permute-start | bytes 6291464 | tf_op jit(solution)/shard_map/ppermute | solution.py:502
  102.1 49.3 %collective-permute-start.7 = (bf16[4096,256]{1,0:T(8,128)(2,1)S(1)}, bf16[4096,256]{1,0:T(8,128)(2,1)S(1)}, u32[]{:S(2)}, u32[]{:S(2)}) collective-permute-start(bf16[4096,256]{1,0:T(8,128)(2,1)S(1)} %collective-permute-done.2.refs_3_), channel_id=1, source_target_pairs={{0,6},{1,25},{2,0},{3,27},{4,2},{5,29},{6,4},{7,31},{8,14},{9,1},{... | collective-permute-start | bytes 6291464 | tf_op jit(solution)/shard_map/ppermute | solution.py:502
  105.3 46.6 %collective-permute-start.11 = (bf16[4096,256]{1,0:T(8,128)(2,1)S(1)}, bf16[4096,256]{1,0:T(8,128)(2,1)S(1)}, u32[]{:S(2)}, u32[]{:S(2)}) collective-permute-start(bf16[4096,256]{1,0:T(8,128)(2,1)S(1)} %collective-permute-done.9.refs_10_), channel_id=1, source_target_pairs={{0,1},{1,0},{2,3},{3,2},{4,5},{5,4},{6,7},{7,6},{8,9},{9,8},{10,11... | collective-permute-start | bytes 6291464 | tf_op jit(solution)/shard_map/ppermute | solution.py:502
  127.9 25.5 %collective-permute-start.10 = (bf16[4096,256]{1,0:T(8,128)(2,1)S(1)}, bf16[4096,256]{1,0:T(8,128)(2,1)S(1)}, u32[]{:S(2)}, u32[]{:S(2)}) collective-permute-start(bf16[4096,256]{1,0:T(8,128)(2,1)S(1)} %collective-permute-done.6.refs_7_), channel_id=1, source_target_pairs={{0,1},{1,0},{2,3},{3,2},{4,5},{5,4},{6,7},{7,6},{8,9},{9,8},{10,11... | collective-permute-start | bytes 6291464 | tf_op jit(solution)/shard_map/ppermute | solution.py:502
  151.3 45.5 %collective-permute-start.15 = (bf16[4096,256]{1,0:T(8,128)(2,1)}, bf16[4096,256]{1,0:T(8,128)(2,1)}, u32[]{:S(2)}, u32[]{:S(2)}) collective-permute-start(bf16[4096,256]{1,0:T(8,128)(2,1)} %collective-permute-done.13.refs_14_), channel_id=1, source_target_pairs={{0,1},{1,0},{2,3},{3,2},{4,5},{5,4},{6,7},{7,6},{8,9},{9,8},{10,11... | collective-permute-start | bytes 6291464 | tf_op jit(solution)/shard_map/ppermute | solution.py:502
  151.4 60.9 %collective-permute-start.21 = (bf16[2,256,256]{2,1,0:T(8,128)(2,1)S(1)}, bf16[2,256,256]{2,1,0:T(8,128)(2,1)}, u32[]{:S(2)}, u32[]{:S(2)}) collective-permute-start(bf16[2,256,256]{2,1,0:T(8,128)(2,1)S(1)} %collective-permute-done.16.refs_1_), channel_id=1, source_target_pairs={{0,1},{1,0},{2,3},{3,2},{4,5},{5,4},{6,7},{7,6},{8,9},{9,8},{10,11... | collective-permute-start | bytes 786440 | tf_op jit(solution)/shard_map/ppermute | solution.py:502
  151.9 60.4 %collective-permute-start.20 = (bf16[2,256,256]{2,1,0:T(8,128)(2,1)S(1)}, bf16[2,256,256]{2,1,0:T(8,128)(2,1)}, u32[]{:S(2)}, u32[]{:S(2)}) collective-permute-start(bf16[2,256,256]{2,1,0:T(8,128)(2,1)S(1)} %collective-permute-done.19.refs_4_), channel_id=1, source_target_pairs={{0,6},{1,25},{2,0},{3,27},{4,2},{5,29},{6,4},{7,31},{8,14},{9,1},{... | collective-permute-start | bytes 786440 | tf_op jit(solution)/shard_map/ppermute | solution.py:502
  153.4 58.9 %collective-permute-start.23 = (bf16[2,256,256]{2,1,0:T(8,128)(2,1)S(1)}, bf16[2,256,256]{2,1,0:T(8,128)(2,1)}, u32[]{:S(2)}, u32[]{:S(2)}) collective-permute-start(bf16[2,256,256]{2,1,0:T(8,128)(2,1)S(1)} %collective-permute-done.18.refs_3_), channel_id=1, source_target_pairs={{0,1},{1,0},{2,3},{3,2},{4,5},{5,4},{6,7},{7,6},{8,9},{9,8},{10,11... | collective-permute-start | bytes 786440 | tf_op jit(solution)/shard_map/ppermute | solution.py:502
  155.1 57.2 %collective-permute-start.22 = (bf16[2,256,256]{2,1,0:T(8,128)(2,1)S(1)}, bf16[2,256,256]{2,1,0:T(8,128)(2,1)}, u32[]{:S(2)}, u32[]{:S(2)}) collective-permute-start(bf16[2,256,256]{2,1,0:T(8,128)(2,1)S(1)} %collective-permute-done.17.refs_2_), channel_id=1, source_target_pairs={{0,1},{1,0},{2,3},{3,2},{4,5},{5,4},{6,7},{7,6},{8,9},{9,8},{10,11... | collective-permute-start | bytes 786440 | tf_op jit(solution)/shard_map/ppermute | solution.py:502
  220.4 14.5 %collective-permute-start.24 = (f32[6,256,256]{2,1,0:T(8,128)}, f32[6,256,256]{2,1,0:T(8,128)S(1)}, u32[]{:S(2)}, u32[]{:S(2)}) collective-permute-start(f32[6,256,256]{2,1,0:T(8,128)} %get-tuple-element.32), channel_id=1, source_target_pairs={{0,1},{1,0},{2,3},{3,2},{4,5},{5,4},{6,7},{7,6},{8,9},{9,8},{10,11... | collective-permute-start | bytes 4718600 | tf_op jit(solution)/shard_map/ppermute | solution.py:502
  231.6 9.7 %collective-permute-start.26 = (f32[2,256,256]{2,1,0:T(8,128)}, f32[2,256,256]{2,1,0:T(8,128)S(1)}, u32[]{:S(2)}, u32[]{:S(2)}) collective-permute-start(f32[2,256,256]{2,1,0:T(8,128)} %get-tuple-element.34), channel_id=1, source_target_pairs={{6,0},{25,1},{0,2},{27,3},{2,4},{29,5},{4,6},{31,7},{14,8},{1,9},{... | collective-permute-start | bytes 1572872 | tf_op jit(solution)/shard_map/ppermute | solution.py:502
  236.5 11.5 %collective-permute-start.28 = (f32[2,256,256]{2,1,0:T(8,128)S(1)}, f32[2,256,256]{2,1,0:T(8,128)S(1)}, u32[]{:S(2)}, u32[]{:S(2)}) collective-permute-start(f32[2,256,256]{2,1,0:T(8,128)S(1)} %get-tuple-element.52), channel_id=1, source_target_pairs={{8,0},{3,1},{10,2},{5,3},{12,4},{7,5},{14,6},{1,7},{16,8},{11,9},{... | collective-permute-start | bytes 1572872 | tf_op jit(solution)/shard_map/ppermute | solution.py:502
  241.4 9.6 %collective-permute-start.27 = (f32[2,256,256]{2,1,0:T(8,128)S(1)}, f32[2,256,256]{2,1,0:T(8,128)S(1)}, u32[]{:S(2)}, u32[]{:S(2)}) collective-permute-start(f32[2,256,256]{2,1,0:T(8,128)S(1)} %add.69), channel_id=1, source_target_pairs={{6,0},{25,1},{0,2},{27,3},{2,4},{29,5},{4,6},{31,7},{14,8},{1,9},{... | collective-permute-start | bytes 1572872 | tf_op jit(solution)/shard_map/ppermute | solution.py:502
  241.5 11.2 %collective-permute-start.25 = (f32[2,256,256]{2,1,0:T(8,128)S(1)}, f32[2,256,256]{2,1,0:T(8,128)S(1)}, u32[]{:S(2)}, u32[]{:S(2)}) collective-permute-start(f32[2,256,256]{2,1,0:T(8,128)S(1)} %get-tuple-element.54), channel_id=1, source_target_pairs={{2,0},{9,1},{4,2},{11,3},{6,4},{13,5},{0,6},{15,7},{10,8},{17,9},{... | collective-permute-start | bytes 1572872 | tf_op jit(solution)/shard_map/ppermute | solution.py:502
  248.1 12.2 %collective-permute-start.29 = (f32[2,256,256]{2,1,0:T(8,128)S(1)}, f32[2,256,256]{2,1,0:T(8,128)S(1)}, u32[]{:S(2)}, u32[]{:S(2)}) collective-permute-start(f32[2,256,256]{2,1,0:T(8,128)S(1)} %add.72), channel_id=1, source_target_pairs={{8,0},{3,1},{10,2},{5,3},{12,4},{7,5},{14,6},{1,7},{16,8},{11,9},{... | collective-permute-start | bytes 1572872 | tf_op jit(solution)/shard_map/ppermute | solution.py:502
  269.1 7.3 %collective-permute-start.30 = (bf16[2,256,256]{2,1,0:T(8,128)(2,1)}, bf16[2,256,256]{2,1,0:T(8,128)(2,1)S(1)}, u32[]{:S(2)}, u32[]{:S(2)}) collective-permute-start(bf16[2,256,256]{2,1,0:T(8,128)(2,1)} %get-tuple-element.38.refs_0_), channel_id=1, source_target_pairs={{0,8},{1,3},{2,10},{3,5},{4,12},{5,7},{6,14},{7,1},{8,16},{9,11},{... | collective-permute-start | bytes 786440 | tf_op jit(solution)/shard_map/ppermute | solution.py:502
  269.6 8.5 %collective-permute-start.33 = (bf16[2,256,256]{2,1,0:T(8,128)(2,1)}, bf16[2,256,256]{2,1,0:T(8,128)(2,1)S(1)}, u32[]{:S(2)}, u32[]{:S(2)}) collective-permute-start(bf16[2,256,256]{2,1,0:T(8,128)(2,1)} %get-tuple-element.38.refs_0_), channel_id=1, source_target_pairs={{0,6},{1,25},{2,0},{3,27},{4,2},{5,29},{6,4},{7,31},{8,14},{9,1},{... | collective-permute-start | bytes 786440 | tf_op jit(solution)/shard_map/ppermute | solution.py:502
  270.0 11.0 %collective-permute-start.32 = (bf16[2,256,256]{2,1,0:T(8,128)(2,1)}, bf16[2,256,256]{2,1,0:T(8,128)(2,1)S(1)}, u32[]{:S(2)}, u32[]{:S(2)}) collective-permute-start(bf16[2,256,256]{2,1,0:T(8,128)(2,1)} %get-tuple-element.38.refs_0_), channel_id=1, source_target_pairs={{0,2},{1,9},{2,4},{3,11},{4,6},{5,13},{6,0},{7,15},{8,10},{9,17},{... | collective-permute-start | bytes 786440 | tf_op jit(solution)/shard_map/ppermute | solution.py:502
  276.4 6.7 %collective-permute-start.31 = (bf16[2,256,256]{2,1,0:T(8,128)(2,1)S(1)}, bf16[2,256,256]{2,1,0:T(8,128)(2,1)S(1)}, u32[]{:S(2)}, u32[]{:S(2)}) collective-permute-start(bf16[2,256,256]{2,1,0:T(8,128)(2,1)S(1)} %collective-permute-done.30.refs_1_), channel_id=1, source_target_pairs={{0,8},{1,3},{2,10},{3,5},{4,12},{5,7},{6,14},{7,1},{8,16},{9,11},{... | collective-permute-start | bytes 786440 | tf_op jit(solution)/shard_map/ppermute | solution.py:502
  276.4 9.2 %collective-permute-start.35 = (bf16[2,256,256]{2,1,0:T(8,128)(2,1)S(1)}, bf16[2,256,256]{2,1,0:T(8,128)(2,1)S(1)}, u32[]{:S(2)}, u32[]{:S(2)}) collective-permute-start(bf16[2,256,256]{2,1,0:T(8,128)(2,1)S(1)} %collective-permute-done.30.refs_1_), channel_id=1, source_target_pairs={{0,1},{1,0},{2,3},{3,2},{4,5},{5,4},{6,7},{7,6},{8,9},{9,8},{10,11... | collective-permute-start | bytes 786440 | tf_op jit(solution)/shard_map/ppermute | solution.py:502
  278.1 7.6 %collective-permute-start.34 = (bf16[2,256,256]{2,1,0:T(8,128)(2,1)S(1)}, bf16[2,256,256]{2,1,0:T(8,128)(2,1)S(1)}, u32[]{:S(2)}, u32[]{:S(2)}) collective-permute-start(bf16[2,256,256]{2,1,0:T(8,128)(2,1)S(1)} %collective-permute-done.33.refs_4_), channel_id=1, source_target_pairs={{0,6},{1,25},{2,0},{3,27},{4,2},{5,29},{6,4},{7,31},{8,14},{9,1},{... | collective-permute-start | bytes 786440 | tf_op jit(solution)/shard_map/ppermute | solution.py:502
  295.6 5.3 %collective-permute-start.38 = (f32[6,256,256]{2,1,0:T(8,128)}, f32[6,256,256]{2,1,0:T(8,128)S(1)}, u32[]{:S(2)}, u32[]{:S(2)}) collective-permute-start(f32[6,256,256]{2,1,0:T(8,128)} %get-tuple-element.41), channel_id=1, source_target_pairs={{0,1},{1,0},{2,3},{3,2},{4,5},{5,4},{6,7},{7,6},{8,9},{9,8},{10,11... | collective-permute-start | bytes 4718600 | tf_op jit(solution)/shard_map/ppermute | solution.py:502
  297.7 9.7 %collective-permute-start.40 = (f32[2,256,256]{2,1,0:T(8,128)}, f32[2,256,256]{2,1,0:T(8,128)S(1)}, u32[]{:S(2)}, u32[]{:S(2)}) collective-permute-start(f32[2,256,256]{2,1,0:T(8,128)} %get-tuple-element.43), channel_id=1, source_target_pairs={{6,0},{25,1},{0,2},{27,3},{2,4},{29,5},{4,6},{31,7},{14,8},{1,9},{... | collective-permute-start | bytes 1572872 | tf_op jit(solution)/shard_map/ppermute | solution.py:502
  302.6 9.0 %collective-permute-start.42 = (f32[2,256,256]{2,1,0:T(8,128)S(1)}, f32[2,256,256]{2,1,0:T(8,128)S(1)}, u32[]{:S(2)}, u32[]{:S(2)}) collective-permute-start(f32[2,256,256]{2,1,0:T(8,128)S(1)} %get-tuple-element.49), channel_id=1, source_target_pairs={{8,0},{3,1},{10,2},{5,3},{12,4},{7,5},{14,6},{1,7},{16,8},{11,9},{... | collective-permute-start | bytes 1572872 | tf_op jit(solution)/shard_map/ppermute | solution.py:502
  307.5 9.6 %collective-permute-start.41 = (f32[2,256,256]{2,1,0:T(8,128)S(1)}, f32[2,256,256]{2,1,0:T(8,128)S(1)}, u32[]{:S(2)}, u32[]{:S(2)}) collective-permute-start(f32[2,256,256]{2,1,0:T(8,128)S(1)} %add.74), channel_id=1, source_target_pairs={{6,0},{25,1},{0,2},{27,3},{2,4},{29,5},{4,6},{31,7},{14,8},{1,9},{... | collective-permute-start | bytes 1572872 | tf_op jit(solution)/shard_map/ppermute | solution.py:502
  307.6 10.7 %collective-permute-start.39 = (f32[2,256,256]{2,1,0:T(8,128)S(1)}, f32[2,256,256]{2,1,0:T(8,128)S(1)}, u32[]{:S(2)}, u32[]{:S(2)}) collective-permute-start(f32[2,256,256]{2,1,0:T(8,128)S(1)} %get-tuple-element.51), channel_id=1, source_target_pairs={{2,0},{9,1},{4,2},{11,3},{6,4},{13,5},{0,6},{15,7},{10,8},{17,9},{... | collective-permute-start | bytes 1572872 | tf_op jit(solution)/shard_map/ppermute | solution.py:502
  311.7 12.1 %collective-permute-start.43 = (f32[2,256,256]{2,1,0:T(8,128)S(1)}, f32[2,256,256]{2,1,0:T(8,128)S(1)}, u32[]{:S(2)}, u32[]{:S(2)}) collective-permute-start(f32[2,256,256]{2,1,0:T(8,128)S(1)} %add.77), channel_id=1, source_target_pairs={{8,0},{3,1},{10,2},{5,3},{12,4},{7,5},{14,6},{1,7},{16,8},{11,9},{... | collective-permute-start | bytes 1572872 | tf_op jit(solution)/shard_map/ppermute | solution.py:502
  335.2 8.7 %collective-permute-start.45 = (f32[128,256]{1,0:T(8,128)S(1)}, f32[128,256]{1,0:T(8,128)S(1)}, u32[]{:S(2)}, u32[]{:S(2)}) collective-permute-start(f32[128,256]{1,0:T(8,128)S(1)} %add.78), channel_id=1, source_target_pairs={{0,32},{32,64},{64,96},{96,0},{1,33},{33,65},{65,97},{97,1},{2,34}... | collective-permute-start | bytes 393224 | tf_op jit(solution)/shard_map/ppermute | solution.py:536
  336.4 9.2 %collective-permute-start.46 = (f32[128,256]{1,0:T(8,128)S(1)}, f32[128,256]{1,0:T(8,128)S(1)}, u32[]{:S(2)}, u32[]{:S(2)}) collective-permute-start(f32[128,256]{1,0:T(8,128)S(1)} %add.78), channel_id=1, source_target_pairs={{0,96},{32,0},{64,32},{96,64},{1,97},{33,1},{65,33},{97,65},{2,98}... | collective-permute-start | bytes 393224 | tf_op jit(solution)/shard_map/ppermute | solution.py:536
  340.2 7.4 %collective-permute-start.47 = (f32[128,256]{1,0:T(8,128)S(1)}, f32[128,256]{1,0:T(8,128)S(1)}, u32[]{:S(2)}, u32[]{:S(2)}) collective-permute-start(f32[128,256]{1,0:T(8,128)S(1)} %add.78), channel_id=1, source_target_pairs={{0,64},{32,96},{64,0},{96,32},{1,65},{33,97},{65,1},{97,33},{2,66}... | collective-permute-start | bytes 393224 | tf_op jit(solution)/shard_map/ppermute | solution.py:536
  347.6 5.1 %collective-permute-start.48 = (f32[128,256]{1,0:T(8,128)S(1)}, f32[128,256]{1,0:T(8,128)S(1)}, u32[]{:S(2)}, u32[]{:S(2)}) collective-permute-start(f32[128,256]{1,0:T(8,128)S(1)} %add_add_fusion.2), channel_id=1, source_target_pairs={{0,8},{8,16},{16,24},{24,0},{1,9},{9,17},{17,25},{25,1},{2,10},{10... | collective-permute-start | bytes 393224 | tf_op jit(solution)/shard_map/ppermute | solution.py:536
  350.4 5.8 %collective-permute-start.50 = (f32[128,256]{1,0:T(8,128)S(1)}, f32[128,256]{1,0:T(8,128)S(1)}, u32[]{:S(2)}, u32[]{:S(2)}) collective-permute-start(f32[128,256]{1,0:T(8,128)S(1)} %add_add_fusion.2), channel_id=1, source_target_pairs={{0,16},{8,24},{16,0},{24,8},{1,17},{9,25},{17,1},{25,9},{2,18},{10... | collective-permute-start | bytes 393224 | tf_op jit(solution)/shard_map/ppermute | solution.py:536
  356.2 5.1 %collective-permute-start.51 = (f32[128,256]{1,0:T(8,128)S(1)}, f32[128,256]{1,0:T(8,128)S(1)}, u32[]{:S(2)}, u32[]{:S(2)}) collective-permute-start(f32[128,256]{1,0:T(8,128)S(1)} %add_add_fusion.1), channel_id=1, source_target_pairs={{0,2},{2,4},{4,6},{6,0},{1,3},{3,5},{5,7},{7,1},{8,10},{10,12},{12... | collective-permute-start | bytes 393224 | tf_op jit(solution)/shard_map/ppermute | solution.py:536
  359.0 5.5 %collective-permute-start.53 = (f32[128,256]{1,0:T(8,128)S(1)}, f32[128,256]{1,0:T(8,128)S(1)}, u32[]{:S(2)}, u32[]{:S(2)}) collective-permute-start(f32[128,256]{1,0:T(8,128)S(1)} %add_add_fusion.1), channel_id=1, source_target_pairs={{0,4},{2,6},{4,0},{6,2},{1,5},{3,7},{5,1},{7,3},{8,12},{10,14},{12... | collective-permute-start | bytes 393224 | tf_op jit(solution)/shard_map/ppermute | solution.py:536
  (46 other events, 1501.8 us)
